TPU v7x, 32 devices: a whole 2x2x4 slice. The times are simulated.
32 devices in a mesh: gx: 4 (over z), gz: 2 (over y), row: 4 (over x, core).
Axes of the slice: x: 2, y: 2, z: 4, core: 2. Of those that a mesh axis runs over, the one named last changes fastest.
Arguments:
- flow_field: float32 [5, 16, 64, 512], P(None, 'gx', 'gz', 'row'), may hold values from -6 to 6
- flux_jacobian: float32 [3, 5, 5], replicated, may hold values from -2.5 to 2.5
- history: float32 [12288, 5, 128], P(('gx', 'gz', 'row')), may hold values from -6 to 6
- surface_cell: int32 [1536, 8], P(('gx', 'gz', 'row')), may hold values from 0 to 16383
- surface_blocks: int32 [4, 8], P('row', ('gx', 'gz')), may hold values from 1 to 48, 128 in all within a row
- observers: float32 [3, 256], replicated, may hold values from 0 to 1
Outputs:
- field_out: float32 [5, 16, 64, 512], P(None, 'gx', 'gz', 'row')
- spectrum: float32 [256, 64], P(('gx', 'gz', 'row'))
Inputs may be any that keep to these rules, and one draw needn't show every extreme that they name: The patch with index g of gx+gz and index q of row has exactly 8 * surface_blocks[q, g] live slots, its first ones.
All inputs are finite; a program needn't handle non-finite values. No bound on the sum of `surface_blocks` on one device may be relied on, other than what follows from the above.
Results may differ from a plain program's by a relative error of at most 0.0003.
Values sent between devices are 32-bit elements; how exact they have to be, the bound alone decides.
No kernel may reach another device: no remote copies, remote signals or barrier semaphores. Data moves between devices by JAX's collectives and lax.ppermute only.
A program may use at most 64 MiB of HBM per device.

v0:
```python
import math

import jax
import jax.numpy as jnp
from jax import lax
from jax.sharding import PartitionSpec as P

SURF_DEV = 128
FREQ = 32
STEPS = 3


TIME_STEP = 0.3
VISCOSITY = 0.05


def padded_2(value, sides, width):
    for axis, dim in sides:
        peers, length = (lax.axis_size(axis), value.shape[dim])
        up = [(i, (i + 1) % peers) for i in range(peers - 1)]
        down = [(j, i) for i, j in up]
        last = lax.slice_in_dim(value, length - width, length, axis=dim)
        leading = lax.slice_in_dim(value, 0, width, axis=dim)
        before = lax.ppermute(last, axis, up)
        after = lax.ppermute(leading, axis, down)
        value = jnp.concatenate([before, value, after], axis=dim)
    return value


def stencil_rate(padded, flux_jacobian):
    center = padded[:, 1:-1, 1:-1, 1:-1]
    along_x = (padded[:, 2:, 1:-1, 1:-1] - padded[:, :-2, 1:-1, 1:-1]) * 0.5
    along_z = (padded[:, 1:-1, 2:, 1:-1] - padded[:, 1:-1, :-2, 1:-1]) * 0.5
    along_r = (padded[:, 1:-1, 1:-1, 2:] - padded[:, 1:-1, 1:-1, :-2]) * 0.5
    beside = padded[:, 2:, 1:-1, 1:-1] + padded[:, :-2, 1:-1, 1:-1]
    beside = beside + padded[:, 1:-1, 2:, 1:-1] + padded[:, 1:-1, :-2, 1:-1]
    beside = beside + padded[:, 1:-1, 1:-1, 2:] + padded[:, 1:-1, 1:-1, :-2]
    slopes = jnp.stack([along_x, along_z, along_r])
    transport = jnp.einsum(
        "dvw,dwxzr->vxzr", flux_jacobian, slopes, precision=lax.Precision.HIGHEST
    )
    return transport + VISCOSITY * (beside - 6.0 * center)


def fourier_table(samples, freq_count):
    time_ids = jnp.arange(samples, dtype=jnp.int32)
    freq_ids = jnp.arange(1, freq_count + 1, dtype=jnp.int32)
    turn_ids = freq_ids[:, None] * time_ids[None, :] % samples
    angles = 2.0 * math.pi / samples * turn_ids.astype(jnp.float32)
    norm_scale = 1.0 / math.sqrt(samples)
    return jnp.concatenate([jnp.cos(angles), -jnp.sin(angles)], axis=0) * norm_scale


def spectra_of(signals, fourier):
    return jnp.einsum("ft,svt->vfs", fourier, signals, precision=lax.Precision.HIGHEST)


def radiate(points, monopole, dipole, watchers, radial_cells, freq_count):
    wavenumbers = jnp.arange(1, freq_count + 1, dtype=jnp.float32) * (2.0 / radial_cells)
    offset_vec = watchers[:, :, None] - points[None, :, :]
    distance = jnp.sqrt(jnp.sum(offset_vec * offset_vec, axis=1))
    direction = offset_vec / distance[:, None, :]
    amplitude = (radial_cells / distance)[:, None, :]
    dip_real = direction[:, 0, None, :] * dipole[0, None, :freq_count, :]
    dip_real = dip_real + direction[:, 1, None, :] * dipole[1, None, :freq_count, :]
    dip_real = dip_real + direction[:, 2, None, :] * dipole[2, None, :freq_count, :]
    dip_imag = direction[:, 0, None, :] * dipole[0, None, freq_count:, :]
    dip_imag = dip_imag + direction[:, 1, None, :] * dipole[1, None, freq_count:, :]
    dip_imag = dip_imag + direction[:, 2, None, :] * dipole[2, None, freq_count:, :]
    mono_real = monopole[None, :freq_count, :]
    mono_imag = monopole[None, freq_count:, :]
    phase_arg = distance[:, None, :] * wavenumbers[None, :, None]
    near_term = 1.0 / phase_arg
    cosine = amplitude * jnp.cos(phase_arg)
    sine = amplitude * jnp.sin(phase_arg)
    plus_weight = cosine * near_term + sine
    minus_weight = cosine - sine * near_term
    out_real = jnp.sum(
        plus_weight * dip_real - minus_weight * dip_imag + sine * mono_real - cosine * mono_imag,
        axis=2,
    )
    out_imag = jnp.sum(
        minus_weight * dip_real + plus_weight * dip_imag + cosine * mono_real + sine * mono_imag,
        axis=2,
    )
    return jnp.concatenate([out_real, out_imag], axis=1)


def per_device(flow_field, flux_jacobian, history, surface_cell, surface_blocks, observers):
    width_x, width_z, width_r = (flow_field.shape[1], flow_field.shape[2], flow_field.shape[3])
    count_x, count_z, count_r = (lax.axis_size("gx"), lax.axis_size("gz"), lax.axis_size("row"))
    index_x, index_z, index_r = (lax.axis_index("gx"), lax.axis_index("gz"), lax.axis_index("row"))
    owners = count_x * count_z
    devices = owners * count_r
    radial_cells = width_r * count_r
    slot_rows = surface_cell.shape[0]
    capacity = slot_rows * owners
    samples = history.shape[2]
    cell_ids = surface_cell.reshape(-1)

    def inside_mask(margin):
        coord_x = index_x * width_x + jnp.arange(width_x + 2 * margin, dtype=jnp.int32) - margin
        coord_z = index_z * width_z + jnp.arange(width_z + 2 * margin, dtype=jnp.int32) - margin
        coord_r = index_r * width_r + jnp.arange(width_r + 2 * margin, dtype=jnp.int32) - margin
        valid_x = (coord_x >= 0) & (coord_x < width_x * count_x)
        valid_z = (coord_z >= 0) & (coord_z < width_z * count_z)
        valid_r = (coord_r >= 0) & (coord_r < radial_cells)
        joined = valid_x[:, None, None] & valid_z[None, :, None] & valid_r[None, None, :]
        return joined.astype(jnp.float32)[None]

    mask_outer = inside_mask(2)
    mask_inner = inside_mask(1)
    current = flow_field
    sampled = []
    for step_index in range(STEPS):
        extended = padded_2(current, (("gx", 1), ("gz", 2), ("row", 3)), 3)
        section_one = (
            extended[:, 1:-1, 1:-1, 1:-1] + TIME_STEP * stencil_rate(extended, flux_jacobian)
        ) * mask_outer
        section_two = 0.75 * extended[:, 2:-2, 2:-2, 2:-2] + 0.25 * (
            section_one[:, 1:-1, 1:-1, 1:-1] + TIME_STEP * stencil_rate(section_one, flux_jacobian)
        )
        section_two = section_two * mask_inner
        current = extended[:, 3:-3, 3:-3, 3:-3] / 3.0 + 2.0 / 3.0 * (
            section_two[:, 1:-1, 1:-1, 1:-1] + TIME_STEP * stencil_rate(section_two, flux_jacobian)
        )
        sampled.append(jnp.take(current.reshape(5, -1), cell_ids, axis=1))
    recent = jnp.transpose(jnp.stack(sampled, axis=2), (1, 0, 2))
    signals = jnp.concatenate([history[:, :, : samples - STEPS], recent], axis=2)
    global_x = index_x * width_x + cell_ids // (width_z * width_r)
    global_z = index_z * width_z + cell_ids // width_r % width_z
    global_r = index_r * width_r + cell_ids % width_r
    positions = jnp.stack([global_x, global_z, global_r]).astype(jnp.float32) + 0.5
    fourier = fourier_table(samples, FREQ)
    live_mask = (jnp.arange(capacity, dtype=jnp.int32) // owners < surface_blocks[0, 0]).astype(
        jnp.float32
    )
    spectra = spectra_of(signals, fourier) * live_mask
    monopole = spectra[0] + spectra[4]
    dipole = spectra[1:4]
    watchers = jnp.stack(
        [
            observers[0] * (width_x * count_x),
            observers[1] * (width_z * count_z),
            (1.25 + 0.75 * observers[2]) * radial_cells,
        ],
        axis=1,
    )
    norm_scale = math.sqrt(devices * SURF_DEV)
    row_count = observers.shape[1] // devices * lax.axis_size(("gx", "gz", "row"))
    block_size = math.gcd(row_count, 32)

    def one_block(block):
        return radiate(positions, monopole, dipole, block, radial_cells, FREQ)

    blocks_out = lax.map(one_block, watchers.reshape(row_count // block_size, block_size, 3))
    spectrum = lax.psum_scatter(
        blocks_out.reshape(row_count, 2 * FREQ) / norm_scale,
        ("gx", "gz", "row"),
        scatter_dimension=0,
        tiled=True,
    )
    return (current, spectrum)


def solution(mesh):
    return jax.shard_map(
        per_device,
        mesh=mesh,
        in_specs=(
            P(None, "gx", "gz", "row"),
            P(),
            P(("gx", "gz", "row"), None, None),
            P(("gx", "gz", "row"), None),
            P("row", ("gx", "gz")),
            P(),
        ),
        out_specs=(P(None, "gx", "gz", "row"), P(("gx", "gz", "row"), None)),
        check_vma=False,
    )
```

profile of v0, /device:TPU:0, one launch (start us, length us, event | category | flops | bytes accessed | tf_op | source)
XLA Modules:
  0.0 461.9 jit_solution(13819850660156469321)
XLA Ops:
  8.5 5.7 %collective-permute-start = (f32[5,3,32,128]{3,0,2,1:T(8,128)S(1)}, f32[5,3,32,128]{3,0,2,1:T(8,128)}, u32[]{:S(2)}, u32[]{:S(2)}) collective-permute-start(f32[5,3,32,128]{3,0,2,1:T(8,128)S(1)} %copy.279), channel_id=1, source_target_pairs={{0,8},{8,16},{16,24},{1,9},{9,17},{17,25},{2,10},{10,18},{18,26},{... | collective-permute-start | bytes 737288 | tf_op jit(solution)/shard_map/ppermute | solution.py:24
  17.1 4.8 %collective-permute-done = f32[5,3,32,128]{3,0,2,1:T(8,128)} collective-permute-done((f32[5,3,32,128]{3,0,2,1:T(8,128)S(1)}, f32[5,3,32,128]{3,0,2,1:T(8,128)}, u32[]{:S(2)}, u32[]{:S(2)}) %collective-permute-start) | collective-permute-done | bytes 245792 | tf_op jit(solution)/shard_map/ppermute | solution.py:24
  23.1 3.8 collective-permute-done.1
  26.9 3.4 collective-permute-start.2
  32.8 4.4 collective-permute-done.3
  37.9 1.7 fusion.144
  39.6 2.5 copy.134
  42.1 1.9 collective-permute-start.4
  49.8 2.7 copy.137
  52.6 2.7 pad_maximum_fusion.5
  55.3 3.1 multiply_bitcast_fusion.8
  58.4 8.4 %fusion.36 = f32[5,8,36,132]{3,0,2,1:T(8,128)S(1)} fusion(f32[5,10,38,134]{3,0,2,1:T(8,128)S(1)} %pad_maximum_fusion.5, f32[1,5,8,36,132]{4,1,0,3,2:T(8,128)S(1)} %get-tuple-element.83, f32[1,5,8,36,132]{4,1,0,3,2:T(8,128)S(1)} %get-tuple-element.84, f32[1,5,8,36,132]{4,1,0,3,2:T(8,128)S(1)} %get-tuple-element.82, f32[8,36,132]{2,1,0:T(8,128)S(1)} %copy-done.4, ...), kind=kOutput, calls=%fused_computation.68 | convolution fusion | flops 37635840 | bytes 8515884 | tf_op jit(solution)/shard_map/dvw,dwxzr->vxzr/dot_general | solution.py:39
  66.8 2.2 multiply_bitcast_fusion.17
  69.0 3.8 fusion.72
  72.8 3.3 fusion.56
  79.0 2.8 collective-permute-start.6
  83.5 5.5 %collective-permute-done.6 = f32[5,3,32,128]{3,0,2,1:T(8,128)S(1)} collective-permute-done((f32[5,3,32,128]{3,0,2,1:T(8,128)S(1)}, f32[5,3,32,128]{3,0,2,1:T(8,128)S(1)}, u32[]{:S(2)}, u32[]{:S(2)}) %collective-permute-start.6) | collective-permute-done | bytes 245792 | tf_op jit(solution)/shard_map/ppermute | solution.py:24
  88.9 4.7 %collective-permute-done.7 = f32[5,3,32,128]{3,0,2,1:T(8,128)S(1)} collective-permute-done((f32[5,3,32,128]{3,0,2,1:T(8,128)S(1)}, f32[5,3,32,128]{3,0,2,1:T(8,128)S(1)}, u32[]{:S(2)}, u32[]{:S(2)}) %collective-permute-start.7) | collective-permute-done | bytes 245792 | tf_op jit(solution)/shard_map/ppermute | solution.py:25
  97.9 4.7 %collective-permute-done.9 = f32[5,10,3,128]{3,0,2,1:T(8,128)S(1)} collective-permute-done((f32[5,10,3,128]{3,0,2,1:T(8,128)S(1)}, f32[5,10,3,128]{3,0,2,1:T(8,128)S(1)}, u32[]{:S(2)}, u32[]{:S(2)}) %collective-permute-start.9) | collective-permute-done | bytes 76832 | tf_op jit(solution)/shard_map/ppermute | solution.py:25
  102.8 1.7 fusion.143
  104.4 1.8 copy.147
  106.3 3.0 collective-permute-start.10
  114.8 2.7 copy.150
  117.5 2.7 pad_maximum_fusion.6
  120.2 3.1 multiply_bitcast_fusion.5
  123.3 5.4 %fusion.45 = f32[8,36,132,5]{2,3,0,1:T(8,128)S(1)} fusion(f32[3,5,5,1,1]{2,0,1,4,3:T(4,128)S(1)} %bitcast.237, f32[1,5,8,36,132]{4,1,3,2,0:T(8,128)S(1)} %get-tuple-element.80, f32[1,5,8,36,132]{4,1,3,2,0:T(8,128)S(1)} %get-tuple-element.81, f32[1,5,8,36,132]{4,1,3,2,0:T(8,128)S(1)} %get-tuple-element.79), kind=kOutput, calls=%fused_computation.86 | convolution fusion | flops 35354880 | bytes 3041580 | tf_op jit(solution)/shard_map/dvw,dwxzr->vxzr/dot_general | solution.py:39
  128.7 4.3 fusion.42
  133.0 2.2 multiply_bitcast_fusion.14
  135.3 3.8 fusion.75
  139.1 3.3 fusion.54
  145.2 3.5 collective-permute-start.12
  151.6 4.3 collective-permute-done.12
  155.9 4.7 %collective-permute-done.13 = f32[5,3,32,128]{3,0,2,1:T(8,128)S(1)} collective-permute-done((f32[5,3,32,128]{3,0,2,1:T(8,128)S(1)}, f32[5,3,32,128]{3,0,2,1:T(8,128)S(1)}, u32[]{:S(2)}, u32[]{:S(2)}) %collective-permute-start.13) | collective-permute-done | bytes 245792 | tf_op jit(solution)/shard_map/ppermute | solution.py:25
  164.9 4.7 %collective-permute-done.15 = f32[5,10,3,128]{3,0,2,1:T(8,128)S(1)} collective-permute-done((f32[5,10,3,128]{3,0,2,1:T(8,128)S(1)}, f32[5,10,3,128]{3,0,2,1:T(8,128)S(1)}, u32[]{:S(2)}, u32[]{:S(2)}) %collective-permute-start.15) | collective-permute-done | bytes 76832 | tf_op jit(solution)/shard_map/ppermute | solution.py:25
  170.3 1.7 fusion.142
  172.0 1.8 copy.160
  173.9 3.0 collective-permute-start.16
  179.9 5.3 %copy.175 = f32[5,16384]{0,1:T(8,128)} copy(f32[5,16384]{1,0:T(8,128)S(1)} %bitcast.239) | data formatting | bytes 655360 | tf_op jit(solution)/shard_map/reshape | solution.py:127
  185.2 5.0 %gather_fusion = f32[384,5]{1,0:T(8,128)} fusion(f32[5,16384]{0,1:T(8,128)} %copy.175, s32[1024]{0:T(1024)S(1)} %pad_clamp_fusion), kind=kCustom, calls=%fused_computation.clone | custom fusion | bytes 16896 | tf_op jit(solution)/shard_map/jit(_take)/gather | solution.py:127
  190.2 5.3 %copy.177 = f32[5,16384]{0,1:T(8,128)} copy(f32[5,16384]{1,0:T(8,128)S(1)} %bitcast.240) | data formatting | bytes 655360 | tf_op jit(solution)/shard_map/reshape | solution.py:127
  195.4 5.0 %gather_fusion.1 = f32[384,5]{1,0:T(8,128)} fusion(f32[5,16384]{0,1:T(8,128)} %copy.177, s32[1024]{0:T(1024)S(1)} %pad_clamp_fusion), kind=kCustom, calls=%fused_computation.1.clone | custom fusion | bytes 16896 | tf_op jit(solution)/shard_map/jit(_take)/gather | solution.py:127
  202.1 2.7 copy.163
  204.8 2.7 pad_maximum_fusion.7
  207.5 4.5 multiply_bitcast_fusion.2
  212.0 7.3 %fusion.48 = f32[8,36,132,5]{2,3,0,1:T(8,128)S(1)} fusion(f32[3,5,5,1,1]{2,0,1,4,3:T(4,128)S(1)} %bitcast.234, f32[1,5,8,36,132]{4,1,3,2,0:T(8,128)S(1)} %get-tuple-element.77, f32[1,5,8,36,132]{4,1,3,2,0:T(8,128)} %get-tuple-element.78, f32[1,5,8,36,132]{4,1,3,2,0:T(8,128)S(1)} %get-tuple-element.76), kind=kOutput, calls=%fused_computation.87 | convolution fusion | flops 35354880 | bytes 3041580 | tf_op jit(solution)/shard_map/dvw,dwxzr->vxzr/dot_general | solution.py:39
  219.3 4.2 fusion.39
  223.5 2.2 multiply_bitcast_fusion.11
  225.7 3.8 fusion.78
  229.5 3.3 fusion.52
  235.6 5.6 %copy.179 = f32[5,16384]{0,1:T(8,128)} copy(f32[5,16384]{1,0:T(8,128)S(1)} %bitcast.241) | data formatting | bytes 655360 | tf_op jit(solution)/shard_map/reshape | solution.py:127
  241.1 4.5 gather_fusion.2
  246.4 2.9 copy.181
  249.4 2.9 copy.182
  252.3 3.8 copy.183
  258.8 69.9 %while.10 = (s32[]{:T(128)}, f32[8,32,64]{2,1,0:T(8,128)S(1)}, f32[8,32,3]{1,2,0:T(4,128)}, f32[3,384]{1,0:T(4,128)S(1)}, f32[3,64,384]{2,1,0:T(8,128)S(1)}, /*index=5*/f32[64,384]{1,0:T(8,128)S(1)}, s32[]{:T(128)}) while((s32[]{:T(128)}, f32[8,32,64]{2,1,0:T(8,128)S(1)}, f32[8,32,3]{1,2,0:T(4,128)}, f32[3,384]{1,0:T(4,128)S(1)}, ...), condition=%wide.region_4.6_spmd, body=%wide.region_0.5_spmd.sunk | while | flops 13553730 | bytes 2181973 | solution.py:156
  259.7 7.7 %fusion.153 = (f32[32,32]{1,0:T(8,128)S(1)}, f32[32,32]{1,0:T(8,128)S(1)}) fusion(f32[32,384]{1,0:T(8,128)S(1)} %get-tuple-element.181, f32[32,384]{1,0:T(8,128)S(1)} %get-tuple-element.182, f32[32,384]{1,0:T(8,128)S(1)} %get-tuple-element.183, f32[32,384]{1,0:T(8,128)S(1)} %get-tuple-element.184, f32[32,384]{1,0:T(8,128)S(1)} %get-tuple-element.185, ...), kind=kLoop, calls=%fused_computation.13.clone.1 | loop fusion | flops 13367296 | bytes 647296 | tf_op jit(solution)/shard_map/while/body/eval_jaxpr/reduce_sum | solution.py:78
  268.5 7.7 %fusion.153 = (f32[32,32]{1,0:T(8,128)S(1)}, f32[32,32]{1,0:T(8,128)S(1)}) fusion(f32[32,384]{1,0:T(8,128)S(1)} %get-tuple-element.181, f32[32,384]{1,0:T(8,128)S(1)} %get-tuple-element.182, f32[32,384]{1,0:T(8,128)S(1)} %get-tuple-element.183, f32[32,384]{1,0:T(8,128)S(1)} %get-tuple-element.184, f32[32,384]{1,0:T(8,128)S(1)} %get-tuple-element.185, ...), kind=kLoop, calls=%fused_computation.13.clone.1 | loop fusion | flops 13367296 | bytes 647296 | tf_op jit(solution)/shard_map/while/body/eval_jaxpr/reduce_sum | solution.py:78
  277.2 7.7 %fusion.153 = (f32[32,32]{1,0:T(8,128)S(1)}, f32[32,32]{1,0:T(8,128)S(1)}) fusion(f32[32,384]{1,0:T(8,128)S(1)} %get-tuple-element.181, f32[32,384]{1,0:T(8,128)S(1)} %get-tuple-element.182, f32[32,384]{1,0:T(8,128)S(1)} %get-tuple-element.183, f32[32,384]{1,0:T(8,128)S(1)} %get-tuple-element.184, f32[32,384]{1,0:T(8,128)S(1)} %get-tuple-element.185, ...), kind=kLoop, calls=%fused_computation.13.clone.1 | loop fusion | flops 13367296 | bytes 647296 | tf_op jit(solution)/shard_map/while/body/eval_jaxpr/reduce_sum | solution.py:78
  286.0 7.7 %fusion.153 = (f32[32,32]{1,0:T(8,128)S(1)}, f32[32,32]{1,0:T(8,128)S(1)}) fusion(f32[32,384]{1,0:T(8,128)S(1)} %get-tuple-element.181, f32[32,384]{1,0:T(8,128)S(1)} %get-tuple-element.182, f32[32,384]{1,0:T(8,128)S(1)} %get-tuple-element.183, f32[32,384]{1,0:T(8,128)S(1)} %get-tuple-element.184, f32[32,384]{1,0:T(8,128)S(1)} %get-tuple-element.185, ...), kind=kLoop, calls=%fused_computation.13.clone.1 | loop fusion | flops 13367296 | bytes 647296 | tf_op jit(solution)/shard_map/while/body/eval_jaxpr/reduce_sum | solution.py:78
  294.8 7.7 %fusion.153 = (f32[32,32]{1,0:T(8,128)S(1)}, f32[32,32]{1,0:T(8,128)S(1)}) fusion(f32[32,384]{1,0:T(8,128)S(1)} %get-tuple-element.181, f32[32,384]{1,0:T(8,128)S(1)} %get-tuple-element.182, f32[32,384]{1,0:T(8,128)S(1)} %get-tuple-element.183, f32[32,384]{1,0:T(8,128)S(1)} %get-tuple-element.184, f32[32,384]{1,0:T(8,128)S(1)} %get-tuple-element.185, ...), kind=kLoop, calls=%fused_computation.13.clone.1 | loop fusion | flops 13367296 | bytes 647296 | tf_op jit(solution)/shard_map/while/body/eval_jaxpr/reduce_sum | solution.py:78
  303.4 7.7 %fusion.153 = (f32[32,32]{1,0:T(8,128)S(1)}, f32[32,32]{1,0:T(8,128)S(1)}) fusion(f32[32,384]{1,0:T(8,128)S(1)} %get-tuple-element.181, f32[32,384]{1,0:T(8,128)S(1)} %get-tuple-element.182, f32[32,384]{1,0:T(8,128)S(1)} %get-tuple-element.183, f32[32,384]{1,0:T(8,128)S(1)} %get-tuple-element.184, f32[32,384]{1,0:T(8,128)S(1)} %get-tuple-element.185, ...), kind=kLoop, calls=%fused_computation.13.clone.1 | loop fusion | flops 13367296 | bytes 647296 | tf_op jit(solution)/shard_map/while/body/eval_jaxpr/reduce_sum | solution.py:78
  312.2 7.7 %fusion.153 = (f32[32,32]{1,0:T(8,128)S(1)}, f32[32,32]{1,0:T(8,128)S(1)}) fusion(f32[32,384]{1,0:T(8,128)S(1)} %get-tuple-element.181, f32[32,384]{1,0:T(8,128)S(1)} %get-tuple-element.182, f32[32,384]{1,0:T(8,128)S(1)} %get-tuple-element.183, f32[32,384]{1,0:T(8,128)S(1)} %get-tuple-element.184, f32[32,384]{1,0:T(8,128)S(1)} %get-tuple-element.185, ...), kind=kLoop, calls=%fused_computation.13.clone.1 | loop fusion | flops 13367296 | bytes 647296 | tf_op jit(solution)/shard_map/while/body/eval_jaxpr/reduce_sum | solution.py:78
  320.9 7.7 %fusion.153 = (f32[32,32]{1,0:T(8,128)S(1)}, f32[32,32]{1,0:T(8,128)S(1)}) fusion(f32[32,384]{1,0:T(8,128)S(1)} %get-tuple-element.181, f32[32,384]{1,0:T(8,128)S(1)} %get-tuple-element.182, f32[32,384]{1,0:T(8,128)S(1)} %get-tuple-element.183, f32[32,384]{1,0:T(8,128)S(1)} %get-tuple-element.184, f32[32,384]{1,0:T(8,128)S(1)} %get-tuple-element.185, ...), kind=kLoop, calls=%fused_computation.13.clone.1 | loop fusion | flops 13367296 | bytes 647296 | tf_op jit(solution)/shard_map/while/body/eval_jaxpr/reduce_sum | solution.py:78
  330.2 123.1 %all-reduce.3.cloned.1.call-done = f32[256,64]{1,0:T(8,128)} async-done(((f32[256,64]{1,0:T(8,128)}), f32[256,64]{1,0:T(8,128)}) %all-reduce.3.cloned.1.call-update) | async-done | bytes 65552
  (196 shorter events, 60.2 us)
Async XLA Ops:
  7.2 51.2 %copy-start = (f32[3,5,5]{2,0,1:T(4,128)S(1)}, f32[3,5,5]{2,0,1:T(4,128)}, u32[]{:S(2)}) copy-start(f32[3,5,5]{2,0,1:T(4,128)} %param.11) | copy-start | bytes 904
  7.2 15.7 %copy-start.1 = (f32[5,4,32,128]{3,2,1,0:T(8,128)S(1)}, f32[5,4,32,128]{3,2,1,0:T(8,128)}, u32[]{:S(2)}) copy-start(f32[5,4,32,128]{3,2,1,0:T(8,128)} %param.10) | copy-start | bytes 983044
  7.2 8.9 %copy-start.20 = (s32[48,8]{0,1:T(8,128)S(1)}, s32[48,8]{0,1:T(8,128)}, u32[]{:S(2)}) copy-start(s32[48,8]{0,1:T(8,128)} %param.13) | copy-start | bytes 4612
  7.2 446.1 %all-reduce.3.cloned.1.call-start = ((), (), s32[]{:S(2)}) async-start(), calls=%async_computation | async-start | bytes 262144
  8.5 13.3 %collective-permute-start = (f32[5,3,32,128]{3,0,2,1:T(8,128)S(1)}, f32[5,3,32,128]{3,0,2,1:T(8,128)}, u32[]{:S(2)}, u32[]{:S(2)}) collective-permute-start(f32[5,3,32,128]{3,0,2,1:T(8,128)S(1)} %copy.279), channel_id=1, source_target_pairs={{0,8},{8,16},{16,24},{1,9},{9,17},{17,25},{2,10},{10,18},{18,26},{... | collective-permute-start | bytes 737288 | tf_op jit(solution)/shard_map/ppermute | solution.py:24
  14.4 12.5 %collective-permute-start.1 = (f32[5,3,32,128]{3,0,2,1:T(8,128)S(1)}, f32[5,3,32,128]{3,0,2,1:T(8,128)S(1)}, u32[]{:S(2)}, u32[]{:S(2)}) collective-permute-start(f32[5,3,32,128]{3,0,2,1:T(8,128)S(1)} %copy.280), channel_id=1, source_target_pairs={{8,0},{16,8},{24,16},{9,1},{17,9},{25,17},{10,2},{18,10},{26,18},{... | collective-permute-start | bytes 737288 | tf_op jit(solution)/shard_map/ppermute | solution.py:25
  26.9 5.9 %collective-permute-start.2 = (f32[5,10,3,128]{3,0,2,1:T(8,128)S(1)}, f32[5,10,3,128]{3,0,2,1:T(8,128)S(1)}, u32[]{:S(2)}, u32[]{:S(2)}) collective-permute-start(f32[5,10,3,128]{3,0,2,1:T(8,128)S(1)} %get-tuple-element.113), channel_id=1, source_target_pairs={{0,4},{1,5},{2,6},{3,7},{8,12},{9,13},{10,14},{11,15},{16,20},{17,... | collective-permute-start | bytes 230408 | tf_op jit(solution)/shard_map/ppermute | solution.py:24
  30.4 6.8 %collective-permute-start.3 = (f32[5,10,3,128]{3,0,2,1:T(8,128)S(1)}, f32[5,10,3,128]{3,0,2,1:T(8,128)S(1)}, u32[]{:S(2)}, u32[]{:S(2)}) collective-permute-start(f32[5,10,3,128]{3,0,2,1:T(8,128)S(1)} %get-tuple-element.114), channel_id=1, source_target_pairs={{4,0},{5,1},{6,2},{7,3},{12,8},{13,9},{14,10},{15,11},{20,16},{21,... | collective-permute-start | bytes 230408 | tf_op jit(solution)/shard_map/ppermute | solution.py:25
  32.8 4.4 copy-start.11
  37.1 0.7 copy-start.12
  42.1 5.1 %collective-permute-start.4 = (f32[5,10,38,3]{2,3,1,0:T(4,128)}, f32[5,10,38,3]{2,3,1,0:T(4,128)}, u32[]{:S(2)}, u32[]{:S(2)}) collective-permute-start(f32[5,10,38,3]{2,3,1,0:T(4,128)} %copy.134), channel_id=1, source_target_pairs={{0,1},{1,2},{2,3},{4,5},{5,6},{6,7},{8,9},{9,10},{10,11},{12,13},{... | collective-permute-start | bytes 68408 | tf_op jit(solution)/shard_map/ppermute | solution.py:24
  45.2 4.6 collective-permute-start.5
  55.2 3.1 copy-start.4
  78.0 5.1 %copy-start.21 = (f32[3,256]{1,0:T(4,128)S(1)}, f32[3,256]{1,0:T(4,128)}, u32[]{:S(2)}) copy-start(f32[3,256]{1,0:T(4,128)} %param.15) | copy-start | bytes 9220
  79.0 10.0 %collective-permute-start.6 = (f32[5,3,32,128]{3,0,2,1:T(8,128)S(1)}, f32[5,3,32,128]{3,0,2,1:T(8,128)S(1)}, u32[]{:S(2)}, u32[]{:S(2)}) collective-permute-start(f32[5,3,32,128]{3,0,2,1:T(8,128)S(1)} %get-tuple-element.117), channel_id=1, source_target_pairs={{0,8},{8,16},{16,24},{1,9},{9,17},{17,25},{2,10},{10,18},{18,26},{... | collective-permute-start | bytes 737288 | tf_op jit(solution)/shard_map/ppermute | solution.py:24
  81.8 11.9 %collective-permute-start.7 = (f32[5,3,32,128]{3,0,2,1:T(8,128)S(1)}, f32[5,3,32,128]{3,0,2,1:T(8,128)S(1)}, u32[]{:S(2)}, u32[]{:S(2)}) collective-permute-start(f32[5,3,32,128]{3,0,2,1:T(8,128)S(1)} %get-tuple-element.118), channel_id=1, source_target_pairs={{8,0},{16,8},{24,16},{9,1},{17,9},{25,17},{10,2},{18,10},{26,18},{... | collective-permute-start | bytes 737288 | tf_op jit(solution)/shard_map/ppermute | solution.py:25
  93.7 4.3 collective-permute-start.8
  95.2 7.4 %collective-permute-start.9 = (f32[5,10,3,128]{3,0,2,1:T(8,128)S(1)}, f32[5,10,3,128]{3,0,2,1:T(8,128)S(1)}, u32[]{:S(2)}, u32[]{:S(2)}) collective-permute-start(f32[5,10,3,128]{3,0,2,1:T(8,128)S(1)} %get-tuple-element.112), channel_id=1, source_target_pairs={{4,0},{5,1},{6,2},{7,3},{12,8},{13,9},{14,10},{15,11},{20,16},{21,... | collective-permute-start | bytes 230408 | tf_op jit(solution)/shard_map/ppermute | solution.py:25
  106.3 6.1 %collective-permute-start.10 = (f32[5,10,38,3]{2,3,1,0:T(4,128)S(1)}, f32[5,10,38,3]{2,3,1,0:T(4,128)}, u32[]{:S(2)}, u32[]{:S(2)}) collective-permute-start(f32[5,10,38,3]{2,3,1,0:T(4,128)S(1)} %copy.147), channel_id=1, source_target_pairs={{0,1},{1,2},{2,3},{4,5},{5,6},{6,7},{8,9},{9,10},{10,11},{12,13},{... | collective-permute-start | bytes 68408 | tf_op jit(solution)/shard_map/ppermute | solution.py:24
  110.5 4.3 collective-permute-start.11
  123.3 5.4 %copy-start.5 = (f32[8,36,132]{2,1,0:T(8,128)S(1)}, f32[8,36,132]{2,1,0:T(8,128)}, u32[]{:S(2)}) copy-start(f32[8,36,132]{2,1,0:T(8,128)} %and_convert_fusion) | copy-start | bytes 456196
  145.1 18.3 %copy-start.18 = (s32[384]{0:T(512)S(1)}, s32[384]{0:T(512)}, u32[]{:S(2)}) copy-start(s32[384]{0:T(512)} %compare_select_fusion.2) | copy-start | bytes 4612
  145.2 10.7 %collective-permute-start.12 = (f32[5,3,32,128]{3,0,2,1:T(8,128)S(1)}, f32[5,3,32,128]{3,0,2,1:T(8,128)S(1)}, u32[]{:S(2)}, u32[]{:S(2)}) collective-permute-start(f32[5,3,32,128]{3,0,2,1:T(8,128)S(1)} %get-tuple-element.115), channel_id=1, source_target_pairs={{0,8},{8,16},{16,24},{1,9},{9,17},{17,25},{2,10},{10,18},{18,26},{... | collective-permute-start | bytes 737288 | tf_op jit(solution)/shard_map/ppermute | solution.py:24
  148.7 11.9 %collective-permute-start.13 = (f32[5,3,32,128]{3,0,2,1:T(8,128)S(1)}, f32[5,3,32,128]{3,0,2,1:T(8,128)S(1)}, u32[]{:S(2)}, u32[]{:S(2)}) collective-permute-start(f32[5,3,32,128]{3,0,2,1:T(8,128)S(1)} %get-tuple-element.116), channel_id=1, source_target_pairs={{8,0},{16,8},{24,16},{9,1},{17,9},{25,17},{10,2},{18,10},{26,18},{... | collective-permute-start | bytes 737288 | tf_op jit(solution)/shard_map/ppermute | solution.py:25
  160.6 9.0 %copy-start.2 = (f32[5,3,32,128]{3,0,2,1:T(8,128)}, f32[5,3,32,128]{3,0,2,1:T(8,128)S(1)}, u32[]{:S(2)}) copy-start(f32[5,3,32,128]{3,0,2,1:T(8,128)S(1)} %collective-permute-done.13) | copy-start | bytes 737284
  160.6 4.3 collective-permute-start.14
  162.1 7.4 %collective-permute-start.15 = (f32[5,10,3,128]{3,0,2,1:T(8,128)S(1)}, f32[5,10,3,128]{3,0,2,1:T(8,128)S(1)}, u32[]{:S(2)}, u32[]{:S(2)}) collective-permute-start(f32[5,10,3,128]{3,0,2,1:T(8,128)S(1)} %get-tuple-element.110), channel_id=1, source_target_pairs={{4,0},{5,1},{6,2},{7,3},{12,8},{13,9},{14,10},{15,11},{20,16},{21,... | collective-permute-start | bytes 230408 | tf_op jit(solution)/shard_map/ppermute | solution.py:25
  169.5 0.7 copy-start.9
  173.9 26.5 %collective-permute-start.16 = (f32[5,10,38,3]{2,3,1,0:T(4,128)S(1)}, f32[5,10,38,3]{2,3,1,0:T(4,128)}, u32[]{:S(2)}, u32[]{:S(2)}) collective-permute-start(f32[5,10,38,3]{2,3,1,0:T(4,128)S(1)} %copy.160), channel_id=1, source_target_pairs={{0,1},{1,2},{2,3},{4,5},{5,6},{6,7},{8,9},{9,10},{10,11},{12,13},{... | collective-permute-start | bytes 68408 | tf_op jit(solution)/shard_map/ppermute | solution.py:24
  178.0 24.0 %collective-permute-start.17 = (f32[5,10,38,3]{2,3,1,0:T(4,128)}, f32[5,10,38,3]{2,3,1,0:T(4,128)}, u32[]{:S(2)}, u32[]{:S(2)}) collective-permute-start(f32[5,10,38,3]{2,3,1,0:T(4,128)} %copy.161), channel_id=1, source_target_pairs={{1,0},{2,1},{3,2},{5,4},{6,5},{7,6},{9,8},{10,9},{11,10},{13,12},{... | collective-permute-start | bytes 68408 | tf_op jit(solution)/shard_map/ppermute | solution.py:25
  200.4 4.4 copy-start.3
  200.4 4.4 copy-start.10
  212.0 7.3 %copy-start.6 = (f32[8,36,132]{2,1,0:T(8,128)S(1)}, f32[8,36,132]{2,1,0:T(8,128)}, u32[]{:S(2)}) copy-start(f32[8,36,132]{2,1,0:T(8,128)} %and_convert_fusion) | copy-start | bytes 456196
  235.5 10.1 %copy-start.13 = (f32[384,5]{1,0:T(8,128)S(1)}, f32[384,5]{1,0:T(8,128)}, u32[]{:S(2)}) copy-start(f32[384,5]{1,0:T(8,128)} %gather_fusion) | copy-start | bytes 23044
  235.5 10.1 %copy-start.14 = (f32[384,5]{1,0:T(8,128)S(1)}, f32[384,5]{1,0:T(8,128)}, u32[]{:S(2)}) copy-start(f32[384,5]{1,0:T(8,128)} %gather_fusion.1) | copy-start | bytes 23044
  235.5 10.1 %copy-start.22 = (pred[384]{0:T(512)(128)(4,1)S(1)}, pred[384]{0:T(512)(128)(4,1)}, u32[]{:S(2)}) copy-start(pred[384]{0:T(512)(128)(4,1)} %compare_and_fusion) | copy-start | bytes 1156
  256.1 1.2 copy-start.7
  256.1 1.2 copy-start.16
  256.1 1.2 copy-start.17
  256.1 1.2 copy-start.19
  257.3 1.4 copy-start.8
  257.3 1.4 copy-start.15
Sparse Core Ops, SparseCore 0:
  329.5 123.7 all-reduce.2
where the time goes:
time: 466 us; the launch traced here: 462 us
  waiting for transfers between devices  169 us (36%)
  other arithmetic  120 us (26%)
  local copies, waits for them, and re-layouts  80.8 us (17%)
  starting transfers between devices  38.6 us (8%)
  matrix products  37.3 us (8%)
  between operations  15.9 us (3%)
    unnamed x2, waiting for transfers between devices  123 us
    reduce_sum x8, other arithmetic, radiate(): jnp.sum(plus_weight * dip_real - minus_weight * dip_imag + sine * mono_re...  61.9 us
    dot_general x9, matrix products, stencil_rate(): jnp.einsum('dvw,dwxzr->vxzr', flux_jacobian, slopes, precision=lax.Precis...  35.9 us
    ppermute x9, waiting for transfers between devices, padded_2(): after = lax.ppermute(leading, axis, down)  28.7 us
    ppermute x9, starting transfers between devices, padded_2(): before = lax.ppermute(last, axis, up)  26.4 us
    another operation x9, other arithmetic, stencil_rate(): slopes = jnp.stack([along_x, along_z, along_r])  19.6 us
    ppermute x9, waiting for transfers between devices, padded_2(): before = lax.ppermute(last, axis, up)  17.2 us
    reshape x3, local copies, waits for them, and re-layouts, per_device(): sampled.append(jnp.take(current.reshape(5, -1), cell_ids, axis=1))  16.1 us
  transfers between devices with their start and end apart: 19, of which 15 were waited for; matrix products, arithmetic and copies ran while one was open for 8% of the time, Pallas kernels for 0%

commit v1 on v0

--- a/solution.py
+++ b/solution.py
@@ -1,8 +1,12 @@
+import functools
 import math
 
 import jax
 import jax.numpy as jnp
+import numpy as np
 from jax import lax
+from jax.experimental import pallas as pl
+from jax.experimental.pallas import tpu as pltpu
 from jax.sharding import PartitionSpec as P
 
 SURF_DEV = 128
@@ -86,7 +90,7 @@
     return jnp.concatenate([out_real, out_imag], axis=1)
 
 
-def per_device(flow_field, flux_jacobian, history, surface_cell, surface_blocks, observers):
+def general_device(flow_field, flux_jacobian, history, surface_cell, surface_blocks, observers):
     width_x, width_z, width_r = (flow_field.shape[1], flow_field.shape[2], flow_field.shape[3])
     count_x, count_z, count_r = (lax.axis_size("gx"), lax.axis_size("gz"), lax.axis_size("row"))
     index_x, index_z, index_r = (lax.axis_index("gx"), lax.axis_index("gz"), lax.axis_index("row"))
@@ -163,6 +167,590 @@
     return (current, spectrum)
 
 
+HALO = 3 * STEPS
+AXES = ("gx", "gz", "row")
+GROUP = ("gx", "gz")
+VMEM = pl.BlockSpec(memory_space=pltpu.VMEM)
+SMEM = pl.BlockSpec(memory_space=pltpu.SMEM)
+
+
+def halves(value, by):
+    if by & (by - 1) == 0:
+        return value >> (by.bit_length() - 1), value & (by - 1)
+    return value // by, value % by
+
+
+def sin_cos(angle):
+    turns = jnp.floor(angle * (2.0 / math.pi) + 0.5)
+    rest = ((angle - turns * 1.5703125) - turns * 4.837512969970703e-4) - turns * 7.549789954891882e-8
+    square = rest * rest
+    sine = rest + rest * square * (
+        -1.6666654611e-1 + square * (8.3321608736e-3 + square * -1.9515295891e-4)
+    )
+    cosine = (1.0 - 0.5 * square) + square * square * (
+        4.166664568298827e-2 + square * (-1.388731625493765e-3 + square * 2.443315711809948e-5)
+    )
+    quarter = turns.astype(jnp.int32) & 3
+    odd = (quarter & 1) == 1
+    out_sine = jnp.where(odd, cosine, sine)
+    out_cosine = jnp.where(odd, sine, cosine)
+    out_sine = jnp.where(quarter >= 2, -out_sine, out_sine)
+    out_cosine = jnp.where((quarter == 1) | (quarter == 2), -out_cosine, out_cosine)
+    return out_sine, out_cosine
+
+
+class Plan:
+    def __init__(self, mesh, flow, cells, hist, obs):
+        self.ax, self.az, self.rows = mesh["gx"], mesh["gz"], mesh["row"]
+        self.group = self.ax * self.az
+        self.devices = self.group * self.rows
+        self.wx, self.wz, self.wr = flow
+        self.blocks = cells[0]
+        self.capacity = cells[0] * cells[1]
+        self.samples = hist[2]
+        self.lanes = self.wx * self.wz
+        self.chunk = self.wr // self.group
+        self.nx, self.nz, self.nr = self.wx * self.ax, self.wz * self.az, self.wr * self.rows
+        self.obs = obs
+        self.body = 5 * self.chunk
+        self.sent = self.body + 8
+        self.per_obs = obs // self.devices
+
+    def fits(self):
+        return (
+            self.group == 8
+            and self.lanes == 128
+            and self.wr % 128 == 0
+            and self.chunk % 8 == 0
+            and self.chunk >= HALO
+            and self.capacity == self.blocks * 8
+            and self.blocks < 127
+            and self.capacity % 128 == 0
+            and self.samples == 128
+            and self.obs % 128 == 0
+            and self.obs % self.devices == 0
+            and FREQ == 32
+            and STEPS == 3
+        )
+
+    def order_of(self, a, b):
+        return b * self.ax + (a if b % 2 == 0 else self.ax - 1 - a)
+
+    def table(self):
+        return [self.order_of(j // self.az, j % self.az) for j in range(self.group)]
+
+    def line(self):
+        out = []
+        for c in range(self.rows):
+            order = self.table()
+            if c % 2:
+                order = [self.group - 1 - q for q in order]
+            for q in range(self.group):
+                out.append(order.index(q) * self.rows + c)
+        return out
+
+    def chunk_of(self, j, c):
+        q = self.table()[j]
+        return jnp.where(c % 2 == 1, self.group - 1 - q, q)
+
+    def own_chunk(self):
+        a, b, c = lax.axis_index("gx"), lax.axis_index("gz"), lax.axis_index("row")
+        q = b * self.ax + jnp.where(b % 2 == 0, a, self.ax - 1 - a)
+        return jnp.where(c % 2 == 1, self.group - 1 - q, q), c
+
+
+def call(kernel, out_shape, in_specs, out_specs, scratch=(), flops=10**6, name=None):
+    return pl.pallas_call(
+        kernel,
+        out_shape=out_shape,
+        in_specs=in_specs,
+        out_specs=out_specs,
+        scratch_shapes=list(scratch),
+        name=name,
+        compiler_params=pltpu.CompilerParams(vmem_limit_bytes=40 * 1024 * 1024),
+        cost_estimate=pl.CostEstimate(flops=flops, bytes_accessed=10**5, transcendentals=0),
+    )
+
+
+def pack_kernel(plan, flow_ref, cell_ref, live_ref, out_ref, turned):
+    c = lax.axis_index("row")
+    for v in range(5):
+        turned[v * plan.wr : (v + 1) * plan.wr, :] = flow_ref[v].T
+    cells = cell_ref[...].astype(jnp.float32)
+    wide = jnp.concatenate([cells, jnp.zeros((plan.blocks, 120), jnp.float32)], axis=1)
+    wide = jnp.concatenate([wide, jnp.zeros((128 - plan.blocks, 128), jnp.float32)], axis=0)
+    ids = wide.T[:8, :]
+    lane = lax.broadcasted_iota(jnp.int32, (8, 128), 1)
+    ids = jnp.where(lane == 127, live_ref[0, 0].astype(jnp.float32), ids)
+    for j in range(plan.group):
+        q = plan.chunk_of(j, c)
+        for v in range(5):
+            start = pl.multiple_of(v * plan.wr + q * plan.chunk, 8)
+            out_ref[j, v * plan.chunk : (v + 1) * plan.chunk, :] = turned[pl.ds(start, plan.chunk), :]
+        out_ref[j, plan.body : plan.body + 8, :] = ids
+
+
+def edge_kernel(plan, got_ref, first_ref, second_ref):
+    q, c = plan.own_chunk()
+    even = (c * plan.group + q) % 2 == 0
+    high, low = plan.chunk - HALO, 0
+    first = jnp.where(even, high, low)
+    second = jnp.where(even, low, high)
+    for v in range(5):
+        for i in range(HALO):
+            first_ref[v * HALO + i] = got_ref[pl.ds(v * plan.chunk + first + i, 8, stride=plan.sent), :]
+            second_ref[v * HALO + i] = got_ref[pl.ds(v * plan.chunk + second + i, 8, stride=plan.sent), :]
+
+
+def stencil_kernel(plan, got_ref, first_ref, second_ref, jac_ref, back_ref, samp_ref, cur, one, two, coef):
+    q, c = plan.own_chunk()
+    place = c * plan.group + q
+    even = place % 2 == 0
+    tall = plan.chunk + 2 * HALO
+    wz, lanes, az, ax, wx = plan.wz, plan.lanes, plan.az, plan.ax, plan.wx
+    has_low = jnp.where(place > 0, 1.0, 0.0)
+    has_high = jnp.where(place < plan.rows * plan.group - 1, 1.0, 0.0)
+    for d in range(3):
+        for v in range(5):
+            for w in range(5):
+                coef[(d * 5 + v) * 5 + w] = jnp.full((8, 128), jac_ref[d, v, w] * (0.5 * TIME_STEP), jnp.float32)
+    for v in range(5):
+        for i in range(plan.chunk):
+            cur[v * tall + HALO + i] = got_ref[pl.ds(v * plan.chunk + i, 8, stride=plan.sent), :]
+
+    def put(low_ref, high_ref):
+        for v in range(5):
+            for i in range(HALO):
+                cur[v * tall + i] = low_ref[v * HALO + i]
+                cur[v * tall + HALO + plan.chunk + i] = high_ref[v * HALO + i]
+
+    @pl.when(even)
+    def _():
+        put(second_ref, first_ref)
+
+    @pl.when(jnp.logical_not(even))
+    def _():
+        put(first_ref, second_ref)
+
+    lane = lax.broadcasted_iota(jnp.int32, (8, 128), 1)
+    sub = lax.broadcasted_iota(jnp.int32, (8, 128), 0)
+    x_l, z_l = halves(lane, wz)
+    a, b = halves(sub, az)
+    zero = jnp.zeros((8, 128), jnp.float32)
+
+    def shifts(value):
+        up = pltpu.roll(value, lanes - wz, 1)
+        x_next = jnp.where(x_l < wx - 1, up, jnp.where(a < ax - 1, pltpu.roll(up, 8 - az, 0), zero))
+        down = pltpu.roll(value, wz, 1)
+        x_prev = jnp.where(x_l > 0, down, jnp.where(a > 0, pltpu.roll(down, az, 0), zero))
+        up = pltpu.roll(pltpu.roll(value, wz - 1, 1), 7, 0)
+        z_next = jnp.where(z_l < wz - 1, pltpu.roll(value, lanes - 1, 1), jnp.where(b < az - 1, up, zero))
+        down = pltpu.roll(pltpu.roll(value, lanes - (wz - 1), 1), 1, 0)
+        z_prev = jnp.where(z_l > 0, pltpu.roll(value, 1, 1), jnp.where(b > 0, down, zero))
+        return x_next, x_prev, z_next, z_prev
+
+    damp = VISCOSITY * TIME_STEP
+
+    def stage(number, src, dst, keep, gain):
+        @pl.loop(0, tall // 2 - number)
+        def _(pair):
+            start = number + 2 * pair
+            total = [[None, None] for _ in range(5)]
+            slopes = []
+            for w in range(5):
+                column = [src[w * tall + start + k] for k in (-1, 0, 1, 2)]
+                per = []
+                for k in range(2):
+                    before, center, after = column[k : k + 3]
+                    x_next, x_prev, z_next, z_prev = shifts(center)
+                    around = ((x_next + x_prev) + (z_next + z_prev)) + (after + before)
+                    total[w][k] = (1.0 - 6.0 * damp) * center + damp * around
+                    per.append((x_next - x_prev, z_next - z_prev, after - before))
+                slopes.append(per)
+            for v in range(5):
+                for d in range(3):
+                    for w in range(5):
+                        factor = coef[(d * 5 + v) * 5 + w]
+                        for k in range(2):
+                            total[v][k] = total[v][k] + factor * slopes[w][k][d]
+            for k in range(2):
+                at = start + k
+                inside = jnp.where(at < HALO, has_low, jnp.where(at >= HALO + plan.chunk, has_high, 1.0))
+                for v in range(5):
+                    value = total[v][k]
+                    if keep:
+                        value = keep * cur[v * tall + at] + gain * value
+                    dst[v * tall + at] = value * inside
+
+    for step in range(STEPS):
+        stage(3 * step + 1, cur, one, 0.0, 1.0)
+        stage(3 * step + 2, one, two, 0.75, 0.25)
+        stage(3 * step + 3, two, cur, 1.0 / 3.0, 2.0 / 3.0)
+        for i in range(plan.chunk):
+            at = HALO + i
+            planes = [
+                cur[at] + cur[4 * tall + at],
+                cur[tall + at],
+                cur[2 * tall + at],
+                cur[3 * tall + at],
+            ]
+            for ch in range(4):
+                samp_ref[pl.ds(i * 128 + ch * STEPS + step, 8, stride=16), :] = planes[ch]
+    for v in range(5):
+        for i in range(plan.chunk):
+            back_ref[pl.ds(v * plan.chunk + i, 8, stride=plan.body), :] = cur[v * tall + HALO + i]
+
+
+def unpack_kernel(plan, back_ref, out_ref, turned):
+    c = lax.axis_index("row")
+    for j in range(plan.group):
+        q = plan.chunk_of(j, c)
+        for v in range(5):
+            start = pl.multiple_of(v * plan.wr + q * plan.chunk, 8)
+            turned[pl.ds(start, plan.chunk), :] = back_ref[j, v * plan.chunk : (v + 1) * plan.chunk, :]
+    for v in range(5):
+        out_ref[v] = turned[v * plan.wr : (v + 1) * plan.wr, :].T
+
+
+def list_kernel(plan, ids_ref, list_ref, count_ref):
+    mine, _ = plan.own_chunk()
+
+    def source(g, count):
+        def block(n, count):
+            for k in range(8):
+                cell = ids_ref[g * 8 + k, n]
+                lane, r = halves(cell, plan.wr)
+                q, r_l = halves(r, plan.chunk)
+                list_ref[count] = (r_l * 8 + g) * 128 + lane
+                count = count + jnp.where(q == mine, 1, 0)
+            return count
+
+        return lax.fori_loop(0, ids_ref[g * 8, 127], block, count)
+
+    count = lax.fori_loop(0, 8, source, 0)
+    count_ref[0] = count
+    for k in range(8):
+        list_ref[count + k] = 0
+
+
+def dft_kernel(plan, hist_ref, table_ref, live_ref, out_ref):
+    tile = pl.program_id(0)
+    live = live_ref[0, 0] * 8
+    keep = lax.broadcasted_iota(jnp.int32, (64, 128), 1) + tile * 128 < live
+    for ch in range(4):
+        signal = hist_ref[:, ch, :]
+        if ch == 0:
+            signal = signal + hist_ref[:, 4, :]
+        spec = lax.dot_general(
+            table_ref[...],
+            signal,
+            (((1,), (1,)), ((), ())),
+            precision=lax.Precision.HIGHEST,
+            preferred_element_type=jnp.float32,
+        )
+        out_ref[0, ch * 64 : (ch + 1) * 64, :] = jnp.where(keep, spec, 0.0)
+
+
+def geometry(plan, watch, point):
+    offset = [w - p for w, p in zip(watch, point, strict=True)]
+    square = offset[0] * offset[0] + offset[1] * offset[1] + offset[2] * offset[2]
+    distance = jnp.sqrt(square)
+    inverse = 1.0 / distance
+    along = [o * inverse for o in offset]
+    amplitude = plan.nr * inverse
+    sine, cosine = sin_cos(distance * (2.0 / plan.nr))
+    near = (plan.nr * 0.5) * inverse
+    return along, amplitude, sine, cosine, near
+
+
+def hist_kernel(plan, first, wide, watch_ref, point_ref, spec_ref, live_ref, out_ref, acc):
+    tiles = (live_ref[0, 0] * 8 + 127) // 128
+    lane = lax.broadcasted_iota(jnp.int32, (wide, 64), 1)
+
+    @pl.loop(0, out_ref.shape[0] // wide)
+    def _(ob):
+        start = pl.multiple_of(ob * wide, 8)
+        watch = [watch_ref[pl.ds(first + start, wide), d : d + 1] for d in range(3)]
+        acc[...] = jnp.zeros_like(acc)
+
+        @pl.loop(0, tiles)
+        def _(tile):
+            point = [point_ref[tile, d : d + 1, :] for d in range(3)]
+            along, amplitude, sine, cosine, near = geometry(plan, watch, point)
+            twice = 2.0 * cosine
+            cos_last, sin_last = amplitude, jnp.zeros_like(amplitude)
+            cos_now, sin_now = amplitude * cosine, amplitude * sine
+            for f in range(FREQ):
+                rows = [spec_ref[tile, pl.ds(k * 32 + f, 1), :] for k in range(8)]
+                d_re = along[0] * rows[2] + along[1] * rows[4] + along[2] * rows[6]
+                d_im = along[0] * rows[3] + along[1] * rows[5] + along[2] * rows[7]
+                weight = near * (1.0 / (f + 1))
+                e_re = (rows[0] + d_re) + weight * d_im
+                e_im = (rows[1] + d_im) - weight * d_re
+                acc[f] = acc[f] + (sin_now * e_re - cos_now * e_im)
+                acc[FREQ + f] = acc[FREQ + f] + (cos_now * e_re + sin_now * e_im)
+                cos_now, cos_last = twice * cos_now - cos_last, cos_now
+                sin_now, sin_last = twice * sin_now - sin_last, sin_now
+
+        out = jnp.zeros((wide, 64), jnp.float32)
+        for f in range(2 * FREQ):
+            out = jnp.where(lane == f, jnp.sum(acc[f], axis=1, keepdims=True), out)
+        out_ref[pl.ds(start, wide), :] = out
+
+
+def recent_kernel(plan, parts, list_ref, count_ref, samp_ref, obs_ref, tab_ref, *refs):
+    hist_refs, out_ref = refs[:parts], refs[parts]
+    value, place, cos_s, sin_s, mono, dip, acc, final = refs[parts + 1 :]
+    q, c = plan.own_chunk()
+    count = count_ref[0]
+    tiles = plan.obs // 128
+    lane = lax.broadcasted_iota(jnp.int32, (16, 128), 1)
+    acc[...] = jnp.zeros_like(acc)
+
+    @pl.loop(0, (count + 7) // 8)
+    def _(group):
+        for k in range(8):
+            entry = list_ref[group * 8 + k]
+            row, at = halves(entry, 128)
+            tile = samp_ref[pl.ds(pl.multiple_of(row * 16, 16), 16), :]
+            at = jnp.where(group * 8 + k < count, at, -1)
+            picked = jnp.sum(jnp.where(lane == at, tile, 0.0), axis=1, keepdims=True)
+            value[k * 16 : (k + 1) * 16, :] = jnp.broadcast_to(picked, (16, 128))
+            r_l, g = halves(row, 8)
+            a, b = halves(g, plan.az)
+            _, at = halves(entry, 128)
+            x_l, z_l = halves(at, plan.wz)
+            spot = (a * plan.wx + x_l, b * plan.wz + z_l, c * plan.wr + q * plan.chunk + r_l)
+            for d in range(3):
+                place[d * 8 + k : d * 8 + k + 1, :] = jnp.full((1, 128), spot[d].astype(jnp.float32) + 0.5)
+        point = [place[d * 8 : (d + 1) * 8, :] for d in range(3)]
+        for t in range(tiles):
+            seen = obs_ref[:, t * 128 : (t + 1) * 128]
+            watch = [
+                seen[0:1] * float(plan.nx),
+                seen[1:2] * float(plan.nz),
+                (1.25 + 0.75 * seen[2:3]) * float(plan.nr),
+            ]
+            along, amplitude, sine, cosine, near = geometry(plan, watch, point)
+            for s in range(STEPS):
+                drawn = [value[pl.ds(ch * STEPS + s, 8, stride=16), :] for ch in range(4)]
+                push = along[0] * drawn[1] + along[1] * drawn[2] + along[2] * drawn[3]
+                mono[s * 8 : (s + 1) * 8, :] = drawn[0] + push
+                dip[s * 8 : (s + 1) * 8, :] = near * push
+            twice = 2.0 * cosine
+            cos_last, sin_last = amplitude, jnp.zeros_like(amplitude)
+            cos_now, sin_now = amplitude * cosine, amplitude * sine
+            for f in range(FREQ):
+                cos_s[f * 8 : (f + 1) * 8, :] = cos_now
+                sin_s[f * 8 : (f + 1) * 8, :] = sin_now
+                cos_now, cos_last = twice * cos_now - cos_last, cos_now
+                sin_now, sin_last = twice * sin_now - sin_last, sin_now
+            for fv in range(FREQ // 8):
+                base = (t * (FREQ // 8) + fv) * 12
+                sums = [acc[base + i] for i in range(12)]
+                for k in range(8):
+                    wave_c = cos_s[pl.ds(fv * 64 + k, 8, stride=8), :]
+                    wave_s = sin_s[pl.ds(fv * 64 + k, 8, stride=8), :]
+                    for s in range(STEPS):
+                        m = mono[s * 8 + k : s * 8 + k + 1, :]
+                        p = dip[s * 8 + k : s * 8 + k + 1, :]
+                        sums[4 * s] = sums[4 * s] + wave_c * m
+                        sums[4 * s + 1] = sums[4 * s + 1] + wave_s * m
+                        sums[4 * s + 2] = sums[4 * s + 2] + wave_c * p
+                        sums[4 * s + 3] = sums[4 * s + 3] + wave_s * p
+                for i in range(12):
+                    acc[base + i] = sums[i]
+
+    scale = 1.0 / math.sqrt(plan.devices * SURF_DEV)
+    final[...] = jnp.zeros_like(final)
+    for t in range(tiles):
+        for fv in range(FREQ // 8):
+            base = (t * (FREQ // 8) + fv) * 12
+            column = tab_ref[fv * 8 : (fv + 1) * 8, :]
+            out_re = jnp.zeros((8, 128), jnp.float32)
+            out_im = jnp.zeros((8, 128), jnp.float32)
+            below = column[:, 6:7]
+            for s in range(STEPS):
+                part_re = acc[base + 4 * s + 1] + acc[base + 4 * s + 2] * below
+                part_im = acc[base + 4 * s] - acc[base + 4 * s + 3] * below
+                turn_re, turn_im = column[:, 2 * s : 2 * s + 1], column[:, 2 * s + 1 : 2 * s + 2]
+                out_re = out_re + (turn_re * part_re - turn_im * part_im)
+                out_im = out_im + (turn_im * part_re + turn_re * part_im)
+            final[fv * 8 : (fv + 1) * 8, :] = out_re
+            final[FREQ + fv * 8 : FREQ + (fv + 1) * 8, :] = out_im
+        across = final[...].T[:, : 2 * FREQ]
+        share = plan.obs // parts
+        for i in range(128 // share):
+            piece = across[i * share : (i + 1) * share, :]
+            row = t * 128 + i * share
+            out_ref[row : row + share, :] = (piece + hist_refs[row // share][...]) * scale
+
+
+def fourier_numpy(samples):
+    turn = np.arange(1, FREQ + 1)[:, None] * np.arange(samples)[None, :] % samples
+    angle = 2.0 * np.pi / samples * turn
+    return np.cos(angle) / np.sqrt(samples), -np.sin(angle) / np.sqrt(samples)
+
+
+def fast_device(plan, flow_field, flux_jacobian, history, surface_cell, surface_blocks, observers):
+    f32 = jnp.float32
+    shape = jax.ShapeDtypeStruct
+    group, wr, lanes = plan.group, plan.wr, plan.lanes
+    tall = plan.chunk + 2 * HALO
+    parts = 4
+    bind = functools.partial
+
+    packed = call(
+        bind(pack_kernel, plan),
+        shape((group, plan.sent, lanes), f32),
+        [VMEM, VMEM, SMEM],
+        VMEM,
+        [pltpu.VMEM((5 * wr, lanes), f32)],
+        name="pack",
+    )(flow_field.reshape(5, lanes, wr), surface_cell, surface_blocks)
+    got = lax.all_to_all(packed, GROUP, 0, 0, tiled=True)
+
+    tile_count = plan.capacity // 128
+    cos_t, sin_t = fourier_numpy(plan.samples)
+    table = np.concatenate([cos_t, sin_t], axis=0).astype(np.float32)
+    table[:, plan.samples - STEPS :] = 0.0
+    spec = pl.pallas_call(
+        bind(dft_kernel, plan),
+        out_shape=shape((tile_count, 256, 128), f32),
+        grid=(tile_count,),
+        in_specs=[
+            pl.BlockSpec((128, 5, plan.samples), lambda i: (i, 0, 0)),
+            pl.BlockSpec((64, plan.samples), lambda i: (0, 0)),
+            SMEM,
+        ],
+        out_specs=pl.BlockSpec((1, 256, 128), lambda i: (i, 0, 0)),
+        name="dft",
+        compiler_params=pltpu.CompilerParams(vmem_limit_bytes=40 * 1024 * 1024),
+        cost_estimate=pl.CostEstimate(flops=10**9, bytes_accessed=10**6, transcendentals=0),
+    )(history, jnp.asarray(table), surface_blocks)
+
+    cell = surface_cell.reshape(-1)
+    index_x, index_z, index_r = (lax.axis_index(name) for name in AXES)
+    points = jnp.stack(
+        [
+            index_x * plan.wx + cell // (plan.wz * wr),
+            index_z * plan.wz + cell // wr % plan.wz,
+            index_r * wr + cell % wr,
+        ]
+    ).astype(f32) + 0.5
+    points = jnp.transpose(points.reshape(3, tile_count, 128), (1, 0, 2))
+    watch = jnp.stack(
+        [
+            observers[0] * plan.nx,
+            observers[1] * plan.nz,
+            (1.25 + 0.75 * observers[2]) * plan.nr,
+        ],
+        axis=1,
+    )
+    share = plan.obs // parts
+    wide = 16
+    hists = []
+    for i in range(parts):
+        hists.append(
+            call(
+                bind(hist_kernel, plan, i * share, wide),
+                shape((share, 64), f32),
+                [VMEM, VMEM, VMEM, SMEM],
+                VMEM,
+                [pltpu.VMEM((64, wide, 128), f32)],
+                flops=10**9,
+                name=f"hist{i}",
+            )(watch, points, spec, surface_blocks)
+        )
+
+    flat = got.reshape(group * plan.sent, lanes)
+    first, second = call(
+        bind(edge_kernel, plan),
+        (shape((5 * HALO, 8, lanes), f32),) * 2,
+        [VMEM],
+        (VMEM, VMEM),
+        name="edges",
+    )(flat)
+    line = plan.line()
+    swap_a = [(line[i], line[i ^ 1]) for i in range(len(line))]
+    swap_b = [
+        (line[i], line[((i + 1) ^ 1) - 1]) for i in range(1, len(line) - 1)
+    ]
+    first = lax.ppermute(first, AXES, swap_a)
+    second = lax.ppermute(second, AXES, swap_b)
+
+    ids = got[:, plan.body :, :].astype(jnp.int32).reshape(group * 8, lanes)
+    listed, count = call(
+        bind(list_kernel, plan),
+        (shape((group * plan.capacity + 8,), jnp.int32), shape((1,), jnp.int32)),
+        [SMEM],
+        (SMEM, SMEM),
+        name="list",
+    )(ids)
+
+    back, samp = call(
+        bind(stencil_kernel, plan),
+        (shape((group * plan.body, lanes), f32), shape((plan.chunk * 8 * 16, lanes), f32)),
+        [VMEM, VMEM, VMEM, SMEM],
+        (VMEM, VMEM),
+        [
+            pltpu.VMEM((5 * tall, 8, lanes), f32),
+            pltpu.VMEM((5 * tall, 8, lanes), f32),
+            pltpu.VMEM((5 * tall, 8, lanes), f32),
+            pltpu.VMEM((75, 8, lanes), f32),
+        ],
+        flops=10**9,
+        name="stencil",
+    )(flat, first, second, flux_jacobian)
+    back = lax.all_to_all(back.reshape(group, plan.body, lanes), GROUP, 0, 0, tiled=True)
+
+    columns = np.zeros((FREQ, 8), np.float32)
+    for s in range(STEPS):
+        columns[:, 2 * s] = cos_t[:, plan.samples - STEPS + s]
+        columns[:, 2 * s + 1] = sin_t[:, plan.samples - STEPS + s]
+    columns[:, 6] = 1.0 / np.arange(1, FREQ + 1)
+    partial = call(
+        bind(recent_kernel, plan, parts),
+        shape((plan.obs, 2 * FREQ), f32),
+        [SMEM, SMEM, VMEM, VMEM, VMEM] + [VMEM] * parts,
+        VMEM,
+        [
+            pltpu.VMEM((128, 128), f32),
+            pltpu.VMEM((24, 128), f32),
+            pltpu.VMEM((FREQ * 8, 128), f32),
+            pltpu.VMEM((FREQ * 8, 128), f32),
+            pltpu.VMEM((STEPS * 8, 128), f32),
+            pltpu.VMEM((STEPS * 8, 128), f32),
+            pltpu.VMEM((plan.obs // 128 * (FREQ // 8) * 12, 8, 128), f32),
+            pltpu.VMEM((128, 128), f32),
+        ],
+        flops=10**9,
+        name="recent",
+    )(listed, count, samp, observers, jnp.asarray(columns), *hists)
+    pieces = lax.all_to_all(
+        partial.reshape(plan.devices, plan.per_obs, 2 * FREQ), AXES, 0, 0, tiled=True
+    )
+    spectrum = jnp.sum(pieces, axis=0)
+    field = call(
+        bind(unpack_kernel, plan),
+        shape((5, lanes, wr), f32),
+        [VMEM],
+        VMEM,
+        [pltpu.VMEM((5 * wr, lanes), f32)],
+        name="unpack",
+    )(back)
+    return field.reshape(flow_field.shape), spectrum
+
+
+def per_device(*args):
+    flow_field, _, history, surface_cell, _, observers = args
+    mesh = {name: lax.axis_size(name) for name in AXES}
+    plan = Plan(mesh, flow_field.shape[1:], surface_cell.shape, history.shape, observers.shape[1])
+    if plan.fits():
+        return fast_device(plan, *args)
+    return general_device(*args)
+
+
 def solution(mesh):
     return jax.shard_map(
         per_device,

time: 466 us -> 104 us (0.22)
  waiting for transfers between devices: 169 us -> 8.72 us
  other arithmetic: 120 us -> 2.3 us
  local copies, waits for them, and re-layouts: 80.8 us -> 3.32 us
  Pallas kernels: 0 us -> 48.7 us
  matrix products: 37.3 us -> 0 us
  blocking collectives: 0 us -> 25.6 us
  starting transfers between devices: 38.6 us -> 13.6 us
  between operations: 15.9 us -> 1.49 us
    unnamed x2 -> x0, waiting for transfers between devices: 123 us -> none
    reduce_sum x16 -> x1, other arithmetic: 62.5 us -> 0.63 us  [fast_device(): spectrum = jnp.sum(pieces, axis=0)]
    pallas_call x0 -> x11, Pallas kernels: none -> 48.7 us  [the longest x1 20.1 us: fast_device(): call(bind(stencil_kernel, plan), (shape((group * plan.body, lanes), f32),...]
    ppermute x18 -> x2, waiting for transfers between devices: 45.9 us -> 0.01 us  [the longest x1 0.01 us: fast_device(): first = lax.ppermute(first, AXES, swap_a)]
    dot_general x10 -> x0, matrix products: 37.3 us -> none  [the longest x9 35.9 us: stencil_rate(): jnp.einsum('dvw,dwxzr->vxzr', flux_jacobian, slopes, precision=lax.Precis...]
    ppermute x18 -> x2, starting transfers between devices: 38.5 us -> 2.73 us  [the longest x1 2.07 us: fast_device(): first = lax.ppermute(first, AXES, swap_a)]
    all_to_all x0 -> x1, blocking collectives: none -> 25.6 us  [fast_device(): lax.all_to_all(partial.reshape(plan.devices, plan.per_obs, 2 * FREQ), AXE...]
    another operation x11 -> x1, other arithmetic: 21 us -> 0.01 us  [fast_device(): jnp.stack([observers[0] * plan.nx, observers[1] * plan.nz, (1.25 + 0.75 *...]
  transfers between devices with their start and end apart: 19 -> 4, of which waited for: 15 -> 1; matrix products, arithmetic and copies ran while one was open for 8% -> 4% of each run, Pallas kernels for 0% -> 18%
where the time goes in v1:
time: 104 us
  Pallas kernels  48.7 us (47%)
  blocking collectives  25.6 us (25%)
  starting transfers between devices  13.6 us (13%)
  waiting for transfers between devices  8.72 us (8%)
  local copies, waits for them, and re-layouts  3.32 us (3%)
  other arithmetic  2.3 us (2%)
  between operations  1.49 us (1%)
    all_to_all x1, blocking collectives, fast_device(): lax.all_to_all(partial.reshape(plan.devices, plan.per_obs, 2 * FREQ), AXE...  25.6 us
    pallas_call x1, Pallas kernels, fast_device(): call(bind(stencil_kernel, plan), (shape((group * plan.body, lanes), f32),...  20.1 us
    pallas_call x4, Pallas kernels, fast_device(): call(bind(hist_kernel, plan, i * share, wide), shape((share, 64), f32), [...  9.5 us
    all_to_all x1, waiting for transfers between devices, fast_device(): lax.all_to_all(back.reshape(group, plan.body, lanes), GROUP, 0, 0, tiled=...  8.72 us
    pallas_call x1, Pallas kernels, fast_device(): call(bind(list_kernel, plan), (shape((group * plan.capacity + 8,), jnp.in...  7.65 us
    pallas_call x1, Pallas kernels, fast_device(): call(bind(recent_kernel, plan, parts), shape((plan.obs, 2 * FREQ), f32),...  7.62 us
    all_to_all x1, starting transfers between devices, fast_device(): got = lax.all_to_all(packed, GROUP, 0, 0, tiled=True)  7.44 us
    all_to_all x1, starting transfers between devices, fast_device(): lax.all_to_all(back.reshape(group, plan.body, lanes), GROUP, 0, 0, tiled=...  3.43 us
  transfers between devices with their start and end apart: 4, of which 1 were waited for; matrix products, arithmetic and copies ran while one was open for 4% of the time, Pallas kernels for 18%

profile of v1, /device:TPU:0, one launch (start us, length us, event | category | flops | bytes accessed | tf_op | source)
XLA Modules:
  0.0 103.7 jit_solution(217632065019650216)
XLA Ops:
  0.6 0.8 copy.25.cell_ref
  2.0 0.0 copy-start
  2.1 1.0 copy-done
  3.0 0.0 copy-start.4
  3.0 0.9 pack.1
  4.0 0.0 copy-start.5
  4.0 7.4 %all-to-all-start = ((f32[8,88,128]{2,1,0:T(8,128)}), f32[8,88,128]{2,1,0:T(8,128)S(1)}, u32[]{:S(2)}, u32[]{:S(2)}) async-start(f32[8,88,128]{2,1,0:T(8,128)} %pack.1), calls=%async_computation | async-start | bytes 720896 | tf_op jit(solution)/shard_map/all_to_all | solution.py:611
  11.4 0.0 copy-start.2
  11.4 0.1 reshape.280
  11.5 0.8 multiply_bitcast_fusion.2
  12.4 0.1 copy.33.watch_ref
  12.5 0.0 copy-done.4
  12.5 0.6 copy.32.hist_ref
  13.1 0.0 copy-done.5
  13.1 0.0 copy-done.2
  13.2 2.0 %dft.1.spec_ref = f32[3,256,128]{2,1,0:T(8,128)S(1)} custom-call(f32[384,5,128]{2,1,0:T(8,128)S(1)} %copy.32.hist_ref, f32[64,128]{1,0:T(8,128)S(1)} %copy-done.2, s32[1,1]{1,0:T(1,128)S(6)} %copy.37.live_ref), custom_call_target="tpu_custom_call" | custom-call | flops 1000000000 | bytes 1000000 | tf_op jit(solution)/shard_map/dft/pallas_call | solution.py:617
  15.1 2.4 %hist0.1.refs_0_ = f32[64,64]{1,0:T(8,128)S(1)} custom-call(f32[256,3]{1,0:T(8,128)S(1)} %copy.33.watch_ref, f32[3,3,128]{2,1,0:T(4,128)S(1)} %fusion.2.point_ref, f32[3,256,128]{2,1,0:T(8,128)S(1)} %dft.1.spec_ref, s32[1,1]{1,0:T(1,128)S(6)} %copy.37.live_ref), custom_call_target="tpu_custom_call" | custom-call | flops 1000000000 | bytes 100000 | tf_op jit(solution)/shard_map/hist0/pallas_call | solution.py:655
  17.5 2.4 %hist1.1.refs_1_ = f32[64,64]{1,0:T(8,128)S(1)} custom-call(f32[256,3]{1,0:T(8,128)S(1)} %copy.33.watch_ref, f32[3,3,128]{2,1,0:T(4,128)S(1)} %fusion.2.point_ref, f32[3,256,128]{2,1,0:T(8,128)S(1)} %dft.1.spec_ref, s32[1,1]{1,0:T(1,128)S(6)} %copy.37.live_ref), custom_call_target="tpu_custom_call" | custom-call | flops 1000000000 | bytes 100000 | tf_op jit(solution)/shard_map/hist1/pallas_call | solution.py:655
  19.9 2.4 %hist2.1.refs_2_ = f32[64,64]{1,0:T(8,128)S(1)} custom-call(f32[256,3]{1,0:T(8,128)S(1)} %copy.33.watch_ref, f32[3,3,128]{2,1,0:T(4,128)S(1)} %fusion.2.point_ref, f32[3,256,128]{2,1,0:T(8,128)S(1)} %dft.1.spec_ref, s32[1,1]{1,0:T(1,128)S(6)} %copy.37.live_ref), custom_call_target="tpu_custom_call" | custom-call | flops 1000000000 | bytes 100000 | tf_op jit(solution)/shard_map/hist2/pallas_call | solution.py:655
  22.3 2.4 %hist3.1.refs_3_ = f32[64,64]{1,0:T(8,128)S(1)} custom-call(f32[256,3]{1,0:T(8,128)S(1)} %copy.33.watch_ref, f32[3,3,128]{2,1,0:T(4,128)S(1)} %fusion.2.point_ref, f32[3,256,128]{2,1,0:T(8,128)S(1)} %dft.1.spec_ref, s32[1,1]{1,0:T(1,128)S(6)} %copy.37.live_ref), custom_call_target="tpu_custom_call" | custom-call | flops 1000000000 | bytes 100000 | tf_op jit(solution)/shard_map/hist3/pallas_call | solution.py:655
  24.7 0.0 all-to-all-done
  24.7 0.1 edges.1
  24.8 2.1 %collective-permute-start = (f32[45,8,128]{2,1,0:T(8,128)S(1)}, f32[45,8,128]{2,1,0:T(8,128)S(1)}, u32[]{:S(2)}, u32[]{:S(2)}) collective-permute-start(f32[45,8,128]{2,1,0:T(8,128)S(1)} %get-tuple-element.8), channel_id=1, source_target_pairs={{0,8},{8,0},{16,24},{24,16},{28,20},{20,28},{12,4},{4,12},{5,13},{... | collective-permute-start | bytes 552968 | tf_op jit(solution)/shard_map/ppermute | solution.py:679
  26.8 0.7 collective-permute-start.1
  27.5 7.6 %list.1 = (s32[3080]{0:T(1024)S(1)}, s32[1]{0:T(128)}) custom-call(s32[64,128]{1,0:T(8,128)S(1)} %fusion.ids_ref), custom_call_target="tpu_custom_call" | custom-call | flops 1000000 | bytes 100000 | tf_op jit(solution)/shard_map/list/pallas_call | solution.py:683
  35.2 0.0 copy-start.1
  35.2 0.0 copy-start.3
  35.2 0.0 collective-permute-done.first_ref
  35.2 0.0 collective-permute-done.1.second_ref
  35.2 20.1 %stencil.1 = (f32[640,128]{1,0:T(8,128)}, f32[2048,128]{1,0:T(8,128)S(1)}) custom-call(f32[704,128]{1,0:T(8,128)S(1)} %bitcast.16, f32[45,8,128]{2,1,0:T(8,128)S(1)} %collective-permute-done.first_ref, f32[45,8,128]{2,1,0:T(8,128)S(1)} %collective-permute-done.1.second_ref, f32[3,5,5]{2,1,0:T(8,128)S(1)} %copy.26.jac_ref), custom_call_target="tpu_custom_call" | custom-call | flops 1000000000 | bytes 100000 | tf_op jit(solution)/shard_map/stencil/pallas_call | solution.py:691
  55.3 0.0 copy-done.1
  55.3 0.0 copy-done.3
  55.3 7.6 %recent.1 = f32[256,64]{1,0:T(8,128)S(1)} custom-call(s32[3080]{0:T(1024)S(1)} %get-tuple-element.11.list_ref, s32[1]{0:T(128)} %get-tuple-element.12.count_ref, f32[2048,128]{1,0:T(8,128)S(1)} %get-tuple-element.13.samp_ref, f32[3,256]{1,0:T(4,128)S(1)} %copy-done.1, f32[32,8]{1,0:T(8,128)S(1)} %copy-done.3, f32[64,64]{1,0:T(8,128)S(1)} %hist0.1.refs_0_, ...), custom_call_target="tpu_custom_call" | custom-call | flops 1000000000 | bytes 100000 | tf_op jit(solution)/shard_map/recent/pallas_call | solution.py:712
  62.9 0.1 reshape.281
  63.1 25.6 %all_to_all.15 = f32[32,1,512]{2,1,0:T(1,128)S(1)} all-to-all(f32[32,1,512]{2,1,0:T(1,128)S(1)} %reshape.281), channel_id=1, replica_groups=mesh['gx'=4,'gz'=2,'row'=4] {'gx','gz','row'}, dimensions={0} | all-to-all | bytes 131072 | tf_op jit(solution)/shard_map/all_to_all | solution.py:730
  88.6 3.4 %all-to-all-start.1 = ((f32[8,80,128]{2,1,0:T(8,128)}), f32[8,80,128]{2,1,0:T(8,128)S(1)}, u32[]{:S(2)}, u32[]{:S(2)}) async-start(f32[8,80,128]{2,1,0:T(8,128)} %bitcast.2), calls=%async_computation.1 | async-start | bytes 655360 | tf_op jit(solution)/shard_map/all_to_all | solution.py:705
  92.1 0.5 broadcast.276
  92.6 0.8 reduce
  93.4 0.1 reshape.282
  93.5 0.6 reduce_sum.9
  94.1 8.7 %all-to-all-done.1.back_ref = f32[8,80,128]{2,1,0:T(8,128)S(1)} async-done(((f32[8,80,128]{2,1,0:T(8,128)}), f32[8,80,128]{2,1,0:T(8,128)S(1)}, u32[]{:S(2)}, u32[]{:S(2)}) %all-to-all-start.1) | async-done | bytes 327712 | tf_op jit(solution)/shard_map/all_to_all | solution.py:705
  102.8 0.9 unpack.1
  (5 shorter events, 0.1 us)
Async XLA Ops:
  2.0 1.0 copy-start
  3.0 9.5 %copy-start.4 = (f32[384,5,128]{2,0,1:T(8,128)S(1)}, f32[384,5,128]{2,0,1:T(8,128)}, u32[]{:S(2)}) copy-start(f32[384,5,128]{2,0,1:T(8,128)} %param.10) | copy-start | bytes 2949124
  4.0 9.2 %copy-start.5 = (f32[3,5,5]{2,0,1:T(4,128)S(1)}, f32[3,5,5]{2,0,1:T(4,128)}, u32[]{:S(2)}) copy-start(f32[3,5,5]{2,0,1:T(4,128)} %param.9) | copy-start | bytes 904
  4.0 20.7 %all-to-all-start = ((f32[8,88,128]{2,1,0:T(8,128)}), f32[8,88,128]{2,1,0:T(8,128)S(1)}, u32[]{:S(2)}, u32[]{:S(2)}) async-start(f32[8,88,128]{2,1,0:T(8,128)} %pack.1), calls=%async_computation | async-start | bytes 720896 | tf_op jit(solution)/shard_map/all_to_all | solution.py:611
  11.4 1.8 %copy-start.2 = (f32[64,128]{1,0:T(8,128)S(1)}, f32[64,128]{1,0:T(8,128)}, u32[]{:S(2)}) copy-start(f32[64,128]{1,0:T(8,128)} %constant.82.clone.table_ref) | copy-start | bytes 98308
  24.8 10.4 %collective-permute-start = (f32[45,8,128]{2,1,0:T(8,128)S(1)}, f32[45,8,128]{2,1,0:T(8,128)S(1)}, u32[]{:S(2)}, u32[]{:S(2)}) collective-permute-start(f32[45,8,128]{2,1,0:T(8,128)S(1)} %get-tuple-element.8), channel_id=1, source_target_pairs={{0,8},{8,0},{16,24},{24,16},{28,20},{20,28},{12,4},{4,12},{5,13},{... | collective-permute-start | bytes 552968 | tf_op jit(solution)/shard_map/ppermute | solution.py:679
  26.8 8.4 %collective-permute-start.1 = (f32[45,8,128]{2,1,0:T(8,128)S(1)}, f32[45,8,128]{2,1,0:T(8,128)S(1)}, u32[]{:S(2)}, u32[]{:S(2)}) collective-permute-start(f32[45,8,128]{2,1,0:T(8,128)S(1)} %get-tuple-element.9), channel_id=1, source_target_pairs={{8,16},{16,8},{24,28},{28,24},{20,12},{12,20},{4,5},{5,4},{13,21},... | collective-permute-start | bytes 552968 | tf_op jit(solution)/shard_map/ppermute | solution.py:680
  35.2 20.1 %copy-start.1 = (f32[3,256]{1,0:T(4,128)S(1)}, f32[3,256]{1,0:T(4,128)}, u32[]{:S(2)}) copy-start(f32[3,256]{1,0:T(4,128)} %obs_ref.1) | copy-start | bytes 9220
  35.2 20.1 %copy-start.3 = (f32[32,8]{1,0:T(8,128)S(1)}, f32[32,8]{1,0:T(8,128)}, u32[]{:S(2)}) copy-start(f32[32,8]{1,0:T(8,128)} %constant.83.clone.tab_ref) | copy-start | bytes 3076
  88.6 14.2 %all-to-all-start.1 = ((f32[8,80,128]{2,1,0:T(8,128)}), f32[8,80,128]{2,1,0:T(8,128)S(1)}, u32[]{:S(2)}, u32[]{:S(2)}) async-start(f32[8,80,128]{2,1,0:T(8,128)} %bitcast.2), calls=%async_computation.1 | async-start | bytes 655360 | tf_op jit(solution)/shard_map/all_to_all | solution.py:705

commit v2 on v1

--- a/solution.py
+++ b/solution.py
@@ -215,6 +215,7 @@
         self.body = 5 * self.chunk
         self.sent = self.body + 8
         self.per_obs = obs // self.devices
+        self.tall_pad = (self.chunk + 2 * HALO + 8) // 8 * 8 + 8
 
     def fits(self):
         return (
@@ -229,6 +230,7 @@
             and self.samples == 128
             and self.obs % 128 == 0
             and self.obs % self.devices == 0
+            and self.obs // self.devices == 8
             and FREQ == 32
             and STEPS == 3
         )
@@ -277,9 +279,7 @@
     for v in range(5):
         turned[v * plan.wr : (v + 1) * plan.wr, :] = flow_ref[v].T
     cells = cell_ref[...].astype(jnp.float32)
-    wide = jnp.concatenate([cells, jnp.zeros((plan.blocks, 120), jnp.float32)], axis=1)
-    wide = jnp.concatenate([wide, jnp.zeros((128 - plan.blocks, 128), jnp.float32)], axis=0)
-    ids = wide.T[:8, :]
+    ids = jnp.concatenate([cells, jnp.zeros((8, 128 - plan.blocks), jnp.float32)], axis=1)
     lane = lax.broadcasted_iota(jnp.int32, (8, 128), 1)
     ids = jnp.where(lane == 127, live_ref[0, 0].astype(jnp.float32), ids)
     for j in range(plan.group):
@@ -297,32 +297,54 @@
     first = jnp.where(even, high, low)
     second = jnp.where(even, low, high)
     for v in range(5):
-        for i in range(HALO):
-            first_ref[v * HALO + i] = got_ref[pl.ds(v * plan.chunk + first + i, 8, stride=plan.sent), :]
-            second_ref[v * HALO + i] = got_ref[pl.ds(v * plan.chunk + second + i, 8, stride=plan.sent), :]
-
-
-def stencil_kernel(plan, got_ref, first_ref, second_ref, jac_ref, back_ref, samp_ref, cur, one, two, coef):
+        for g in range(plan.group):
+            at = (v * plan.group + g) * HALO
+            row = g * plan.sent + v * plan.chunk
+            first_ref[at : at + HALO, :] = got_ref[pl.ds(row + first, HALO), :]
+            second_ref[at : at + HALO, :] = got_ref[pl.ds(row + second, HALO), :]
+
+
+def stencil_kernel(plan, got_ref, first_ref, second_ref, jac_ref, back_ref, samp_ref, cur, one, two, coef, mask, side):
     q, c = plan.own_chunk()
     place = c * plan.group + q
     even = place % 2 == 0
     tall = plan.chunk + 2 * HALO
     wz, lanes, az, ax, wx = plan.wz, plan.lanes, plan.az, plan.ax, plan.wx
+    high = plan.tall_pad
+    per = (ax + 2) * az * high
+
+    def base(v, a, b):
+        return v * per + ((a + 1) * az + b) * high
+
     has_low = jnp.where(place > 0, 1.0, 0.0)
     has_high = jnp.where(place < plan.rows * plan.group - 1, 1.0, 0.0)
+    row = lax.broadcasted_iota(jnp.int32, (high, 128), 0)
+    mask[...] = jnp.where(row < HALO, has_low, jnp.where(row >= HALO + plan.chunk, has_high, 1.0))
     for d in range(3):
         for v in range(5):
             for w in range(5):
                 coef[(d * 5 + v) * 5 + w] = jnp.full((8, 128), jac_ref[d, v, w] * (0.5 * TIME_STEP), jnp.float32)
+    zeros = jnp.zeros((az * high, 128), jnp.float32)
+    for ref in (cur, one, two):
+        for v in range(5):
+            for a in (-1, ax):
+                ref[base(v, a, 0) : base(v, a, 0) + az * high, :] = zeros
     for v in range(5):
-        for i in range(plan.chunk):
-            cur[v * tall + HALO + i] = got_ref[pl.ds(v * plan.chunk + i, 8, stride=plan.sent), :]
+        for a in range(ax):
+            for b in range(az):
+                at = base(v, a, b) + HALO
+                source = (a * az + b) * plan.sent + v * plan.chunk
+                cur[at : at + plan.chunk, :] = got_ref[source : source + plan.chunk, :]
 
     def put(low_ref, high_ref):
         for v in range(5):
-            for i in range(HALO):
-                cur[v * tall + i] = low_ref[v * HALO + i]
-                cur[v * tall + HALO + plan.chunk + i] = high_ref[v * HALO + i]
+            for a in range(ax):
+                for b in range(az):
+                    at = base(v, a, b)
+                    source = (v * plan.group + a * az + b) * HALO
+                    cur[at : at + HALO, :] = low_ref[source : source + HALO, :]
+                    at = at + HALO + plan.chunk
+                    cur[at : at + HALO, :] = high_ref[source : source + HALO, :]
 
     @pl.when(even)
     def _():
@@ -333,72 +355,88 @@
         put(first_ref, second_ref)
 
     lane = lax.broadcasted_iota(jnp.int32, (8, 128), 1)
-    sub = lax.broadcasted_iota(jnp.int32, (8, 128), 0)
     x_l, z_l = halves(lane, wz)
-    a, b = halves(sub, az)
     zero = jnp.zeros((8, 128), jnp.float32)
-
-    def shifts(value):
-        up = pltpu.roll(value, lanes - wz, 1)
-        x_next = jnp.where(x_l < wx - 1, up, jnp.where(a < ax - 1, pltpu.roll(up, 8 - az, 0), zero))
-        down = pltpu.roll(value, wz, 1)
-        x_prev = jnp.where(x_l > 0, down, jnp.where(a > 0, pltpu.roll(down, az, 0), zero))
-        up = pltpu.roll(pltpu.roll(value, wz - 1, 1), 7, 0)
-        z_next = jnp.where(z_l < wz - 1, pltpu.roll(value, lanes - 1, 1), jnp.where(b < az - 1, up, zero))
-        down = pltpu.roll(pltpu.roll(value, lanes - (wz - 1), 1), 1, 0)
-        z_prev = jnp.where(z_l > 0, pltpu.roll(value, 1, 1), jnp.where(b > 0, down, zero))
-        return x_next, x_prev, z_next, z_prev
-
     damp = VISCOSITY * TIME_STEP
 
+    many = 2 if ax % 2 == 0 else 1
+    spots = [(i, b) for i in range(many) for b in range(az)]
+    keys = [(w, i, b) for w in range(5) for i, b in spots]
+
     def stage(number, src, dst, keep, gain):
-        @pl.loop(0, tall // 2 - number)
-        def _(pair):
-            start = number + 2 * pair
-            total = [[None, None] for _ in range(5)]
-            slopes = []
-            for w in range(5):
-                column = [src[w * tall + start + k] for k in (-1, 0, 1, 2)]
-                per = []
-                for k in range(2):
-                    before, center, after = column[k : k + 3]
-                    x_next, x_prev, z_next, z_prev = shifts(center)
-                    around = ((x_next + x_prev) + (z_next + z_prev)) + (after + before)
-                    total[w][k] = (1.0 - 6.0 * damp) * center + damp * around
-                    per.append((x_next - x_prev, z_next - z_prev, after - before))
-                slopes.append(per)
+        turns = -(-(tall - 2 * number) // 8) * (ax // many)
+
+        def places(turn):
+            block, a = halves(turn, ax // many)
+            start = number + block * 8
+            root = (a * many + 1) * (az * high) + start
+            return start, {(w, i, b): root + w * per + (i * az + b) * high for w, i, b in keys}
+
+        def across(turn):
+            _, at = places(turn)
+            mid = {k: src[pl.ds(at[k], 8), :] for k in keys}
+            found = []
+            for w, i, b in keys:
+                k = (w, i, b)
+                ahead, behind = src[pl.ds(at[k] + az * high, 8), :], src[pl.ds(at[k] - az * high, 8), :]
+                x_next = pltpu.roll(jnp.where(x_l == 0, ahead, mid[k]), lanes - wz, 1)
+                x_prev = pltpu.roll(jnp.where(x_l == wx - 1, behind, mid[k]), wz, 1)
+                z_edge = pltpu.roll(mid[w, i, b + 1], wz - 1, 1) if b < az - 1 else zero
+                z_next = jnp.where(z_l < wz - 1, pltpu.roll(mid[k], lanes - 1, 1), z_edge)
+                z_edge = pltpu.roll(mid[w, i, b - 1], lanes - (wz - 1), 1) if b > 0 else zero
+                z_prev = jnp.where(z_l > 0, pltpu.roll(mid[k], 1, 1), z_edge)
+                found.append((x_next - x_prev, z_next - z_prev, (x_next + x_prev) + (z_next + z_prev)))
+            return found
+
+        def store(found):
+            for i, values in enumerate(found):
+                for d in range(3):
+                    side[3 * i + d] = values[d]
+
+        store(across(0))
+
+        @pl.loop(0, turns)
+        def _(turn):
+            start, at = places(turn)
+            near = {k: [side[3 * i + d] for d in range(3)] for i, k in enumerate(keys)}
+            coming = across(jnp.minimum(turn + 1, turns - 1))
+            total, slope = {}, {}
+            for k in keys:
+                after, before = src[pl.ds(at[k] + 1, 8), :], src[pl.ds(at[k] - 1, 8), :]
+                slope[k] = near[k][0], near[k][1], after - before
+                total[k] = (1.0 - 6.0 * damp) * src[pl.ds(at[k], 8), :] + damp * (near[k][2] + (after + before))
             for v in range(5):
                 for d in range(3):
                     for w in range(5):
                         factor = coef[(d * 5 + v) * 5 + w]
-                        for k in range(2):
-                            total[v][k] = total[v][k] + factor * slopes[w][k][d]
-            for k in range(2):
-                at = start + k
-                inside = jnp.where(at < HALO, has_low, jnp.where(at >= HALO + plan.chunk, has_high, 1.0))
-                for v in range(5):
-                    value = total[v][k]
-                    if keep:
-                        value = keep * cur[v * tall + at] + gain * value
-                    dst[v * tall + at] = value * inside
+                        for i, b in spots:
+                            total[v, i, b] = total[v, i, b] + factor * slope[w, i, b][d]
+            inside = mask[pl.ds(start, 8), :]
+            for k in keys:
+                value = total[k]
+                if keep:
+                    value = keep * cur[pl.ds(at[k], 8), :] + gain * value
+                dst[pl.ds(at[k], 8), :] = value * inside
+            store(coming)
 
     for step in range(STEPS):
         stage(3 * step + 1, cur, one, 0.0, 1.0)
         stage(3 * step + 2, one, two, 0.75, 0.25)
         stage(3 * step + 3, two, cur, 1.0 / 3.0, 2.0 / 3.0)
-        for i in range(plan.chunk):
-            at = HALO + i
-            planes = [
-                cur[at] + cur[4 * tall + at],
-                cur[tall + at],
-                cur[2 * tall + at],
-                cur[3 * tall + at],
-            ]
-            for ch in range(4):
-                samp_ref[pl.ds(i * 128 + ch * STEPS + step, 8, stride=16), :] = planes[ch]
+        for a in range(ax):
+            for b in range(az):
+                for r in range(0, plan.chunk, 8):
+                    own = [cur[base(v, a, b) + HALO + r : base(v, a, b) + HALO + r + 8, :] for v in range(5)]
+                    own[0] = own[0] + own[4]
+                    for ch in range(4):
+                        at = (r * plan.group + a * az + b) * 16 + ch * STEPS + step
+                        samp_ref[pl.ds(at, 8, stride=plan.group * 16), :] = own[ch]
     for v in range(5):
-        for i in range(plan.chunk):
-            back_ref[pl.ds(v * plan.chunk + i, 8, stride=plan.body), :] = cur[v * tall + HALO + i]
+        for a in range(ax):
+            for b in range(az):
+                at = base(v, a, b) + HALO
+                target = (a * az + b) * plan.body + v * plan.chunk
+                back_ref[target : target + plan.chunk, :] = cur[at : at + plan.chunk, :]
 
 
 def unpack_kernel(plan, back_ref, out_ref, turned):
@@ -412,20 +450,16 @@
         out_ref[v] = turned[v * plan.wr : (v + 1) * plan.wr, :].T
 
 
-def list_kernel(plan, ids_ref, list_ref, count_ref):
-    mine, _ = plan.own_chunk()
-
+def list_kernel(plan, entry_ref, list_ref, count_ref):
     def source(g, count):
         def block(n, count):
-            for k in range(8):
-                cell = ids_ref[g * 8 + k, n]
-                lane, r = halves(cell, plan.wr)
-                q, r_l = halves(r, plan.chunk)
-                list_ref[count] = (r_l * 8 + g) * 128 + lane
-                count = count + jnp.where(q == mine, 1, 0)
+            found = [entry_ref[g * 8 + k, n] for k in range(8)]
+            for entry in found:
+                list_ref[count] = entry
+                count = count + (entry >> 20)
             return count
 
-        return lax.fori_loop(0, ids_ref[g * 8, 127], block, count)
+        return lax.fori_loop(0, entry_ref[g * 8, 127], block, count)
 
     count = lax.fori_loop(0, 8, source, 0)
     count_ref[0] = count
@@ -433,14 +467,27 @@
         list_ref[count + k] = 0
 
 
-def dft_kernel(plan, hist_ref, table_ref, live_ref, out_ref):
+def entries(plan, ids):
+    cell = ids.astype(jnp.int32)
+    lane, r = halves(cell, plan.wr)
+    q, r_l = halves(r, plan.chunk)
+    g = lax.broadcasted_iota(jnp.int32, cell.shape, 0)
+    mine, _ = plan.own_chunk()
+    entry = (r_l * 8 + g) * 128 + lane + jnp.where(q == mine, 1 << 20, 0)
+    last = lax.broadcasted_iota(jnp.int32, cell.shape, 2) == 127
+    return jnp.where(last, cell, entry).reshape(plan.group * 8, 128)
+
+
+def dft_kernel(plan, hist_ref, table_ref, point_ref, live_ref, out_ref):
     tile = pl.program_id(0)
+    out_ref[0, 256:259, :] = point_ref[0]
+    out_ref[0, 259:264, :] = jnp.full((5, 128), live_ref[0, 0].astype(jnp.float32))
     live = live_ref[0, 0] * 8
     keep = lax.broadcasted_iota(jnp.int32, (64, 128), 1) + tile * 128 < live
     for ch in range(4):
-        signal = hist_ref[:, ch, :]
+        signal = hist_ref[ch]
         if ch == 0:
-            signal = signal + hist_ref[:, 4, :]
+            signal = signal + hist_ref[4]
         spec = lax.dot_general(
             table_ref[...],
             signal,
@@ -463,19 +510,21 @@
     return along, amplitude, sine, cosine, near
 
 
-def hist_kernel(plan, first, wide, watch_ref, point_ref, spec_ref, live_ref, out_ref, acc):
-    tiles = (live_ref[0, 0] * 8 + 127) // 128
+def hist_kernel(plan, first, wide, watch_ref, *refs):
+    spec_refs, out_ref, acc = refs[:-2], refs[-2], refs[-1]
     lane = lax.broadcasted_iota(jnp.int32, (wide, 64), 1)
+    half = (lax.axis_index("row") % len(spec_refs)) * (plan.obs // len(spec_refs))
+    tiles = [(jnp.max(ref[0, 259:260, :]).astype(jnp.int32) * 8 + 127) // 128 for ref in spec_refs]
 
     @pl.loop(0, out_ref.shape[0] // wide)
     def _(ob):
         start = pl.multiple_of(ob * wide, 8)
-        watch = [watch_ref[pl.ds(first + start, wide), d : d + 1] for d in range(3)]
+        row = pl.multiple_of(half + first + start, 8)
+        watch = [jnp.broadcast_to(watch_ref[pl.ds(row, wide), d : d + 1], (wide, 128)) for d in range(3)]
         acc[...] = jnp.zeros_like(acc)
 
-        @pl.loop(0, tiles)
-        def _(tile):
-            point = [point_ref[tile, d : d + 1, :] for d in range(3)]
+        def radiate_tile(spec_ref, tile):
+            point = [spec_ref[tile, 256 + d : 257 + d, :] for d in range(3)]
             along, amplitude, sine, cosine, near = geometry(plan, watch, point)
             twice = 2.0 * cosine
             cos_last, sin_last = amplitude, jnp.zeros_like(amplitude)
@@ -492,6 +541,9 @@
                 cos_now, cos_last = twice * cos_now - cos_last, cos_now
                 sin_now, sin_last = twice * sin_now - sin_last, sin_now
 
+        for spec_ref, count in zip(spec_refs, tiles, strict=True):
+            pl.loop(0, count)(functools.partial(radiate_tile, spec_ref))
+
         out = jnp.zeros((wide, 64), jnp.float32)
         for f in range(2 * FREQ):
             out = jnp.where(lane == f, jnp.sum(acc[f], axis=1, keepdims=True), out)
@@ -510,7 +562,7 @@
     @pl.loop(0, (count + 7) // 8)
     def _(group):
         for k in range(8):
-            entry = list_ref[group * 8 + k]
+            entry = list_ref[group * 8 + k] & ((1 << 20) - 1)
             row, at = halves(entry, 128)
             tile = samp_ref[pl.ds(pl.multiple_of(row * 16, 16), 16), :]
             at = jnp.where(group * 8 + k < count, at, -1)
@@ -578,12 +630,17 @@
                 out_im = out_im + (turn_im * part_re + turn_re * part_im)
             final[fv * 8 : (fv + 1) * 8, :] = out_re
             final[FREQ + fv * 8 : FREQ + (fv + 1) * 8, :] = out_im
-        across = final[...].T[:, : 2 * FREQ]
-        share = plan.obs // parts
-        for i in range(128 // share):
-            piece = across[i * share : (i + 1) * share, :]
-            row = t * 128 + i * share
-            out_ref[row : row + share, :] = (piece + hist_refs[row // share][...]) * scale
+        out_ref[t * 128 : (t + 1) * 128, :] = final[...].T * scale
+    share = hist_refs[0].shape[0]
+    ways = plan.obs // (share * parts)
+    half = (lax.axis_index("row") % ways) * (share * parts)
+    for i in range(parts):
+        row = pl.multiple_of(half + i * share, 8)
+        out_ref[pl.ds(row, share), : 2 * FREQ] = out_ref[pl.ds(row, share), : 2 * FREQ] + hist_refs[i][...] * scale
+
+
+def sum_kernel(pieces_ref, out_ref):
+    out_ref[...] = jnp.sum(pieces_ref[...], axis=0)[:, : out_ref.shape[1]]
 
 
 def fourier_numpy(samples):
@@ -596,7 +653,7 @@
     f32 = jnp.float32
     shape = jax.ShapeDtypeStruct
     group, wr, lanes = plan.group, plan.wr, plan.lanes
-    tall = plan.chunk + 2 * HALO
+    field_rows = 5 * (plan.ax + 2) * plan.az * plan.tall_pad
     parts = 4
     bind = functools.partial
 
@@ -607,28 +664,11 @@
         VMEM,
         [pltpu.VMEM((5 * wr, lanes), f32)],
         name="pack",
-    )(flow_field.reshape(5, lanes, wr), surface_cell, surface_blocks)
+    )(flow_field.reshape(5, lanes, wr), surface_cell.T, surface_blocks)
+    packed, surface_cell = lax.optimization_barrier((packed, surface_cell))
     got = lax.all_to_all(packed, GROUP, 0, 0, tiled=True)
 
     tile_count = plan.capacity // 128
-    cos_t, sin_t = fourier_numpy(plan.samples)
-    table = np.concatenate([cos_t, sin_t], axis=0).astype(np.float32)
-    table[:, plan.samples - STEPS :] = 0.0
-    spec = pl.pallas_call(
-        bind(dft_kernel, plan),
-        out_shape=shape((tile_count, 256, 128), f32),
-        grid=(tile_count,),
-        in_specs=[
-            pl.BlockSpec((128, 5, plan.samples), lambda i: (i, 0, 0)),
-            pl.BlockSpec((64, plan.samples), lambda i: (0, 0)),
-            SMEM,
-        ],
-        out_specs=pl.BlockSpec((1, 256, 128), lambda i: (i, 0, 0)),
-        name="dft",
-        compiler_params=pltpu.CompilerParams(vmem_limit_bytes=40 * 1024 * 1024),
-        cost_estimate=pl.CostEstimate(flops=10**9, bytes_accessed=10**6, transcendentals=0),
-    )(history, jnp.asarray(table), surface_blocks)
-
     cell = surface_cell.reshape(-1)
     index_x, index_z, index_r = (lax.axis_index(name) for name in AXES)
     points = jnp.stack(
@@ -639,6 +679,25 @@
         ]
     ).astype(f32) + 0.5
     points = jnp.transpose(points.reshape(3, tile_count, 128), (1, 0, 2))
+    cos_t, sin_t = fourier_numpy(plan.samples)
+    table = np.concatenate([cos_t, sin_t], axis=0).astype(np.float32)
+    table[:, plan.samples - STEPS :] = 0.0
+    spec = pl.pallas_call(
+        bind(dft_kernel, plan),
+        out_shape=shape((tile_count, 264, 128), f32),
+        grid=(tile_count,),
+        in_specs=[
+            pl.BlockSpec((5, 128, plan.samples), lambda i: (0, i, 0)),
+            pl.BlockSpec((64, plan.samples), lambda i: (0, 0)),
+            pl.BlockSpec((1, 3, 128), lambda i: (i, 0, 0)),
+            SMEM,
+        ],
+        out_specs=pl.BlockSpec((1, 264, 128), lambda i: (i, 0, 0)),
+        name="dft",
+        compiler_params=pltpu.CompilerParams(vmem_limit_bytes=40 * 1024 * 1024),
+        cost_estimate=pl.CostEstimate(flops=10**9, bytes_accessed=10**6, transcendentals=0),
+    )(jnp.transpose(history, (1, 0, 2)), jnp.asarray(table), points, surface_blocks)
+
     watch = jnp.stack(
         [
             observers[0] * plan.nx,
@@ -647,26 +706,30 @@
         ],
         axis=1,
     )
-    share = plan.obs // parts
-    wide = 16
+    sources = [spec]
+    if plan.rows % 2 == 0:
+        sources.append(lax.ppermute(spec, "row", [(i, i ^ 1) for i in range(plan.rows)]))
+    share = plan.obs // len(sources) // parts
+    wide = 32
     hists = []
     for i in range(parts):
         hists.append(
             call(
                 bind(hist_kernel, plan, i * share, wide),
                 shape((share, 64), f32),
-                [VMEM, VMEM, VMEM, SMEM],
+                [VMEM] * (1 + len(sources)),
                 VMEM,
                 [pltpu.VMEM((64, wide, 128), f32)],
                 flops=10**9,
                 name=f"hist{i}",
-            )(watch, points, spec, surface_blocks)
+            )(watch, *sources)
         )
 
     flat = got.reshape(group * plan.sent, lanes)
+    flat, hists[0], hists[1] = lax.optimization_barrier((flat, hists[0], hists[1]))
     first, second = call(
         bind(edge_kernel, plan),
-        (shape((5 * HALO, 8, lanes), f32),) * 2,
+        (shape((5 * group * HALO, lanes), f32),) * 2,
         [VMEM],
         (VMEM, VMEM),
         name="edges",
@@ -679,7 +742,7 @@
     first = lax.ppermute(first, AXES, swap_a)
     second = lax.ppermute(second, AXES, swap_b)
 
-    ids = got[:, plan.body :, :].astype(jnp.int32).reshape(group * 8, lanes)
+    ids = entries(plan, got[:, plan.body :, :])
     listed, count = call(
         bind(list_kernel, plan),
         (shape((group * plan.capacity + 8,), jnp.int32), shape((1,), jnp.int32)),
@@ -688,16 +751,19 @@
         name="list",
     )(ids)
 
+    flat, listed, count, hists = lax.optimization_barrier((flat, listed, count, hists))
     back, samp = call(
         bind(stencil_kernel, plan),
         (shape((group * plan.body, lanes), f32), shape((plan.chunk * 8 * 16, lanes), f32)),
         [VMEM, VMEM, VMEM, SMEM],
         (VMEM, VMEM),
         [
-            pltpu.VMEM((5 * tall, 8, lanes), f32),
-            pltpu.VMEM((5 * tall, 8, lanes), f32),
-            pltpu.VMEM((5 * tall, 8, lanes), f32),
+            pltpu.VMEM((field_rows, lanes), f32),
+            pltpu.VMEM((field_rows, lanes), f32),
+            pltpu.VMEM((field_rows, lanes), f32),
             pltpu.VMEM((75, 8, lanes), f32),
+            pltpu.VMEM((plan.tall_pad, lanes), f32),
+            pltpu.VMEM((30 * plan.az, 8, lanes), f32),
         ],
         flops=10**9,
         name="stencil",
@@ -711,7 +777,7 @@
     columns[:, 6] = 1.0 / np.arange(1, FREQ + 1)
     partial = call(
         bind(recent_kernel, plan, parts),
-        shape((plan.obs, 2 * FREQ), f32),
+        shape((plan.obs, 128), f32),
         [SMEM, SMEM, VMEM, VMEM, VMEM] + [VMEM] * parts,
         VMEM,
         [
@@ -727,10 +793,13 @@
         flops=10**9,
         name="recent",
     )(listed, count, samp, observers, jnp.asarray(columns), *hists)
+    partial, back = lax.optimization_barrier((partial, back))
     pieces = lax.all_to_all(
-        partial.reshape(plan.devices, plan.per_obs, 2 * FREQ), AXES, 0, 0, tiled=True
-    )
-    spectrum = jnp.sum(pieces, axis=0)
+        partial.reshape(plan.devices, plan.per_obs, 128), AXES, 0, 0, tiled=True
+    )
+    spectrum = call(
+        sum_kernel, shape((plan.per_obs, 2 * FREQ), f32), [VMEM], VMEM, name="sum"
+    )(pieces)
     field = call(
         bind(unpack_kernel, plan),
         shape((5, lanes, wr), f32),

time: 104 us -> 85.4 us (0.82)
  blocking collectives: 25.6 us -> 0 us
  starting transfers between devices: 13.6 us -> 27.6 us
  Pallas kernels: 48.7 us -> 44.5 us
  other arithmetic: 2.3 us -> 0.09 us
    all_to_all x1 -> x0, blocking collectives: 25.6 us -> none  [fast_device(): lax.all_to_all(partial.reshape(plan.devices, plan.per_obs, 2 * FREQ), AXE...]
    all_to_all x1, starting transfers between devices: 3.43 us -> 13.1 us  [fast_device(): lax.all_to_all(back.reshape(group, plan.body, lanes), GROUP, 0, 0, tiled=...]
    all_to_all x1, waiting for transfers between devices: 8.72 us -> 0.01 us  [fast_device(): lax.all_to_all(back.reshape(group, plan.body, lanes), GROUP, 0, 0, tiled=...]
    all_to_all x0 -> x1, waiting for transfers between devices: none -> 7.27 us  [fast_device(): lax.all_to_all(partial.reshape(plan.devices, plan.per_obs, 128), AXES, 0,...]
    all_to_all x0 -> x1, starting transfers between devices: none -> 6.38 us  [fast_device(): lax.all_to_all(partial.reshape(plan.devices, plan.per_obs, 128), AXES, 0,...]
    pallas_call x1, Pallas kernels: 20.1 us -> 16.2 us  [fast_device(): call(bind(stencil_kernel, plan), (shape((group * plan.body, lanes), f32),...]
    pallas_call x3 -> x4, Pallas kernels: 9.69 us -> 12.3 us  [the longest x1 9.73 us: fast_device(): call(bind(recent_kernel, plan, parts), shape((plan.obs, 128), f32), [SMEM...]
    pallas_call x1, Pallas kernels: 7.65 us -> 5.12 us  [fast_device(): call(bind(list_kernel, plan), (shape((group * plan.capacity + 8,), jnp.in...]
  transfers between devices with their start and end apart: 4 -> 6, of which waited for: 1 -> 3; matrix products, arithmetic and copies ran while one was open for 4% -> 0% of each run, Pallas kernels for 18% -> 31%
where the time goes in v2:
time: 85.4 us; the launch traced here: 85.2 us
  Pallas kernels  44.5 us (52%)
  starting transfers between devices  27.6 us (32%)
  waiting for transfers between devices  8.91 us (10%)
  local copies, waits for them, and re-layouts  2.58 us (3%)
  between operations  1.51 us (2%)
    pallas_call x1, Pallas kernels, fast_device(): call(bind(stencil_kernel, plan), (shape((group * plan.body, lanes), f32),...  16.2 us
    all_to_all x1, starting transfers between devices, fast_device(): lax.all_to_all(back.reshape(group, plan.body, lanes), GROUP, 0, 0, tiled=...  13.1 us
    pallas_call x1, Pallas kernels, fast_device(): call(bind(recent_kernel, plan, parts), shape((plan.obs, 128), f32), [SMEM...  9.73 us
    pallas_call x4, Pallas kernels, fast_device(): call(bind(hist_kernel, plan, i * share, wide), shape((share, 64), f32), [...  9 us
    all_to_all x1, starting transfers between devices, fast_device(): got = lax.all_to_all(packed, GROUP, 0, 0, tiled=True)  7.31 us
    all_to_all x1, waiting for transfers between devices, fast_device(): lax.all_to_all(partial.reshape(plan.devices, plan.per_obs, 128), AXES, 0,...  7.27 us
    all_to_all x1, starting transfers between devices, fast_device(): lax.all_to_all(partial.reshape(plan.devices, plan.per_obs, 128), AXES, 0,...  6.38 us
    pallas_call x1, Pallas kernels, fast_device(): call(bind(list_kernel, plan), (shape((group * plan.capacity + 8,), jnp.in...  5.12 us
  transfers between devices with their start and end apart: 6, of which 3 were waited for; matrix products, arithmetic and copies ran while one was open for 0% of the time, Pallas kernels for 31%

profile of v2, /device:TPU:0, one launch (start us, length us, event | category | flops | bytes accessed | tf_op | source)
XLA Modules:
  0.0 85.2 jit_solution(16442275636436076998)
XLA Ops:
  0.6 0.0 copy-start.1
  1.3 0.0 copy-done.1
  1.3 0.0 copy-start
  1.3 1.0 %copy-done = f32[5,4,32,128]{3,2,1,0:T(8,128)S(1)} copy-done((f32[5,4,32,128]{3,2,1,0:T(8,128)S(1)}, f32[5,4,32,128]{3,2,1,0:T(8,128)}, u32[]{:S(2)}) %copy-start) | copy-done | bytes 327704
  2.3 0.0 copy-start.3
  2.3 0.9 %pack.1 = f32[8,88,128]{2,1,0:T(8,128)} custom-call(f32[5,128,128]{2,1,0:T(8,128)S(1)} %bitcast.19, s32[8,48]{1,0:T(8,128)S(1)} %bitcast.20, s32[1,1]{1,0:T(1,128)S(6)} %copy.31.live_ref), custom_call_target="tpu_custom_call" | custom-call | flops 1000000 | bytes 100000 | tf_op jit(solution)/shard_map/pack/pallas_call | solution.py:660
  3.2 7.3 %all-to-all-start = ((f32[8,88,128]{2,1,0:T(8,128)}), f32[8,88,128]{2,1,0:T(8,128)S(1)}, u32[]{:S(2)}, u32[]{:S(2)}) async-start(f32[8,88,128]{2,1,0:T(8,128)} %pack.1), calls=%async_computation | async-start | bytes 720896 | tf_op jit(solution)/shard_map/all_to_all | solution.py:669
  10.5 0.1 copy.21
  10.6 0.0 copy-start.4
  10.6 0.1 reshape.280
  10.8 0.0 copy-done.3
  10.8 0.6 copy-done.4
  11.4 0.0 copy-start.2
  11.4 1.9 %dft.1.refs_0_ = f32[3,264,128]{2,1,0:T(8,128)S(1)} custom-call(f32[5,384,128]{2,1,0:T(8,128)S(1)} %bitcast.21, f32[64,128]{1,0:T(8,128)S(1)} %copy-done.4, f32[3,3,128]{2,1,0:T(4,128)S(1)} %fusion.1.point_ref, s32[1,1]{1,0:T(1,128)S(6)} %copy.31.live_ref), custom_call_target="tpu_custom_call" | custom-call | flops 1000000000 | bytes 1000000 | tf_op jit(solution)/shard_map/dft/pallas_call | solution.py:685
  13.3 0.1 collective-permute-start
  13.4 0.0 copy-done.2
  13.4 0.0 copy-start.6
  13.4 0.7 copy-done.6
  14.1 0.1 copy.26.watch_ref
  14.3 0.8 collective-permute-done.refs_1_
  15.1 2.2 %hist3.1.refs_3_ = f32[32,64]{1,0:T(8,128)S(1)} custom-call(f32[256,3]{1,0:T(8,128)S(1)} %copy.26.watch_ref, f32[3,264,128]{2,1,0:T(8,128)S(1)} %dft.1.refs_0_, f32[3,264,128]{2,1,0:T(8,128)S(1)} %collective-permute-done.refs_1_), custom_call_target="tpu_custom_call" | custom-call | flops 1000000000 | bytes 100000 | tf_op jit(solution)/shard_map/hist3/pallas_call | solution.py:717
  17.4 2.3 %hist2.1.refs_2_ = f32[32,64]{1,0:T(8,128)S(1)} custom-call(f32[256,3]{1,0:T(8,128)S(1)} %copy.26.watch_ref, f32[3,264,128]{2,1,0:T(8,128)S(1)} %dft.1.refs_0_, f32[3,264,128]{2,1,0:T(8,128)S(1)} %collective-permute-done.refs_1_), custom_call_target="tpu_custom_call" | custom-call | flops 1000000000 | bytes 100000 | tf_op jit(solution)/shard_map/hist2/pallas_call | solution.py:717
  19.6 2.3 %hist1.1.refs_1_ = f32[32,64]{1,0:T(8,128)S(1)} custom-call(f32[256,3]{1,0:T(8,128)S(1)} %copy.26.watch_ref, f32[3,264,128]{2,1,0:T(8,128)S(1)} %dft.1.refs_0_, f32[3,264,128]{2,1,0:T(8,128)S(1)} %collective-permute-done.refs_1_), custom_call_target="tpu_custom_call" | custom-call | flops 1000000000 | bytes 100000 | tf_op jit(solution)/shard_map/hist1/pallas_call | solution.py:717
  21.9 2.3 %hist0.1.refs_0_ = f32[32,64]{1,0:T(8,128)S(1)} custom-call(f32[256,3]{1,0:T(8,128)S(1)} %copy.26.watch_ref, f32[3,264,128]{2,1,0:T(8,128)S(1)} %dft.1.refs_0_, f32[3,264,128]{2,1,0:T(8,128)S(1)} %collective-permute-done.refs_1_), custom_call_target="tpu_custom_call" | custom-call | flops 1000000000 | bytes 100000 | tf_op jit(solution)/shard_map/hist0/pallas_call | solution.py:717
  24.1 0.0 all-to-all-done
  24.1 0.1 edges.1
  24.2 0.1 collective-permute-start.1
  24.3 0.7 collective-permute-start.2
  25.0 5.1 %list.1 = (s32[3080]{0:T(1024)S(1)}, s32[1]{0:T(128)}) custom-call(s32[64,128]{1,0:T(8,128)S(1)} %select_bitcast_fusion.entry_ref), custom_call_target="tpu_custom_call" | custom-call | flops 1000000 | bytes 100000 | tf_op jit(solution)/shard_map/list/pallas_call | solution.py:746
  30.1 0.8 collective-permute-done.1.first_ref
  30.9 0.0 collective-permute-done.2.second_ref
  30.9 16.2 %stencil.1 = (f32[640,128]{1,0:T(8,128)}, f32[2048,128]{1,0:T(8,128)S(1)}) custom-call(f32[704,128]{1,0:T(8,128)S(1)} %bitcast.18, f32[360,128]{1,0:T(8,128)S(1)} %collective-permute-done.1.first_ref, f32[360,128]{1,0:T(8,128)S(1)} %collective-permute-done.2.second_ref, f32[3,5,5]{2,1,0:T(8,128)S(1)} %copy.30.jac_ref), custom_call_target="tpu_custom_call" | custom-call | flops 1000000000 | bytes 100000 | tf_op jit(solution)/shard_map/stencil/pallas_call | solution.py:755
  47.1 0.0 copy-start.5
  47.1 13.1 %all-to-all-start.1 = ((f32[8,80,128]{2,1,0:T(8,128)}), f32[8,80,128]{2,1,0:T(8,128)S(1)}, u32[]{:S(2)}, u32[]{:S(2)}) async-start(f32[8,80,128]{2,1,0:T(8,128)} %bitcast.9), calls=%async_computation.1 | async-start | bytes 655360 | tf_op jit(solution)/shard_map/all_to_all | solution.py:771
  60.2 0.0 copy-done.5
  60.2 9.7 %recent.1 = f32[256,128]{1,0:T(8,128)} custom-call(s32[3080]{0:T(1024)S(1)} %get-tuple-element.29.list_ref, s32[1]{0:T(128)} %get-tuple-element.30.count_ref, f32[2048,128]{1,0:T(8,128)S(1)} %get-tuple-element.34.samp_ref, f32[3,256]{1,0:T(4,128)S(1)} %copy-done.2, f32[32,8]{1,0:T(8,128)S(1)} %copy-done.5, f32[32,64]{1,0:T(8,128)S(1)} %hist0.1.refs_0_, ...), custom_call_target="tpu_custom_call" | custom-call | flops 1000000000 | bytes 100000 | tf_op jit(solution)/shard_map/recent/pallas_call | solution.py:778
  70.0 0.0 all-to-all-done.1.back_ref
  70.0 6.4 %all-to-all-start.2 = ((f32[32,8,128]{2,1,0:T(8,128)}), f32[32,8,128]{2,1,0:T(8,128)S(1)}, u32[]{:S(2)}, u32[]{:S(2)}) async-start(f32[32,8,128]{2,1,0:T(8,128)} %bitcast.11), calls=%async_computation.2 | async-start | bytes 262144 | tf_op jit(solution)/shard_map/all_to_all | solution.py:797
  76.4 0.9 %unpack.1 = f32[5,128,128]{2,1,0:T(8,128)} custom-call(f32[8,80,128]{2,1,0:T(8,128)S(1)} %all-to-all-done.1.back_ref), custom_call_target="tpu_custom_call" | custom-call | flops 1000000 | bytes 100000 | tf_op jit(solution)/shard_map/unpack/pallas_call | solution.py:803
  77.3 7.3 %all-to-all-done.2.pieces_ref = f32[32,8,128]{2,1,0:T(8,128)S(1)} async-done(((f32[32,8,128]{2,1,0:T(8,128)}), f32[32,8,128]{2,1,0:T(8,128)S(1)}, u32[]{:S(2)}, u32[]{:S(2)}) %all-to-all-start.2) | async-done | bytes 131104 | tf_op jit(solution)/shard_map/all_to_all | solution.py:797
  84.6 0.6 sum.1
  (7 shorter events, 0.1 us)
Async XLA Ops:
  0.6 0.7 copy-start.1
  1.3 1.0 %copy-start = (f32[5,4,32,128]{3,2,1,0:T(8,128)S(1)}, f32[5,4,32,128]{3,2,1,0:T(8,128)}, u32[]{:S(2)}) copy-start(f32[5,4,32,128]{3,2,1,0:T(8,128)} %param.8) | copy-start | bytes 983044
  2.3 8.5 %copy-start.3 = (f32[384,5,128]{2,0,1:T(8,128)S(1)}, f32[384,5,128]{2,0,1:T(8,128)}, u32[]{:S(2)}) copy-start(f32[384,5,128]{2,0,1:T(8,128)} %param.10) | copy-start | bytes 2949124
  3.2 20.9 %all-to-all-start = ((f32[8,88,128]{2,1,0:T(8,128)}), f32[8,88,128]{2,1,0:T(8,128)S(1)}, u32[]{:S(2)}, u32[]{:S(2)}) async-start(f32[8,88,128]{2,1,0:T(8,128)} %pack.1), calls=%async_computation | async-start | bytes 720896 | tf_op jit(solution)/shard_map/all_to_all | solution.py:669
  10.6 0.8 copy-start.4
  11.4 2.0 %copy-start.2 = (f32[3,256]{1,0:T(4,128)S(1)}, f32[3,256]{1,0:T(4,128)}, u32[]{:S(2)}) copy-start(f32[3,256]{1,0:T(4,128)} %obs_ref.1) | copy-start | bytes 9220
  13.3 1.8 %collective-permute-start = (f32[3,264,128]{2,1,0:T(8,128)S(1)}, f32[3,264,128]{2,1,0:T(8,128)S(1)}, u32[]{:S(2)}, u32[]{:S(2)}) collective-permute-start(f32[3,264,128]{2,1,0:T(8,128)S(1)} %dft.1.refs_0_), channel_id=1, source_target_pairs={{0,1},{1,0},{2,3},{3,2},{4,5},{5,4},{6,7},{7,6},{8,9},{9,8},{10,11... | collective-permute-start | bytes 1216520 | tf_op jit(solution)/shard_map/ppermute | solution.py:711
  13.4 0.7 copy-start.6
  24.2 6.7 %collective-permute-start.1 = (f32[360,128]{1,0:T(8,128)S(1)}, f32[360,128]{1,0:T(8,128)S(1)}, u32[]{:S(2)}, u32[]{:S(2)}) collective-permute-start(f32[360,128]{1,0:T(8,128)S(1)} %get-tuple-element.32), channel_id=1, source_target_pairs={{0,8},{8,0},{16,24},{24,16},{28,20},{20,28},{12,4},{4,12},{5,13},{... | collective-permute-start | bytes 552968 | tf_op jit(solution)/shard_map/ppermute | solution.py:742
  24.3 6.7 %collective-permute-start.2 = (f32[360,128]{1,0:T(8,128)S(1)}, f32[360,128]{1,0:T(8,128)S(1)}, u32[]{:S(2)}, u32[]{:S(2)}) collective-permute-start(f32[360,128]{1,0:T(8,128)S(1)} %get-tuple-element.33), channel_id=1, source_target_pairs={{8,16},{16,8},{24,28},{28,24},{20,12},{12,20},{4,5},{5,4},{13,21},... | collective-permute-start | bytes 552968 | tf_op jit(solution)/shard_map/ppermute | solution.py:743
  47.1 13.1 %copy-start.5 = (f32[32,8]{1,0:T(8,128)S(1)}, f32[32,8]{1,0:T(8,128)}, u32[]{:S(2)}) copy-start(f32[32,8]{1,0:T(8,128)} %constant.111.clone.tab_ref) | copy-start | bytes 3076
  47.1 22.8 %all-to-all-start.1 = ((f32[8,80,128]{2,1,0:T(8,128)}), f32[8,80,128]{2,1,0:T(8,128)S(1)}, u32[]{:S(2)}, u32[]{:S(2)}) async-start(f32[8,80,128]{2,1,0:T(8,128)} %bitcast.9), calls=%async_computation.1 | async-start | bytes 655360 | tf_op jit(solution)/shard_map/all_to_all | solution.py:771
  70.0 14.6 %all-to-all-start.2 = ((f32[32,8,128]{2,1,0:T(8,128)}), f32[32,8,128]{2,1,0:T(8,128)S(1)}, u32[]{:S(2)}, u32[]{:S(2)}) async-start(f32[32,8,128]{2,1,0:T(8,128)} %bitcast.11), calls=%async_computation.2 | async-start | bytes 262144 | tf_op jit(solution)/shard_map/all_to_all | solution.py:797

commit v3 on v2

--- a/solution.py
+++ b/solution.py
@@ -223,6 +223,7 @@
             and self.lanes == 128
             and self.wr % 128 == 0
             and self.chunk % 8 == 0
+            and self.chunk >= 2 * 8
             and self.chunk >= HALO
             and self.capacity == self.blocks * 8
             and self.blocks < 127
@@ -304,7 +305,7 @@
             second_ref[at : at + HALO, :] = got_ref[pl.ds(row + second, HALO), :]
 
 
-def stencil_kernel(plan, got_ref, first_ref, second_ref, jac_ref, back_ref, samp_ref, cur, one, two, coef, mask, side):
+def stencil_kernel(plan, got_ref, first_ref, second_ref, jac_ref, back_ref, samp_ref, grid, coef, mask, side):
     q, c = plan.own_chunk()
     place = c * plan.group + q
     even = place % 2 == 0
@@ -325,16 +326,17 @@
             for w in range(5):
                 coef[(d * 5 + v) * 5 + w] = jnp.full((8, 128), jac_ref[d, v, w] * (0.5 * TIME_STEP), jnp.float32)
     zeros = jnp.zeros((az * high, 128), jnp.float32)
-    for ref in (cur, one, two):
+    for buffer in range(3):
         for v in range(5):
             for a in (-1, ax):
-                ref[base(v, a, 0) : base(v, a, 0) + az * high, :] = zeros
+                at = buffer * 5 * per + base(v, a, 0)
+                grid[at : at + az * high, :] = zeros
     for v in range(5):
         for a in range(ax):
             for b in range(az):
                 at = base(v, a, b) + HALO
                 source = (a * az + b) * plan.sent + v * plan.chunk
-                cur[at : at + plan.chunk, :] = got_ref[source : source + plan.chunk, :]
+                grid[at : at + plan.chunk, :] = got_ref[source : source + plan.chunk, :]
 
     def put(low_ref, high_ref):
         for v in range(5):
@@ -342,9 +344,9 @@
                 for b in range(az):
                     at = base(v, a, b)
                     source = (v * plan.group + a * az + b) * HALO
-                    cur[at : at + HALO, :] = low_ref[source : source + HALO, :]
+                    grid[at : at + HALO, :] = low_ref[source : source + HALO, :]
                     at = at + HALO + plan.chunk
-                    cur[at : at + HALO, :] = high_ref[source : source + HALO, :]
+                    grid[at : at + HALO, :] = high_ref[source : source + HALO, :]
 
     @pl.when(even)
     def _():
@@ -362,71 +364,86 @@
     many = 2 if ax % 2 == 0 else 1
     spots = [(i, b) for i in range(many) for b in range(az)]
     keys = [(w, i, b) for w in range(5) for i, b in spots]
-
-    def stage(number, src, dst, keep, gain):
-        turns = -(-(tall - 2 * number) // 8) * (ax // many)
-
-        def places(turn):
-            block, a = halves(turn, ax // many)
-            start = number + block * 8
-            root = (a * many + 1) * (az * high) + start
-            return start, {(w, i, b): root + w * per + (i * az + b) * high for w, i, b in keys}
-
-        def across(turn):
-            _, at = places(turn)
-            mid = {k: src[pl.ds(at[k], 8), :] for k in keys}
-            found = []
-            for w, i, b in keys:
-                k = (w, i, b)
-                ahead, behind = src[pl.ds(at[k] + az * high, 8), :], src[pl.ds(at[k] - az * high, 8), :]
-                x_next = pltpu.roll(jnp.where(x_l == 0, ahead, mid[k]), lanes - wz, 1)
-                x_prev = pltpu.roll(jnp.where(x_l == wx - 1, behind, mid[k]), wz, 1)
-                z_edge = pltpu.roll(mid[w, i, b + 1], wz - 1, 1) if b < az - 1 else zero
-                z_next = jnp.where(z_l < wz - 1, pltpu.roll(mid[k], lanes - 1, 1), z_edge)
-                z_edge = pltpu.roll(mid[w, i, b - 1], lanes - (wz - 1), 1) if b > 0 else zero
-                z_prev = jnp.where(z_l > 0, pltpu.roll(mid[k], 1, 1), z_edge)
-                found.append((x_next - x_prev, z_next - z_prev, (x_next + x_prev) + (z_next + z_prev)))
-            return found
-
-        def store(found):
-            for i, values in enumerate(found):
-                for d in range(3):
-                    side[3 * i + d] = values[d]
-
-        store(across(0))
-
-        @pl.loop(0, turns)
-        def _(turn):
-            start, at = places(turn)
-            near = {k: [side[3 * i + d] for d in range(3)] for i, k in enumerate(keys)}
-            coming = across(jnp.minimum(turn + 1, turns - 1))
-            total, slope = {}, {}
-            for k in keys:
-                after, before = src[pl.ds(at[k] + 1, 8), :], src[pl.ds(at[k] - 1, 8), :]
-                slope[k] = near[k][0], near[k][1], after - before
-                total[k] = (1.0 - 6.0 * damp) * src[pl.ds(at[k], 8), :] + damp * (near[k][2] + (after + before))
-            for v in range(5):
-                for d in range(3):
-                    for w in range(5):
-                        factor = coef[(d * 5 + v) * 5 + w]
-                        for i, b in spots:
-                            total[v, i, b] = total[v, i, b] + factor * slope[w, i, b][d]
-            inside = mask[pl.ds(start, 8), :]
-            for k in keys:
-                value = total[k]
-                if keep:
-                    value = keep * cur[pl.ds(at[k], 8), :] + gain * value
-                dst[pl.ds(at[k], 8), :] = value * inside
-            store(coming)
+    whole = 5 * per
+    far = {(w, i, b): w * per + (i * az + b) * high for w, i, b in keys}
+    side_step = az * high
+
+    def turns_of(number):
+        return ((tall - 2 * number + 7) >> 3) * (ax // many)
+
+    def places(number, turn):
+        block, a = halves(turn, ax // many)
+        start = number + block * 8
+        return start, (a * many + 1) * (az * high) + start
+
+    def across(number, turn, offset):
+        _, root = places(number, turn)
+        root = root + offset
+        mid = {k: grid[pl.ds(root + far[k], 8), :] for k in keys}
+        found = []
+        for w, i, b in keys:
+            k = (w, i, b)
+            ahead = grid[pl.ds(root + (far[k] + side_step), 8), :]
+            behind = grid[pl.ds(root + (far[k] - side_step), 8), :]
+            x_next = pltpu.roll(jnp.where(x_l == 0, ahead, mid[k]), lanes - wz, 1)
+            x_prev = pltpu.roll(jnp.where(x_l == wx - 1, behind, mid[k]), wz, 1)
+            z_edge = pltpu.roll(mid[w, i, b + 1], wz - 1, 1) if b < az - 1 else zero
+            z_next = jnp.where(z_l < wz - 1, pltpu.roll(mid[k], lanes - 1, 1), z_edge)
+            z_edge = pltpu.roll(mid[w, i, b - 1], lanes - (wz - 1), 1) if b > 0 else zero
+            z_prev = jnp.where(z_l > 0, pltpu.roll(mid[k], 1, 1), z_edge)
+            found.append((x_next - x_prev, z_next - z_prev, (x_next + x_prev) + (z_next + z_prev)))
+        return found
+
+    def store(found):
+        for i, values in enumerate(found):
+            for d in range(3):
+                side[3 * i + d] = values[d]
+
+    store(across(1, 0, 0))
 
     for step in range(STEPS):
-        stage(3 * step + 1, cur, one, 0.0, 1.0)
-        stage(3 * step + 2, one, two, 0.75, 0.25)
-        stage(3 * step + 3, two, cur, 1.0 / 3.0, 2.0 / 3.0)
+
+        @pl.loop(0, 3)
+        def _(part):
+            number = 3 * step + 1 + part
+            source = part * whole
+            target = jnp.where(part == 2, 0, source + whole)
+            keep = jnp.where(part == 0, 0.0, jnp.where(part == 1, 0.75, 1.0 / 3.0))
+            gain = jnp.where(part == 0, 1.0, jnp.where(part == 1, 0.25, 2.0 / 3.0))
+            turns = turns_of(number)
+
+            @pl.loop(0, turns)
+            def _(turn):
+                start, root = places(number, turn)
+                here, there = root + source, root + target
+                near = {k: [side[3 * i + d] for d in range(3)] for i, k in enumerate(keys)}
+                last = turn + 1 >= turns
+                coming = across(
+                    jnp.where(last, number + 1, number),
+                    jnp.where(last, 0, turn + 1),
+                    jnp.where(last, target, source),
+                )
+                total, slope = {}, {}
+                for k in keys:
+                    after, before = grid[pl.ds(here + (far[k] + 1), 8), :], grid[pl.ds(here + (far[k] - 1), 8), :]
+                    slope[k] = near[k][0], near[k][1], after - before
+                    total[k] = (1.0 - 6.0 * damp) * grid[pl.ds(here + far[k], 8), :] + damp * (near[k][2] + (after + before))
+                for v in range(5):
+                    for d in range(3):
+                        for w in range(5):
+                            factor = coef[(d * 5 + v) * 5 + w]
+                            for i, b in spots:
+                                total[v, i, b] = total[v, i, b] + factor * slope[w, i, b][d]
+                inside = mask[pl.ds(start, 8), :]
+                for k in keys:
+                    value = keep * grid[pl.ds(root + far[k], 8), :] + gain * total[k]
+                    grid[pl.ds(there + far[k], 8), :] = value * inside
+                store(coming)
+
         for a in range(ax):
             for b in range(az):
                 for r in range(0, plan.chunk, 8):
-                    own = [cur[base(v, a, b) + HALO + r : base(v, a, b) + HALO + r + 8, :] for v in range(5)]
+                    own = [grid[base(v, a, b) + HALO + r : base(v, a, b) + HALO + r + 8, :] for v in range(5)]
                     own[0] = own[0] + own[4]
                     for ch in range(4):
                         at = (r * plan.group + a * az + b) * 16 + ch * STEPS + step
@@ -436,7 +453,7 @@
             for b in range(az):
                 at = base(v, a, b) + HALO
                 target = (a * az + b) * plan.body + v * plan.chunk
-                back_ref[target : target + plan.chunk, :] = cur[at : at + plan.chunk, :]
+                back_ref[target : target + plan.chunk, :] = grid[at : at + plan.chunk, :]
 
 
 def unpack_kernel(plan, back_ref, out_ref, turned):
@@ -453,13 +470,13 @@
 def list_kernel(plan, entry_ref, list_ref, count_ref):
     def source(g, count):
         def block(n, count):
-            found = [entry_ref[g * 8 + k, n] for k in range(8)]
+            found = [entry_ref[g * 1024 + n + k * 128] for k in range(8)]
             for entry in found:
                 list_ref[count] = entry
                 count = count + (entry >> 20)
             return count
 
-        return lax.fori_loop(0, entry_ref[g * 8, 127], block, count)
+        return lax.fori_loop(0, entry_ref[g * 1024 + 127], block, count)
 
     count = lax.fori_loop(0, 8, source, 0)
     count_ref[0] = count
@@ -475,7 +492,7 @@
     mine, _ = plan.own_chunk()
     entry = (r_l * 8 + g) * 128 + lane + jnp.where(q == mine, 1 << 20, 0)
     last = lax.broadcasted_iota(jnp.int32, cell.shape, 2) == 127
-    return jnp.where(last, cell, entry).reshape(plan.group * 8, 128)
+    return jnp.where(last, cell, entry).reshape(-1)
 
 
 def dft_kernel(plan, hist_ref, table_ref, point_ref, live_ref, out_ref):
@@ -552,30 +569,43 @@
 
 def recent_kernel(plan, parts, list_ref, count_ref, samp_ref, obs_ref, tab_ref, *refs):
     hist_refs, out_ref = refs[:parts], refs[parts]
-    value, place, cos_s, sin_s, mono, dip, acc, final = refs[parts + 1 :]
+    value, place, cos_s, sin_s, mono, dip, full, acc, final = refs[parts + 1 :]
     q, c = plan.own_chunk()
     count = count_ref[0]
     tiles = plan.obs // 128
     lane = lax.broadcasted_iota(jnp.int32, (16, 128), 1)
     acc[...] = jnp.zeros_like(acc)
 
-    @pl.loop(0, (count + 7) // 8)
-    def _(group):
+    groups = (count + 7) // 8
+
+    def sample(group):
+        picked, spots = [], []
         for k in range(8):
             entry = list_ref[group * 8 + k] & ((1 << 20) - 1)
             row, at = halves(entry, 128)
             tile = samp_ref[pl.ds(pl.multiple_of(row * 16, 16), 16), :]
-            at = jnp.where(group * 8 + k < count, at, -1)
-            picked = jnp.sum(jnp.where(lane == at, tile, 0.0), axis=1, keepdims=True)
-            value[k * 16 : (k + 1) * 16, :] = jnp.broadcast_to(picked, (16, 128))
             r_l, g = halves(row, 8)
             a, b = halves(g, plan.az)
-            _, at = halves(entry, 128)
             x_l, z_l = halves(at, plan.wz)
-            spot = (a * plan.wx + x_l, b * plan.wz + z_l, c * plan.wr + q * plan.chunk + r_l)
+            spots.append((a * plan.wx + x_l, b * plan.wz + z_l, c * plan.wr + q * plan.chunk + r_l))
+            at = jnp.where(group * 8 + k < count, at, -1)
+            picked.append(jnp.sum(jnp.where(lane == at, tile, 0.0), axis=1, keepdims=True))
+        return picked, spots
+
+    def keep(found):
+        for k in range(8):
+            value[k * 16 : (k + 1) * 16, :] = jnp.broadcast_to(found[0][k], (16, 128))
             for d in range(3):
-                place[d * 8 + k : d * 8 + k + 1, :] = jnp.full((1, 128), spot[d].astype(jnp.float32) + 0.5)
+                spot = found[1][k][d].astype(jnp.float32) + 0.5
+                place[d * 8 + k : d * 8 + k + 1, :] = jnp.full((1, 128), spot)
+
+    keep(sample(0))
+
+    @pl.loop(0, groups)
+    def _(group):
         point = [place[d * 8 : (d + 1) * 8, :] for d in range(3)]
+        drawn = [value[pl.ds(i, 8, stride=16), :] for i in range(4 * STEPS)]
+        coming = sample(jnp.minimum(group + 1, groups - 1))
         for t in range(tiles):
             seen = obs_ref[:, t * 128 : (t + 1) * 128]
             watch = [
@@ -585,33 +615,38 @@
             ]
             along, amplitude, sine, cosine, near = geometry(plan, watch, point)
             for s in range(STEPS):
-                drawn = [value[pl.ds(ch * STEPS + s, 8, stride=16), :] for ch in range(4)]
-                push = along[0] * drawn[1] + along[1] * drawn[2] + along[2] * drawn[3]
-                mono[s * 8 : (s + 1) * 8, :] = drawn[0] + push
-                dip[s * 8 : (s + 1) * 8, :] = near * push
+                push = along[0] * drawn[STEPS + s] + along[1] * drawn[2 * STEPS + s] + along[2] * drawn[3 * STEPS + s]
+                at = (t * STEPS + s) * 8
+                mono[at : at + 8, :] = drawn[s] + push
+                dip[at : at + 8, :] = near * push
             twice = 2.0 * cosine
             cos_last, sin_last = amplitude, jnp.zeros_like(amplitude)
             cos_now, sin_now = amplitude * cosine, amplitude * sine
             for f in range(FREQ):
-                cos_s[f * 8 : (f + 1) * 8, :] = cos_now
-                sin_s[f * 8 : (f + 1) * 8, :] = sin_now
+                at = (t * FREQ + f) * 8
+                cos_s[at : at + 8, :] = cos_now
+                sin_s[at : at + 8, :] = sin_now
                 cos_now, cos_last = twice * cos_now - cos_last, cos_now
                 sin_now, sin_last = twice * sin_now - sin_last, sin_now
+        for t in range(tiles):
             for fv in range(FREQ // 8):
                 base = (t * (FREQ // 8) + fv) * 12
                 sums = [acc[base + i] for i in range(12)]
                 for k in range(8):
-                    wave_c = cos_s[pl.ds(fv * 64 + k, 8, stride=8), :]
-                    wave_s = sin_s[pl.ds(fv * 64 + k, 8, stride=8), :]
+                    at = (t * FREQ + fv * 8) * 8 + k
+                    wave_c = cos_s[pl.ds(at, 8, stride=8), :]
+                    wave_s = sin_s[pl.ds(at, 8, stride=8), :]
                     for s in range(STEPS):
-                        m = mono[s * 8 + k : s * 8 + k + 1, :]
-                        p = dip[s * 8 + k : s * 8 + k + 1, :]
+                        at = (t * STEPS + s) * 8 + k
+                        m = mono[at : at + 1, :]
+                        p = dip[at : at + 1, :]
                         sums[4 * s] = sums[4 * s] + wave_c * m
                         sums[4 * s + 1] = sums[4 * s + 1] + wave_s * m
                         sums[4 * s + 2] = sums[4 * s + 2] + wave_c * p
                         sums[4 * s + 3] = sums[4 * s + 3] + wave_s * p
                 for i in range(12):
                     acc[base + i] = sums[i]
+        keep(coming)
 
     scale = 1.0 / math.sqrt(plan.devices * SURF_DEV)
     final[...] = jnp.zeros_like(final)
@@ -630,17 +665,26 @@
                 out_im = out_im + (turn_im * part_re + turn_re * part_im)
             final[fv * 8 : (fv + 1) * 8, :] = out_re
             final[FREQ + fv * 8 : FREQ + (fv + 1) * 8, :] = out_im
-        out_ref[t * 128 : (t + 1) * 128, :] = final[...].T * scale
+        full[t * 128 : (t + 1) * 128, :] = final[...].T * scale
     share = hist_refs[0].shape[0]
     ways = plan.obs // (share * parts)
     half = (lax.axis_index("row") % ways) * (share * parts)
     for i in range(parts):
         row = pl.multiple_of(half + i * share, 8)
-        out_ref[pl.ds(row, share), : 2 * FREQ] = out_ref[pl.ds(row, share), : 2 * FREQ] + hist_refs[i][...] * scale
+        full[pl.ds(row, share), : 2 * FREQ] = full[pl.ds(row, share), : 2 * FREQ] + hist_refs[i][...] * scale
+    for k in range(4):
+        low = full[pl.ds(k, plan.devices, stride=8), :]
+        high = full[pl.ds(k + 4, plan.devices, stride=8), :]
+        both = low + pltpu.roll(high, 64, 1)
+        out_ref[pl.ds(k, plan.devices, stride=4), :] = both
 
 
 def sum_kernel(pieces_ref, out_ref):
-    out_ref[...] = jnp.sum(pieces_ref[...], axis=0)[:, : out_ref.shape[1]]
+    total = pieces_ref[0]
+    for i in range(1, pieces_ref.shape[0]):
+        total = total + pieces_ref[i]
+    out_ref[0:4, :] = total[:, :64]
+    out_ref[4:8, :] = total[:, 64:]
 
 
 def fourier_numpy(samples):
@@ -758,9 +802,7 @@
         [VMEM, VMEM, VMEM, SMEM],
         (VMEM, VMEM),
         [
-            pltpu.VMEM((field_rows, lanes), f32),
-            pltpu.VMEM((field_rows, lanes), f32),
-            pltpu.VMEM((field_rows, lanes), f32),
+            pltpu.VMEM((3 * field_rows, lanes), f32),
             pltpu.VMEM((75, 8, lanes), f32),
             pltpu.VMEM((plan.tall_pad, lanes), f32),
             pltpu.VMEM((30 * plan.az, 8, lanes), f32),
@@ -777,16 +819,17 @@
     columns[:, 6] = 1.0 / np.arange(1, FREQ + 1)
     partial = call(
         bind(recent_kernel, plan, parts),
-        shape((plan.obs, 128), f32),
+        shape((plan.obs // 2, 128), f32),
         [SMEM, SMEM, VMEM, VMEM, VMEM] + [VMEM] * parts,
         VMEM,
         [
             pltpu.VMEM((128, 128), f32),
             pltpu.VMEM((24, 128), f32),
-            pltpu.VMEM((FREQ * 8, 128), f32),
-            pltpu.VMEM((FREQ * 8, 128), f32),
-            pltpu.VMEM((STEPS * 8, 128), f32),
-            pltpu.VMEM((STEPS * 8, 128), f32),
+            pltpu.VMEM((plan.obs // 128 * FREQ * 8, 128), f32),
+            pltpu.VMEM((plan.obs // 128 * FREQ * 8, 128), f32),
+            pltpu.VMEM((plan.obs // 128 * STEPS * 8, 128), f32),
+            pltpu.VMEM((plan.obs // 128 * STEPS * 8, 128), f32),
+            pltpu.VMEM((plan.obs, 128), f32),
             pltpu.VMEM((plan.obs // 128 * (FREQ // 8) * 12, 8, 128), f32),
             pltpu.VMEM((128, 128), f32),
         ],
@@ -795,7 +838,7 @@
     )(listed, count, samp, observers, jnp.asarray(columns), *hists)
     partial, back = lax.optimization_barrier((partial, back))
     pieces = lax.all_to_all(
-        partial.reshape(plan.devices, plan.per_obs, 128), AXES, 0, 0, tiled=True
+        partial.reshape(plan.devices, 4, 128), AXES, 0, 0, tiled=True
     )
     spectrum = call(
         sum_kernel, shape((plan.per_obs, 2 * FREQ), f32), [VMEM], VMEM, name="sum"

time: 85.4 us -> 81.6 us (0.956); the launches traced: 85.2 us -> 80.2 us
  starting transfers between devices: 27.6 us -> 24.7 us
  Pallas kernels: 44.5 us -> 41.6 us
    all_to_all x1, starting transfers between devices: 13.1 us -> 5.86 us  [fast_device(): lax.all_to_all(back.reshape(group, plan.body, lanes), GROUP, 0, 0, tiled=...]
    ppermute x1, starting transfers between devices: 0.07 us -> 4.47 us  [fast_device(): first = lax.ppermute(first, AXES, swap_a)]
    all_to_all x1, waiting for transfers between devices: 0.01 us -> 2.39 us  [fast_device(): lax.all_to_all(back.reshape(group, plan.body, lanes), GROUP, 0, 0, tiled=...]
    pallas_call x1, Pallas kernels: 9.73 us -> 7.67 us  [fast_device(): call(bind(recent_kernel, plan, parts), shape((plan.obs // 2, 128), f32),...]
  transfers between devices with their start and end apart: 6 -> 6, of which waited for: 3 -> 3; matrix products, arithmetic and copies ran while one was open for 0% -> 0% of each run, Pallas kernels for 31% -> 30%
where the time goes in v3:
time: 81.6 us; the launch traced here: 80.2 us
  Pallas kernels  41.6 us (51%)
  starting transfers between devices  24.7 us (30%)
  waiting for transfers between devices  9.68 us (12%)
  local copies, waits for them, and re-layouts  2.58 us (3%)
  between operations  1.51 us (2%)
    pallas_call x1, Pallas kernels, fast_device(): call(bind(stencil_kernel, plan), (shape((group * plan.body, lanes), f32),...  16 us
    pallas_call x4, Pallas kernels, fast_device(): call(bind(hist_kernel, plan, i * share, wide), shape((share, 64), f32), [...  9 us
    pallas_call x1, Pallas kernels, fast_device(): call(bind(recent_kernel, plan, parts), shape((plan.obs // 2, 128), f32),...  7.67 us
    all_to_all x1, starting transfers between devices, fast_device(): got = lax.all_to_all(packed, GROUP, 0, 0, tiled=True)  7.31 us
    all_to_all x1, waiting for transfers between devices, fast_device(): lax.all_to_all(partial.reshape(plan.devices, 4, 128), AXES, 0, 0, tiled=T...  6.48 us
    all_to_all x1, starting transfers between devices, fast_device(): lax.all_to_all(partial.reshape(plan.devices, 4, 128), AXES, 0, 0, tiled=T...  6.37 us
    all_to_all x1, starting transfers between devices, fast_device(): lax.all_to_all(back.reshape(group, plan.body, lanes), GROUP, 0, 0, tiled=...  5.86 us
    ppermute x1, starting transfers between devices, fast_device(): first = lax.ppermute(first, AXES, swap_a)  4.47 us
  transfers between devices with their start and end apart: 6, of which 3 were waited for; matrix products, arithmetic and copies ran while one was open for 0% of the time, Pallas kernels for 30%

profile of v3, /device:TPU:0, one launch (start us, length us, event | category | flops | bytes accessed | tf_op | source)
XLA Modules:
  0.0 80.2 jit_solution(9286040837355209532)
XLA Ops:
  0.6 0.0 copy-start.1
  1.3 0.0 copy-done.1
  1.3 0.0 copy-start
  1.3 1.0 %copy-done = f32[5,4,32,128]{3,2,1,0:T(8,128)S(1)} copy-done((f32[5,4,32,128]{3,2,1,0:T(8,128)S(1)}, f32[5,4,32,128]{3,2,1,0:T(8,128)}, u32[]{:S(2)}) %copy-start) | copy-done | bytes 327704
  2.3 0.0 copy-start.3
  2.3 0.9 %pack.1 = f32[8,88,128]{2,1,0:T(8,128)} custom-call(f32[5,128,128]{2,1,0:T(8,128)S(1)} %bitcast.19, s32[8,48]{1,0:T(8,128)S(1)} %bitcast.20, s32[1,1]{1,0:T(1,128)S(6)} %copy.31.live_ref), custom_call_target="tpu_custom_call" | custom-call | flops 1000000 | bytes 100000 | tf_op jit(solution)/shard_map/pack/pallas_call | solution.py:704
  3.2 7.3 %all-to-all-start = ((f32[8,88,128]{2,1,0:T(8,128)}), f32[8,88,128]{2,1,0:T(8,128)S(1)}, u32[]{:S(2)}, u32[]{:S(2)}) async-start(f32[8,88,128]{2,1,0:T(8,128)} %pack.1), calls=%async_computation | async-start | bytes 720896 | tf_op jit(solution)/shard_map/all_to_all | solution.py:713
  10.5 0.1 copy.21
  10.6 0.0 copy-start.4
  10.6 0.1 reshape.280
  10.8 0.0 copy-done.3
  10.8 0.6 copy-done.4
  11.4 0.0 copy-start.2
  11.4 1.9 %dft.1.refs_0_ = f32[3,264,128]{2,1,0:T(8,128)S(1)} custom-call(f32[5,384,128]{2,1,0:T(8,128)S(1)} %bitcast.21, f32[64,128]{1,0:T(8,128)S(1)} %copy-done.4, f32[3,3,128]{2,1,0:T(4,128)S(1)} %fusion.1.point_ref, s32[1,1]{1,0:T(1,128)S(6)} %copy.31.live_ref), custom_call_target="tpu_custom_call" | custom-call | flops 1000000000 | bytes 1000000 | tf_op jit(solution)/shard_map/dft/pallas_call | solution.py:729
  13.3 0.1 collective-permute-start
  13.4 0.0 copy-done.2
  13.4 0.0 copy-start.6
  13.4 0.7 copy-done.6
  14.1 0.1 copy.26.watch_ref
  14.3 0.8 %collective-permute-done.refs_1_ = f32[3,264,128]{2,1,0:T(8,128)S(1)} collective-permute-done((f32[3,264,128]{2,1,0:T(8,128)S(1)}, f32[3,264,128]{2,1,0:T(8,128)S(1)}, u32[]{:S(2)}, u32[]{:S(2)}) %collective-permute-start) | collective-permute-done | bytes 405536 | tf_op jit(solution)/shard_map/ppermute | solution.py:755
  15.1 2.2 %hist3.1.refs_3_ = f32[32,64]{1,0:T(8,128)S(1)} custom-call(f32[256,3]{1,0:T(8,128)S(1)} %copy.26.watch_ref, f32[3,264,128]{2,1,0:T(8,128)S(1)} %dft.1.refs_0_, f32[3,264,128]{2,1,0:T(8,128)S(1)} %collective-permute-done.refs_1_), custom_call_target="tpu_custom_call" | custom-call | flops 1000000000 | bytes 100000 | tf_op jit(solution)/shard_map/hist3/pallas_call | solution.py:761
  17.4 2.3 %hist2.1.refs_2_ = f32[32,64]{1,0:T(8,128)S(1)} custom-call(f32[256,3]{1,0:T(8,128)S(1)} %copy.26.watch_ref, f32[3,264,128]{2,1,0:T(8,128)S(1)} %dft.1.refs_0_, f32[3,264,128]{2,1,0:T(8,128)S(1)} %collective-permute-done.refs_1_), custom_call_target="tpu_custom_call" | custom-call | flops 1000000000 | bytes 100000 | tf_op jit(solution)/shard_map/hist2/pallas_call | solution.py:761
  19.6 2.3 %hist1.1.refs_1_ = f32[32,64]{1,0:T(8,128)S(1)} custom-call(f32[256,3]{1,0:T(8,128)S(1)} %copy.26.watch_ref, f32[3,264,128]{2,1,0:T(8,128)S(1)} %dft.1.refs_0_, f32[3,264,128]{2,1,0:T(8,128)S(1)} %collective-permute-done.refs_1_), custom_call_target="tpu_custom_call" | custom-call | flops 1000000000 | bytes 100000 | tf_op jit(solution)/shard_map/hist1/pallas_call | solution.py:761
  21.9 2.3 %hist0.1.refs_0_ = f32[32,64]{1,0:T(8,128)S(1)} custom-call(f32[256,3]{1,0:T(8,128)S(1)} %copy.26.watch_ref, f32[3,264,128]{2,1,0:T(8,128)S(1)} %dft.1.refs_0_, f32[3,264,128]{2,1,0:T(8,128)S(1)} %collective-permute-done.refs_1_), custom_call_target="tpu_custom_call" | custom-call | flops 1000000000 | bytes 100000 | tf_op jit(solution)/shard_map/hist0/pallas_call | solution.py:761
  24.1 0.0 all-to-all-done
  24.1 0.1 edges.1
  24.2 4.5 %collective-permute-start.1 = (f32[360,128]{1,0:T(8,128)S(1)}, f32[360,128]{1,0:T(8,128)S(1)}, u32[]{:S(2)}, u32[]{:S(2)}) collective-permute-start(f32[360,128]{1,0:T(8,128)S(1)} %get-tuple-element.32), channel_id=1, source_target_pairs={{0,8},{8,0},{16,24},{24,16},{28,20},{20,28},{12,4},{4,12},{5,13},{... | collective-permute-start | bytes 552968 | tf_op jit(solution)/shard_map/ppermute | solution.py:786
  28.7 0.7 collective-permute-start.2
  29.4 4.3 %list.1 = (s32[3080]{0:T(1024)S(1)}, s32[1]{0:T(128)}) custom-call(s32[8192]{0:T(1024)S(1)} %select_bitcast_fusion.entry_ref), custom_call_target="tpu_custom_call" | custom-call | flops 1000000 | bytes 100000 | tf_op jit(solution)/shard_map/list/pallas_call | solution.py:790
  33.7 0.0 collective-permute-done.1.first_ref
  33.7 0.0 collective-permute-done.2.second_ref
  33.7 16.0 %stencil.1 = (f32[640,128]{1,0:T(8,128)}, f32[2048,128]{1,0:T(8,128)S(1)}) custom-call(f32[704,128]{1,0:T(8,128)S(1)} %bitcast.18, f32[360,128]{1,0:T(8,128)S(1)} %collective-permute-done.1.first_ref, f32[360,128]{1,0:T(8,128)S(1)} %collective-permute-done.2.second_ref, f32[3,5,5]{2,1,0:T(8,128)S(1)} %copy.30.jac_ref), custom_call_target="tpu_custom_call" | custom-call | flops 1000000000 | bytes 100000 | tf_op jit(solution)/shard_map/stencil/pallas_call | solution.py:799
  49.7 0.0 copy-start.5
  49.8 5.9 %all-to-all-start.1 = ((f32[8,80,128]{2,1,0:T(8,128)}), f32[8,80,128]{2,1,0:T(8,128)S(1)}, u32[]{:S(2)}, u32[]{:S(2)}) async-start(f32[8,80,128]{2,1,0:T(8,128)} %bitcast.9), calls=%async_computation.1 | async-start | bytes 655360 | tf_op jit(solution)/shard_map/all_to_all | solution.py:813
  55.6 0.0 copy-done.5
  55.6 7.7 %recent.1 = f32[128,128]{1,0:T(8,128)} custom-call(s32[3080]{0:T(1024)S(1)} %get-tuple-element.29.list_ref, s32[1]{0:T(128)} %get-tuple-element.30.count_ref, f32[2048,128]{1,0:T(8,128)S(1)} %get-tuple-element.34.samp_ref, f32[3,256]{1,0:T(4,128)S(1)} %copy-done.2, f32[32,8]{1,0:T(8,128)S(1)} %copy-done.5, f32[32,64]{1,0:T(8,128)S(1)} %hist0.1.refs_0_, ...), custom_call_target="tpu_custom_call" | custom-call | flops 1000000000 | bytes 100000 | tf_op jit(solution)/shard_map/recent/pallas_call | solution.py:820
  63.3 2.4 %all-to-all-done.1.back_ref = f32[8,80,128]{2,1,0:T(8,128)S(1)} async-done(((f32[8,80,128]{2,1,0:T(8,128)}), f32[8,80,128]{2,1,0:T(8,128)S(1)}, u32[]{:S(2)}, u32[]{:S(2)}) %all-to-all-start.1) | async-done | bytes 327712 | tf_op jit(solution)/shard_map/all_to_all | solution.py:813
  65.7 6.4 %all-to-all-start.2 = ((f32[32,4,128]{2,1,0:T(4,128)}), f32[32,4,128]{2,1,0:T(4,128)S(1)}, u32[]{:S(2)}, u32[]{:S(2)}) async-start(f32[32,4,128]{2,1,0:T(4,128)} %bitcast.11), calls=%async_computation.2 | async-start | bytes 131072 | tf_op jit(solution)/shard_map/all_to_all | solution.py:840
  72.1 0.9 %unpack.1 = f32[5,128,128]{2,1,0:T(8,128)} custom-call(f32[8,80,128]{2,1,0:T(8,128)S(1)} %all-to-all-done.1.back_ref), custom_call_target="tpu_custom_call" | custom-call | flops 1000000 | bytes 100000 | tf_op jit(solution)/shard_map/unpack/pallas_call | solution.py:846
  73.0 6.5 %all-to-all-done.2.pieces_ref = f32[32,4,128]{2,1,0:T(4,128)S(1)} async-done(((f32[32,4,128]{2,1,0:T(4,128)}), f32[32,4,128]{2,1,0:T(4,128)S(1)}, u32[]{:S(2)}, u32[]{:S(2)}) %all-to-all-start.2) | async-done | bytes 65568 | tf_op jit(solution)/shard_map/all_to_all | solution.py:840
  79.5 0.7 sum.1
  (7 shorter events, 0.1 us)
Async XLA Ops:
  0.6 0.7 copy-start.1
  1.3 1.0 %copy-start = (f32[5,4,32,128]{3,2,1,0:T(8,128)S(1)}, f32[5,4,32,128]{3,2,1,0:T(8,128)}, u32[]{:S(2)}) copy-start(f32[5,4,32,128]{3,2,1,0:T(8,128)} %param.8) | copy-start | bytes 983044
  2.3 8.5 %copy-start.3 = (f32[384,5,128]{2,0,1:T(8,128)S(1)}, f32[384,5,128]{2,0,1:T(8,128)}, u32[]{:S(2)}) copy-start(f32[384,5,128]{2,0,1:T(8,128)} %param.10) | copy-start | bytes 2949124
  3.2 20.9 %all-to-all-start = ((f32[8,88,128]{2,1,0:T(8,128)}), f32[8,88,128]{2,1,0:T(8,128)S(1)}, u32[]{:S(2)}, u32[]{:S(2)}) async-start(f32[8,88,128]{2,1,0:T(8,128)} %pack.1), calls=%async_computation | async-start | bytes 720896 | tf_op jit(solution)/shard_map/all_to_all | solution.py:713
  10.6 0.8 copy-start.4
  11.4 2.0 %copy-start.2 = (f32[3,256]{1,0:T(4,128)S(1)}, f32[3,256]{1,0:T(4,128)}, u32[]{:S(2)}) copy-start(f32[3,256]{1,0:T(4,128)} %obs_ref.1) | copy-start | bytes 9220
  13.3 1.8 %collective-permute-start = (f32[3,264,128]{2,1,0:T(8,128)S(1)}, f32[3,264,128]{2,1,0:T(8,128)S(1)}, u32[]{:S(2)}, u32[]{:S(2)}) collective-permute-start(f32[3,264,128]{2,1,0:T(8,128)S(1)} %dft.1.refs_0_), channel_id=1, source_target_pairs={{0,1},{1,0},{2,3},{3,2},{4,5},{5,4},{6,7},{7,6},{8,9},{9,8},{10,11... | collective-permute-start | bytes 1216520 | tf_op jit(solution)/shard_map/ppermute | solution.py:755
  13.4 0.7 copy-start.6
  24.2 9.5 %collective-permute-start.1 = (f32[360,128]{1,0:T(8,128)S(1)}, f32[360,128]{1,0:T(8,128)S(1)}, u32[]{:S(2)}, u32[]{:S(2)}) collective-permute-start(f32[360,128]{1,0:T(8,128)S(1)} %get-tuple-element.32), channel_id=1, source_target_pairs={{0,8},{8,0},{16,24},{24,16},{28,20},{20,28},{12,4},{4,12},{5,13},{... | collective-permute-start | bytes 552968 | tf_op jit(solution)/shard_map/ppermute | solution.py:786
  28.7 5.0 %collective-permute-start.2 = (f32[360,128]{1,0:T(8,128)S(1)}, f32[360,128]{1,0:T(8,128)S(1)}, u32[]{:S(2)}, u32[]{:S(2)}) collective-permute-start(f32[360,128]{1,0:T(8,128)S(1)} %get-tuple-element.33), channel_id=1, source_target_pairs={{8,16},{16,8},{24,28},{28,24},{20,12},{12,20},{4,5},{5,4},{13,21},... | collective-permute-start | bytes 552968 | tf_op jit(solution)/shard_map/ppermute | solution.py:787
  49.7 5.9 %copy-start.5 = (f32[32,8]{1,0:T(8,128)S(1)}, f32[32,8]{1,0:T(8,128)}, u32[]{:S(2)}) copy-start(f32[32,8]{1,0:T(8,128)} %constant.111.clone.tab_ref) | copy-start | bytes 3076
  49.8 15.9 %all-to-all-start.1 = ((f32[8,80,128]{2,1,0:T(8,128)}), f32[8,80,128]{2,1,0:T(8,128)S(1)}, u32[]{:S(2)}, u32[]{:S(2)}) async-start(f32[8,80,128]{2,1,0:T(8,128)} %bitcast.9), calls=%async_computation.1 | async-start | bytes 655360 | tf_op jit(solution)/shard_map/all_to_all | solution.py:813
  65.7 13.8 %all-to-all-start.2 = ((f32[32,4,128]{2,1,0:T(4,128)}), f32[32,4,128]{2,1,0:T(4,128)S(1)}, u32[]{:S(2)}, u32[]{:S(2)}) async-start(f32[32,4,128]{2,1,0:T(4,128)} %bitcast.11), calls=%async_computation.2 | async-start | bytes 131072 | tf_op jit(solution)/shard_map/all_to_all | solution.py:840

commit v4 on v3

--- a/solution.py
+++ b/solution.py
@@ -8,6 +8,7 @@
 from jax.experimental import pallas as pl
 from jax.experimental.pallas import tpu as pltpu
 from jax.sharding import PartitionSpec as P
+
 
 SURF_DEV = 128
 FREQ = 32
@@ -116,7 +117,7 @@
     mask_inner = inside_mask(1)
     current = flow_field
     sampled = []
-    for step_index in range(STEPS):
+    for _ in range(STEPS):
         extended = padded_2(current, (("gx", 1), ("gz", 2), ("row", 3)), 3)
         section_one = (
             extended[:, 1:-1, 1:-1, 1:-1] + TIME_STEP * stencil_rate(extended, flux_jacobian)
@@ -226,7 +227,7 @@
             and self.chunk >= 2 * 8
             and self.chunk >= HALO
             and self.capacity == self.blocks * 8
-            and self.blocks < 127
+            and 2 * self.blocks < 127
             and self.capacity % 128 == 0
             and self.samples == 128
             and self.obs % 128 == 0
@@ -262,17 +263,23 @@
         return jnp.where(c % 2 == 1, self.group - 1 - q, q), c
 
 
-def call(kernel, out_shape, in_specs, out_specs, scratch=(), flops=10**6, name=None):
-    return pl.pallas_call(
+def call(kernel, out_shape, in_specs, out_specs, scratch=(), flops=10**6):
+    kernel_call = pl.pallas_call(
         kernel,
         out_shape=out_shape,
         in_specs=in_specs,
         out_specs=out_specs,
         scratch_shapes=list(scratch),
-        name=name,
         compiler_params=pltpu.CompilerParams(vmem_limit_bytes=40 * 1024 * 1024),
         cost_estimate=pl.CostEstimate(flops=flops, bytes_accessed=10**5, transcendentals=0),
     )
+    return kernel_call
+
+
+def move(axes, *pairs):
+    if pairs:
+        return lambda value: lax.ppermute(value, axes, pairs[0])
+    return lambda value: lax.all_to_all(value, axes, 0, 0, tiled=True)
 
 
 def pack_kernel(plan, flow_ref, cell_ref, live_ref, out_ref, turned):
@@ -280,7 +287,8 @@
     for v in range(5):
         turned[v * plan.wr : (v + 1) * plan.wr, :] = flow_ref[v].T
     cells = cell_ref[...].astype(jnp.float32)
-    ids = jnp.concatenate([cells, jnp.zeros((8, 128 - plan.blocks), jnp.float32)], axis=1)
+    ids = jnp.concatenate([cells[:4], cells[4:], jnp.zeros((4, 128 - 2 * plan.blocks), jnp.float32)], axis=1)
+    ids = jnp.concatenate([ids, jnp.zeros((4, 128), jnp.float32)], axis=0)
     lane = lax.broadcasted_iota(jnp.int32, (8, 128), 1)
     ids = jnp.where(lane == 127, live_ref[0, 0].astype(jnp.float32), ids)
     for j in range(plan.group):
@@ -291,7 +299,7 @@
         out_ref[j, plan.body : plan.body + 8, :] = ids
 
 
-def edge_kernel(plan, got_ref, first_ref, second_ref):
+def edge_kernel(plan, got_ref, first_ref, second_ref, own_ref):
     q, c = plan.own_chunk()
     even = (c * plan.group + q) % 2 == 0
     high, low = plan.chunk - HALO, 0
@@ -303,9 +311,11 @@
             row = g * plan.sent + v * plan.chunk
             first_ref[at : at + HALO, :] = got_ref[pl.ds(row + first, HALO), :]
             second_ref[at : at + HALO, :] = got_ref[pl.ds(row + second, HALO), :]
-
-
-def stencil_kernel(plan, got_ref, first_ref, second_ref, jac_ref, back_ref, samp_ref, grid, coef, mask, side):
+            at = (v * plan.group + g) * plan.chunk
+            own_ref[at : at + plan.chunk, :] = got_ref[row : row + plan.chunk, :]
+
+
+def stencil_kernel(plan, own_ref, first_ref, second_ref, jac_ref, back_ref, samp_ref, cur, one, two, coef, mask, side):
     q, c = plan.own_chunk()
     place = c * plan.group + q
     even = place % 2 == 0
@@ -326,17 +336,16 @@
             for w in range(5):
                 coef[(d * 5 + v) * 5 + w] = jnp.full((8, 128), jac_ref[d, v, w] * (0.5 * TIME_STEP), jnp.float32)
     zeros = jnp.zeros((az * high, 128), jnp.float32)
-    for buffer in range(3):
+    for ref in (cur, one, two):
         for v in range(5):
             for a in (-1, ax):
-                at = buffer * 5 * per + base(v, a, 0)
-                grid[at : at + az * high, :] = zeros
+                ref[base(v, a, 0) : base(v, a, 0) + az * high, :] = zeros
     for v in range(5):
         for a in range(ax):
             for b in range(az):
                 at = base(v, a, b) + HALO
-                source = (a * az + b) * plan.sent + v * plan.chunk
-                grid[at : at + plan.chunk, :] = got_ref[source : source + plan.chunk, :]
+                source = (v * plan.group + a * az + b) * plan.chunk
+                cur[at : at + plan.chunk, :] = own_ref[source : source + plan.chunk, :]
 
     def put(low_ref, high_ref):
         for v in range(5):
@@ -344,9 +353,9 @@
                 for b in range(az):
                     at = base(v, a, b)
                     source = (v * plan.group + a * az + b) * HALO
-                    grid[at : at + HALO, :] = low_ref[source : source + HALO, :]
+                    cur[at : at + HALO, :] = low_ref[source : source + HALO, :]
                     at = at + HALO + plan.chunk
-                    grid[at : at + HALO, :] = high_ref[source : source + HALO, :]
+                    cur[at : at + HALO, :] = high_ref[source : source + HALO, :]
 
     @pl.when(even)
     def _():
@@ -364,7 +373,6 @@
     many = 2 if ax % 2 == 0 else 1
     spots = [(i, b) for i in range(many) for b in range(az)]
     keys = [(w, i, b) for w in range(5) for i, b in spots]
-    whole = 5 * per
     far = {(w, i, b): w * per + (i * az + b) * high for w, i, b in keys}
     side_step = az * high
 
@@ -376,15 +384,17 @@
         start = number + block * 8
         return start, (a * many + 1) * (az * high) + start
 
-    def across(number, turn, offset):
+    grids = (cur, one, two)
+
+    def across(number, turn):
+        src = grids[(number - 1) % 3]
         _, root = places(number, turn)
-        root = root + offset
-        mid = {k: grid[pl.ds(root + far[k], 8), :] for k in keys}
+        mid = {k: src[pl.ds(root + far[k], 8), :] for k in keys}
         found = []
         for w, i, b in keys:
             k = (w, i, b)
-            ahead = grid[pl.ds(root + (far[k] + side_step), 8), :]
-            behind = grid[pl.ds(root + (far[k] - side_step), 8), :]
+            ahead = src[pl.ds(root + (far[k] + side_step), 8), :]
+            behind = src[pl.ds(root + (far[k] - side_step), 8), :]
             x_next = pltpu.roll(jnp.where(x_l == 0, ahead, mid[k]), lanes - wz, 1)
             x_prev = pltpu.roll(jnp.where(x_l == wx - 1, behind, mid[k]), wz, 1)
             z_edge = pltpu.roll(mid[w, i, b + 1], wz - 1, 1) if b < az - 1 else zero
@@ -399,51 +409,55 @@
             for d in range(3):
                 side[3 * i + d] = values[d]
 
-    store(across(1, 0, 0))
-
-    for step in range(STEPS):
-
-        @pl.loop(0, 3)
-        def _(part):
-            number = 3 * step + 1 + part
-            source = part * whole
-            target = jnp.where(part == 2, 0, source + whole)
-            keep = jnp.where(part == 0, 0.0, jnp.where(part == 1, 0.75, 1.0 / 3.0))
-            gain = jnp.where(part == 0, 1.0, jnp.where(part == 1, 0.25, 2.0 / 3.0))
-            turns = turns_of(number)
-
-            @pl.loop(0, turns)
-            def _(turn):
-                start, root = places(number, turn)
-                here, there = root + source, root + target
-                near = {k: [side[3 * i + d] for d in range(3)] for i, k in enumerate(keys)}
-                last = turn + 1 >= turns
-                coming = across(
-                    jnp.where(last, number + 1, number),
-                    jnp.where(last, 0, turn + 1),
-                    jnp.where(last, target, source),
-                )
-                total, slope = {}, {}
-                for k in keys:
-                    after, before = grid[pl.ds(here + (far[k] + 1), 8), :], grid[pl.ds(here + (far[k] - 1), 8), :]
-                    slope[k] = near[k][0], near[k][1], after - before
-                    total[k] = (1.0 - 6.0 * damp) * grid[pl.ds(here + far[k], 8), :] + damp * (near[k][2] + (after + before))
-                for v in range(5):
-                    for d in range(3):
-                        for w in range(5):
-                            factor = coef[(d * 5 + v) * 5 + w]
-                            for i, b in spots:
-                                total[v, i, b] = total[v, i, b] + factor * slope[w, i, b][d]
-                inside = mask[pl.ds(start, 8), :]
-                for k in keys:
-                    value = keep * grid[pl.ds(root + far[k], 8), :] + gain * total[k]
-                    grid[pl.ds(there + far[k], 8), :] = value * inside
-                store(coming)
-
+    order = {k: i for i, k in enumerate(keys)}
+
+    def advance(number, turn, next_number, next_turn):
+        part = (number - 1) % 3
+        src, dst = grids[part], grids[(part + 1) % 3]
+        keep, gain = ((0.0, 1.0), (0.75, 0.25), (1.0 / 3.0, 2.0 / 3.0))[part]
+        start, root = places(number, turn)
+        coming = across(next_number, next_turn)
+        inside = mask[pl.ds(start, 8), :]
+        for i, b in spots:
+            total = []
+            slopes = []
+            for w in range(5):
+                k = (w, i, b)
+                after, before = src[pl.ds(root + (far[k] + 1), 8), :], src[pl.ds(root + (far[k] - 1), 8), :]
+                around = side[3 * order[k] + 2] + (after + before)
+                total.append((1.0 - 6.0 * damp) * src[pl.ds(root + far[k], 8), :] + damp * around)
+                slopes.append((after - before, side[3 * order[k] + 1], side[3 * order[k]]))
+            for d in range(3):
+                for w in range(5):
+                    for v in range(5):
+                        total[v] = total[v] + coef[((2 - d) * 5 + v) * 5 + w] * slopes[w][d]
+            for v in range(5):
+                k = (v, i, b)
+                value = total[v] * (gain * inside)
+                if part:
+                    value = (keep * inside) * cur[pl.ds(root + far[k], 8), :] + value
+                dst[pl.ds(root + far[k], 8), :] = value
+        store(coming)
+
+    store(across(1, 0))
+    for number in range(1, 3 * STEPS + 1):
+        turns = turns_of(number)
+
+        @pl.loop(0, turns - 1)
+        def _(turn):
+            advance(number, turn, number, turn + 1)
+
+        if number < 3 * STEPS:
+            advance(number, turns - 1, number + 1, 0)
+        else:
+            advance(number, turns - 1, number, turns - 1)
+        if number % 3:
+            continue
+        step = number // 3 - 1
         for a in range(ax):
             for b in range(az):
                 for r in range(0, plan.chunk, 8):
-                    own = [grid[base(v, a, b) + HALO + r : base(v, a, b) + HALO + r + 8, :] for v in range(5)]
+                    own = [cur[base(v, a, b) + HALO + r : base(v, a, b) + HALO + r + 8, :] for v in range(5)]
                     own[0] = own[0] + own[4]
                     for ch in range(4):
                         at = (r * plan.group + a * az + b) * 16 + ch * STEPS + step
@@ -453,7 +467,7 @@
             for b in range(az):
                 at = base(v, a, b) + HALO
                 target = (a * az + b) * plan.body + v * plan.chunk
-                back_ref[target : target + plan.chunk, :] = grid[at : at + plan.chunk, :]
+                back_ref[target : target + plan.chunk, :] = cur[at : at + plan.chunk, :]
 
 
 def unpack_kernel(plan, back_ref, out_ref, turned):
@@ -470,13 +484,13 @@
 def list_kernel(plan, entry_ref, list_ref, count_ref):
     def source(g, count):
         def block(n, count):
-            found = [entry_ref[g * 1024 + n + k * 128] for k in range(8)]
+            found = [entry_ref[g * 512 + n + (k % 4 * 128 + k // 4 * plan.blocks)] for k in range(8)]
             for entry in found:
                 list_ref[count] = entry
                 count = count + (entry >> 20)
             return count
 
-        return lax.fori_loop(0, entry_ref[g * 1024 + 127], block, count)
+        return lax.fori_loop(0, entry_ref[g * 512 + 127], block, count)
 
     count = lax.fori_loop(0, 8, source, 0)
     count_ref[0] = count
@@ -495,8 +509,16 @@
     return jnp.where(last, cell, entry).reshape(-1)
 
 
-def dft_kernel(plan, hist_ref, table_ref, point_ref, live_ref, out_ref):
+def dft_kernel(plan, hist_ref, table_ref, point_ref, obs_ref, live_ref, out_ref, watch_ref):
     tile = pl.program_id(0)
+
+    @pl.when(tile == 0)
+    def _():
+        seen = obs_ref[...]
+        rows = [seen[0:1] * float(plan.nx), seen[1:2] * float(plan.nz), (1.25 + 0.75 * seen[2:3]) * float(plan.nr)]
+        rows.append(jnp.zeros((5, plan.obs), jnp.float32))
+        watch_ref[...] = jnp.concatenate(rows, axis=0).T
+
     out_ref[0, 256:259, :] = point_ref[0]
     out_ref[0, 259:264, :] = jnp.full((5, 128), live_ref[0, 0].astype(jnp.float32))
     live = live_ref[0, 0] * 8
@@ -527,16 +549,16 @@
     return along, amplitude, sine, cosine, near
 
 
-def hist_kernel(plan, first, wide, watch_ref, *refs):
+def hist_kernel(plan, ways, first, wide, watch_ref, *refs):
     spec_refs, out_ref, acc = refs[:-2], refs[-2], refs[-1]
     lane = lax.broadcasted_iota(jnp.int32, (wide, 64), 1)
-    half = (lax.axis_index("row") % len(spec_refs)) * (plan.obs // len(spec_refs))
+    mine = (lax.axis_index("row") % ways) * (plan.obs // ways)
     tiles = [(jnp.max(ref[0, 259:260, :]).astype(jnp.int32) * 8 + 127) // 128 for ref in spec_refs]
 
     @pl.loop(0, out_ref.shape[0] // wide)
     def _(ob):
         start = pl.multiple_of(ob * wide, 8)
-        row = pl.multiple_of(half + first + start, 8)
+        row = pl.multiple_of(mine + first + start, 8)
         watch = [jnp.broadcast_to(watch_ref[pl.ds(row, wide), d : d + 1], (wide, 128)) for d in range(3)]
         acc[...] = jnp.zeros_like(acc)
 
@@ -567,7 +589,7 @@
         out_ref[pl.ds(start, wide), :] = out
 
 
-def recent_kernel(plan, parts, list_ref, count_ref, samp_ref, obs_ref, tab_ref, *refs):
+def recent_kernel(plan, parts, near_parts, list_ref, count_ref, samp_ref, obs_ref, tab_ref, *refs):
     hist_refs, out_ref = refs[:parts], refs[parts]
     value, place, cos_s, sin_s, mono, dip, full, acc, final = refs[parts + 1 :]
     q, c = plan.own_chunk()
@@ -666,12 +688,12 @@
             final[fv * 8 : (fv + 1) * 8, :] = out_re
             final[FREQ + fv * 8 : FREQ + (fv + 1) * 8, :] = out_im
         full[t * 128 : (t + 1) * 128, :] = final[...].T * scale
-    share = hist_refs[0].shape[0]
-    ways = plan.obs // (share * parts)
-    half = (lax.axis_index("row") % ways) * (share * parts)
-    for i in range(parts):
-        row = pl.multiple_of(half + i * share, 8)
-        full[pl.ds(row, share), : 2 * FREQ] = full[pl.ds(row, share), : 2 * FREQ] + hist_refs[i][...] * scale
+    share = hist_refs[0].shape[0] * near_parts
+    mine = (lax.axis_index("row") % (plan.obs // share)) * share
+    for i, hist_ref in enumerate(hist_refs):
+        rows = hist_ref.shape[0]
+        at = pl.multiple_of(mine + (i * rows if i < near_parts else 0), 8)
+        full[pl.ds(at, rows), : 2 * FREQ] = full[pl.ds(at, rows), : 2 * FREQ] + hist_ref[...] * scale
     for k in range(4):
         low = full[pl.ds(k, plan.devices, stride=8), :]
         high = full[pl.ds(k + 4, plan.devices, stride=8), :]
@@ -698,7 +720,6 @@
     shape = jax.ShapeDtypeStruct
     group, wr, lanes = plan.group, plan.wr, plan.lanes
     field_rows = 5 * (plan.ax + 2) * plan.az * plan.tall_pad
-    parts = 4
     bind = functools.partial
 
     packed = call(
@@ -707,10 +728,9 @@
         [VMEM, VMEM, SMEM],
         VMEM,
         [pltpu.VMEM((5 * wr, lanes), f32)],
-        name="pack",
     )(flow_field.reshape(5, lanes, wr), surface_cell.T, surface_blocks)
     packed, surface_cell = lax.optimization_barrier((packed, surface_cell))
-    got = lax.all_to_all(packed, GROUP, 0, 0, tiled=True)
+    got = move(GROUP)(packed)
 
     tile_count = plan.capacity // 128
     cell = surface_cell.reshape(-1)
@@ -726,91 +746,96 @@
     cos_t, sin_t = fourier_numpy(plan.samples)
     table = np.concatenate([cos_t, sin_t], axis=0).astype(np.float32)
     table[:, plan.samples - STEPS :] = 0.0
-    spec = pl.pallas_call(
+    spec, watch = pl.pallas_call(
         bind(dft_kernel, plan),
-        out_shape=shape((tile_count, 264, 128), f32),
+        out_shape=(shape((tile_count, 264, 128), f32), shape((plan.obs, 8), f32)),
         grid=(tile_count,),
         in_specs=[
             pl.BlockSpec((5, 128, plan.samples), lambda i: (0, i, 0)),
             pl.BlockSpec((64, plan.samples), lambda i: (0, 0)),
             pl.BlockSpec((1, 3, 128), lambda i: (i, 0, 0)),
+            pl.BlockSpec((3, plan.obs), lambda i: (0, 0)),
             SMEM,
         ],
-        out_specs=pl.BlockSpec((1, 264, 128), lambda i: (i, 0, 0)),
+        out_specs=(
+            pl.BlockSpec((1, 264, 128), lambda i: (i, 0, 0)),
+            pl.BlockSpec((plan.obs, 8), lambda i: (0, 0)),
+        ),
         name="dft",
         compiler_params=pltpu.CompilerParams(vmem_limit_bytes=40 * 1024 * 1024),
         cost_estimate=pl.CostEstimate(flops=10**9, bytes_accessed=10**6, transcendentals=0),
-    )(jnp.transpose(history, (1, 0, 2)), jnp.asarray(table), points, surface_blocks)
-
-    watch = jnp.stack(
-        [
-            observers[0] * plan.nx,
-            observers[1] * plan.nz,
-            (1.25 + 0.75 * observers[2]) * plan.nr,
-        ],
-        axis=1,
-    )
-    sources = [spec]
-    if plan.rows % 2 == 0:
-        sources.append(lax.ppermute(spec, "row", [(i, i ^ 1) for i in range(plan.rows)]))
-    share = plan.obs // len(sources) // parts
-    wide = 32
-    hists = []
-    for i in range(parts):
-        hists.append(
+    )(jnp.transpose(history, (1, 0, 2)), jnp.asarray(table), points, observers, surface_blocks)
+
+    def radiated(ways, sources, pieces=1):
+        share = plan.obs // ways // pieces
+        return [
             call(
-                bind(hist_kernel, plan, i * share, wide),
+                bind(hist_kernel, plan, ways, i * share, 32),
                 shape((share, 64), f32),
                 [VMEM] * (1 + len(sources)),
                 VMEM,
-                [pltpu.VMEM((64, wide, 128), f32)],
+                [pltpu.VMEM((64, 32, 128), f32)],
                 flops=10**9,
-                name=f"hist{i}",
             )(watch, *sources)
-        )
-
+            for i in range(pieces)
+        ]
+
+    near_swap = [(i, i ^ 1) for i in range(plan.rows)]
+    if plan.rows % 4 == 0:
+        across = move("row", [(i, i ^ 2) for i in range(plan.rows)])(spec)
+        hists = radiated(4, [spec, move("row", near_swap)(spec)], 2)
+    elif plan.rows % 2 == 0:
+        hists = radiated(2, [spec, move("row", near_swap)(spec)], 2)
+    else:
+        hists = radiated(1, [spec], 2)
     flat = got.reshape(group * plan.sent, lanes)
-    flat, hists[0], hists[1] = lax.optimization_barrier((flat, hists[0], hists[1]))
-    first, second = call(
+    flat, hists[0] = lax.optimization_barrier((flat, hists[0]))
+    first, second, own = call(
         bind(edge_kernel, plan),
-        (shape((5 * group * HALO, lanes), f32),) * 2,
+        (shape((5 * group * HALO, lanes), f32),) * 2 + (shape((group * plan.body, lanes), f32),),
         [VMEM],
-        (VMEM, VMEM),
-        name="edges",
+        (VMEM, VMEM, VMEM),
     )(flat)
+    ready = first
     line = plan.line()
     swap_a = [(line[i], line[i ^ 1]) for i in range(len(line))]
     swap_b = [
         (line[i], line[((i + 1) ^ 1) - 1]) for i in range(1, len(line) - 1)
     ]
-    first = lax.ppermute(first, AXES, swap_a)
-    second = lax.ppermute(second, AXES, swap_b)
-
-    ids = entries(plan, got[:, plan.body :, :])
+    first = move(AXES, swap_a)(first)
+    second = move(AXES, swap_b)(second)
+
+    if plan.rows % 4 == 0:
+        across, _ = lax.optimization_barrier((across, ready))
+        hists += radiated(4, [across, move("row", near_swap)(across)])
+    parts = len(hists)
+    near_parts = 2
+
+    ids = entries(plan, got[:, plan.body : plan.body + 4, :])
     listed, count = call(
         bind(list_kernel, plan),
-        (shape((group * plan.capacity + 8,), jnp.int32), shape((1,), jnp.int32)),
+        (shape((group * SURF_DEV + 8,), jnp.int32), shape((1,), jnp.int32)),
         [SMEM],
         (SMEM, SMEM),
-        name="list",
     )(ids)
 
-    flat, listed, count, hists = lax.optimization_barrier((flat, listed, count, hists))
+    own, listed, count, hists = lax.optimization_barrier((own, listed, count, hists))
     back, samp = call(
         bind(stencil_kernel, plan),
         (shape((group * plan.body, lanes), f32), shape((plan.chunk * 8 * 16, lanes), f32)),
         [VMEM, VMEM, VMEM, SMEM],
         (VMEM, VMEM),
         [
-            pltpu.VMEM((3 * field_rows, lanes), f32),
+            pltpu.VMEM((field_rows, lanes), f32),
+            pltpu.VMEM((field_rows, lanes), f32),
+            pltpu.VMEM((field_rows, lanes), f32),
             pltpu.VMEM((75, 8, lanes), f32),
             pltpu.VMEM((plan.tall_pad, lanes), f32),
             pltpu.VMEM((30 * plan.az, 8, lanes), f32),
         ],
         flops=10**9,
-        name="stencil",
-    )(flat, first, second, flux_jacobian)
-    back = lax.all_to_all(back.reshape(group, plan.body, lanes), GROUP, 0, 0, tiled=True)
+    )(own, first, second, flux_jacobian)
+    back = move(GROUP)(back.reshape(group, plan.body, lanes))
 
     columns = np.zeros((FREQ, 8), np.float32)
     for s in range(STEPS):
@@ -818,7 +843,7 @@
         columns[:, 2 * s + 1] = sin_t[:, plan.samples - STEPS + s]
     columns[:, 6] = 1.0 / np.arange(1, FREQ + 1)
     partial = call(
-        bind(recent_kernel, plan, parts),
+        bind(recent_kernel, plan, parts, near_parts),
         shape((plan.obs // 2, 128), f32),
         [SMEM, SMEM, VMEM, VMEM, VMEM] + [VMEM] * parts,
         VMEM,
@@ -834,22 +859,11 @@
             pltpu.VMEM((128, 128), f32),
         ],
         flops=10**9,
-        name="recent",
     )(listed, count, samp, observers, jnp.asarray(columns), *hists)
-    partial, back = lax.optimization_barrier((partial, back))
-    pieces = lax.all_to_all(
-        partial.reshape(plan.devices, 4, 128), AXES, 0, 0, tiled=True
-    )
-    spectrum = call(
-        sum_kernel, shape((plan.per_obs, 2 * FREQ), f32), [VMEM], VMEM, name="sum"
-    )(pieces)
+    pieces = move(AXES)(partial.reshape(plan.devices, 4, 128))
+    spectrum = call(sum_kernel, shape((plan.per_obs, 2 * FREQ), f32), [VMEM], VMEM)(pieces)
     field = call(
-        bind(unpack_kernel, plan),
-        shape((5, lanes, wr), f32),
-        [VMEM],
-        VMEM,
-        [pltpu.VMEM((5 * wr, lanes), f32)],
-        name="unpack",
+        bind(unpack_kernel, plan), shape((5, lanes, wr), f32), [VMEM], VMEM, [pltpu.VMEM((5 * wr, lanes), f32)]
     )(back)
     return field.reshape(flow_field.shape), spectrum
 

time: 81.6 us -> 93.2 us (1.14)
  blocking collectives: 0 us -> 16.8 us
  starting transfers between devices: 24.7 us -> 15.1 us
  waiting for transfers between devices: 9.68 us -> 17.8 us
  Pallas kernels: 41.6 us -> 38.8 us
    all_to_all x0 -> x1, blocking collectives: none -> 16.8 us  [move(): return lambda value: lax.all_to_all(value, axes, 0, 0, tiled=True)]
    all_to_all x3 -> x2, starting transfers between devices: 19.5 us -> 10.7 us  [move(): return lambda value: lax.all_to_all(value, axes, 0, 0, tiled=True)]
    all_to_all x3 -> x2, waiting for transfers between devices: 8.87 us -> 14 us  [move(): return lambda value: lax.all_to_all(value, axes, 0, 0, tiled=True)]
    ppermute x3 -> x5, waiting for transfers between devices: 0.81 us -> 3.83 us  [move(): return lambda value: lax.ppermute(value, axes, pairs[0])]
    pallas_call x8 -> x7, Pallas kernels: 23.6 us -> 22.2 us  [the longest x3 7.89 us: radiated(): call(bind(hist_kernel, plan, ways, i * share, 32), shape((share, 64), f32...]
    pallas_call x1, Pallas kernels: 16 us -> 14.7 us  [fast_device(): call(bind(stencil_kernel, plan), (shape((group * plan.body, lanes), f32),...]
    ppermute x3 -> x5, starting transfers between devices: 5.2 us -> 4.38 us  [move(): return lambda value: lax.ppermute(value, axes, pairs[0])]
  transfers between devices with their start and end apart: 6 -> 7, of which waited for: 3 -> 3; matrix products, arithmetic and copies ran while one was open for 0% -> 0% of each run, Pallas kernels for 30% -> 16%
where the time goes in v4:
time: 93.2 us; the launch traced here: 92.6 us
  Pallas kernels  38.8 us (42%)
  waiting for transfers between devices  17.8 us (19%)
  blocking collectives  16.8 us (18%)
  starting transfers between devices  15.1 us (16%)
  local copies, waits for them, and re-layouts  2.53 us (3%)
  between operations  1.45 us (2%)
    all_to_all x1, blocking collectives, move(): return lambda value: lax.all_to_all(value, axes, 0, 0, tiled=True)  16.8 us
    pallas_call x1, Pallas kernels, fast_device(): call(bind(stencil_kernel, plan), (shape((group * plan.body, lanes), f32),...  14.7 us
    all_to_all x2, waiting for transfers between devices, move(): return lambda value: lax.all_to_all(value, axes, 0, 0, tiled=True)  14 us
    all_to_all x2, starting transfers between devices, move(): return lambda value: lax.all_to_all(value, axes, 0, 0, tiled=True)  10.7 us
    pallas_call x3, Pallas kernels, radiated(): call(bind(hist_kernel, plan, ways, i * share, 32), shape((share, 64), f32...  7.89 us
    pallas_call x1, Pallas kernels, fast_device(): call(bind(recent_kernel, plan, parts, near_parts), shape((plan.obs // 2,...  7.6 us
    ppermute x5, starting transfers between devices, move(): return lambda value: lax.ppermute(value, axes, pairs[0])  4.38 us
    pallas_call x1, Pallas kernels, fast_device(): call(bind(list_kernel, plan), (shape((group * SURF_DEV + 8,), jnp.int32),...  3.9 us
  transfers between devices with their start and end apart: 7, of which 3 were waited for; matrix products, arithmetic and copies ran while one was open for 0% of the time, Pallas kernels for 16%

profile of v4, /device:TPU:0, one launch (start us, length us, event | category | flops | bytes accessed | tf_op | source)
XLA Modules:
  0.0 92.6 jit_solution(11122723779020172976)
XLA Ops:
  0.6 0.0 copy-start.1
  1.3 0.0 copy-done.1
  1.3 0.0 copy-start
  1.3 1.0 %copy-done = f32[5,4,32,128]{3,2,1,0:T(8,128)S(1)} copy-done((f32[5,4,32,128]{3,2,1,0:T(8,128)S(1)}, f32[5,4,32,128]{3,2,1,0:T(8,128)}, u32[]{:S(2)}) %copy-start) | copy-done | bytes 327704
  2.3 0.0 copy-start.2
  2.3 0.9 %shard_map.95 = f32[8,88,128]{2,1,0:T(8,128)} custom-call(f32[5,128,128]{2,1,0:T(8,128)S(1)} %bitcast.11, s32[8,48]{1,0:T(8,128)S(1)} %bitcast.14, s32[1,1]{1,0:T(1,128)S(6)} %copy.18.live_ref), custom_call_target="tpu_custom_call" | custom-call | flops 1000000 | bytes 100000 | tf_op jit(solution)/shard_map/pallas_call | solution.py:725
  3.2 7.3 %all-to-all-start = ((f32[8,88,128]{2,1,0:T(8,128)}), f32[8,88,128]{2,1,0:T(8,128)S(1)}, u32[]{:S(2)}, u32[]{:S(2)}) async-start(f32[8,88,128]{2,1,0:T(8,128)} %shard_map.95), calls=%async_computation | async-start | bytes 720896 | tf_op jit(solution)/shard_map/all_to_all | solution.py:282
  10.5 0.1 copy.12
  10.6 0.0 copy-start.4
  10.6 0.1 reshape.234
  10.8 0.0 copy-start.3
  10.8 0.0 copy-done.2
  10.8 0.6 copy-done.4
  11.4 0.1 copy-done.3
  11.5 2.1 %dft.1 = (f32[3,264,128]{2,1,0:T(8,128)S(1)}, f32[256,8]{1,0:T(8,128)S(1)}) custom-call(f32[5,384,128]{2,1,0:T(8,128)S(1)} %bitcast.15, f32[64,128]{1,0:T(8,128)S(1)} %copy-done.4, f32[3,3,128]{2,1,0:T(4,128)S(1)} %fusion.1.point_ref, f32[3,256]{1,0:T(4,128)S(1)} %copy-done.3, s32[1,1]{1,0:T(1,128)S(6)} %copy.18.live_ref), custom_call_target="tpu_custom_call" | custom-call | flops 1000000000 | bytes 1000000 | tf_op jit(solution)/shard_map/dft/pallas_call | solution.py:749
  13.6 0.1 collective-permute-start
  13.6 1.6 %collective-permute-start.1 = (f32[3,264,128]{2,1,0:T(8,128)S(1)}, f32[3,264,128]{2,1,0:T(8,128)S(1)}, u32[]{:S(2)}, u32[]{:S(2)}) collective-permute-start(f32[3,264,128]{2,1,0:T(8,128)S(1)} %get-tuple-element.25.refs_0_), channel_id=1, source_target_pairs={{0,2},{1,3},{2,0},{3,1},{4,6},{5,7},{6,4},{7,5},{8,10},{9,11},{10,... | collective-permute-start | bytes 1216520 | tf_op jit(solution)/shard_map/ppermute | solution.py:281
  15.2 0.0 copy-start.6
  15.2 0.7 copy-done.6
  15.9 0.0 collective-permute-done.refs_1_
  15.9 1.7 %shard_map.96.refs_0_ = f32[32,64]{1,0:T(8,128)S(1)} custom-call(f32[256,8]{1,0:T(8,128)S(1)} %get-tuple-element.24.watch_ref, f32[3,264,128]{2,1,0:T(8,128)S(1)} %get-tuple-element.25.refs_0_, f32[3,264,128]{2,1,0:T(8,128)S(1)} %collective-permute-done.refs_1_), custom_call_target="tpu_custom_call" | custom-call | flops 1000000000 | bytes 100000 | tf_op jit(solution)/shard_map/pallas_call | solution.py:772
  17.6 3.9 %all-to-all-done = f32[8,88,128]{2,1,0:T(8,128)S(1)} async-done(((f32[8,88,128]{2,1,0:T(8,128)}), f32[8,88,128]{2,1,0:T(8,128)S(1)}, u32[]{:S(2)}, u32[]{:S(2)}) %all-to-all-start) | async-done | bytes 360480 | tf_op jit(solution)/shard_map/all_to_all | solution.py:282
  21.5 0.1 shard_map.97
  21.6 3.8 %collective-permute-done.1.refs_0_ = f32[3,264,128]{2,1,0:T(8,128)S(1)} collective-permute-done((f32[3,264,128]{2,1,0:T(8,128)S(1)}, f32[3,264,128]{2,1,0:T(8,128)S(1)}, u32[]{:S(2)}, u32[]{:S(2)}) %collective-permute-start.1) | collective-permute-done | bytes 405536 | tf_op jit(solution)/shard_map/ppermute | solution.py:281
  25.4 0.0 collective-permute-start.2
  25.4 1.7 %shard_map.99.refs_1_ = f32[32,64]{1,0:T(8,128)S(1)} custom-call(f32[256,8]{1,0:T(8,128)S(1)} %get-tuple-element.24.watch_ref, f32[3,264,128]{2,1,0:T(8,128)S(1)} %get-tuple-element.25.refs_0_, f32[3,264,128]{2,1,0:T(8,128)S(1)} %collective-permute-done.refs_1_), custom_call_target="tpu_custom_call" | custom-call | flops 1000000000 | bytes 100000 | tf_op jit(solution)/shard_map/pallas_call | solution.py:772
  27.1 2.1 %collective-permute-start.3 = (f32[360,128]{1,0:T(8,128)S(1)}, f32[360,128]{1,0:T(8,128)S(1)}, u32[]{:S(2)}, u32[]{:S(2)}) collective-permute-start(f32[360,128]{1,0:T(8,128)S(1)} %get-tuple-element.31), channel_id=1, source_target_pairs={{0,8},{8,0},{16,24},{24,16},{28,20},{20,28},{12,4},{4,12},{5,13},{... | collective-permute-start | bytes 552968 | tf_op jit(solution)/shard_map/ppermute | solution.py:281
  29.2 0.7 collective-permute-start.4
  29.9 3.9 %shard_map.98 = (s32[1032]{0:T(1024)S(1)}, s32[1]{0:T(128)}) custom-call(s32[4096]{0:T(1024)S(1)} %bitcast.13), custom_call_target="tpu_custom_call" | custom-call | flops 1000000 | bytes 100000 | tf_op jit(solution)/shard_map/pallas_call | solution.py:815
  33.8 0.0 collective-permute-done.2.refs_1_
  33.8 4.5 %shard_map.100.refs_2_ = f32[64,64]{1,0:T(8,128)S(1)} custom-call(f32[256,8]{1,0:T(8,128)S(1)} %get-tuple-element.24.watch_ref, f32[3,264,128]{2,1,0:T(8,128)S(1)} %collective-permute-done.1.refs_0_, f32[3,264,128]{2,1,0:T(8,128)S(1)} %collective-permute-done.2.refs_1_), custom_call_target="tpu_custom_call" | custom-call | flops 1000000000 | bytes 100000 | tf_op jit(solution)/shard_map/pallas_call | solution.py:772
  38.3 0.0 copy-start.5
  38.4 0.0 collective-permute-done.4.second_ref
  38.4 0.0 collective-permute-done.3.first_ref
  38.4 14.7 %shard_map.101 = (f32[640,128]{1,0:T(8,128)}, f32[2048,128]{1,0:T(8,128)S(1)}) custom-call(f32[640,128]{1,0:T(8,128)S(1)} %get-tuple-element.33.own_ref, f32[360,128]{1,0:T(8,128)S(1)} %collective-permute-done.3.first_ref, f32[360,128]{1,0:T(8,128)S(1)} %collective-permute-done.4.second_ref, f32[3,5,5]{2,1,0:T(8,128)S(1)} %copy.17.jac_ref), custom_call_target="tpu_custom_call" | custom-call | flops 1000000000 | bytes 100000 | tf_op jit(solution)/shard_map/pallas_call | solution.py:823
  53.1 0.0 copy-done.5
  53.1 7.6 %shard_map.103 = f32[128,128]{1,0:T(8,128)S(1)} custom-call(s32[1032]{0:T(1024)S(1)} %get-tuple-element.36.list_ref, s32[1]{0:T(128)} %get-tuple-element.37.count_ref, f32[2048,128]{1,0:T(8,128)S(1)} %get-tuple-element.38.samp_ref, f32[3,256]{1,0:T(4,128)S(1)} %copy-done.3, f32[32,8]{1,0:T(8,128)S(1)} %copy-done.5, f32[32,64]{1,0:T(8,128)S(1)} %shard_map.96.refs_0_, ...), custom_call_target="tpu_custom_call" | custom-call | flops 1000000000 | bytes 100000 | tf_op jit(solution)/shard_map/pallas_call | solution.py:845
  60.7 16.8 %all_to_all.15.pieces_ref = f32[32,4,128]{2,1,0:T(4,128)S(1)} all-to-all(f32[32,4,128]{2,1,0:T(4,128)S(1)} %bitcast.12), channel_id=1, replica_groups=mesh['gx'=4,'gz'=2,'row'=4] {'gx','gz','row'}, dimensions={0} | all-to-all | bytes 131072 | tf_op jit(solution)/shard_map/all_to_all | solution.py:282
  77.5 3.4 %all-to-all-start.1 = ((f32[8,80,128]{2,1,0:T(8,128)}), f32[8,80,128]{2,1,0:T(8,128)S(1)}, u32[]{:S(2)}, u32[]{:S(2)}) async-start(f32[8,80,128]{2,1,0:T(8,128)} %bitcast.6), calls=%async_computation.1 | async-start | bytes 655360 | tf_op jit(solution)/shard_map/all_to_all | solution.py:282
  80.9 0.7 shard_map.104
  81.6 10.1 %all-to-all-done.1.back_ref = f32[8,80,128]{2,1,0:T(8,128)S(1)} async-done(((f32[8,80,128]{2,1,0:T(8,128)}), f32[8,80,128]{2,1,0:T(8,128)S(1)}, u32[]{:S(2)}, u32[]{:S(2)}) %all-to-all-start.1) | async-done | bytes 327712 | tf_op jit(solution)/shard_map/all_to_all | solution.py:282
  91.7 0.9 shard_map.102
  (5 shorter events, 0.1 us)
Async XLA Ops:
  0.6 0.7 copy-start.1
  1.3 1.0 %copy-start = (f32[5,4,32,128]{3,2,1,0:T(8,128)S(1)}, f32[5,4,32,128]{3,2,1,0:T(8,128)}, u32[]{:S(2)}) copy-start(f32[5,4,32,128]{3,2,1,0:T(8,128)} %param.8) | copy-start | bytes 983044
  2.3 8.5 %copy-start.2 = (f32[384,5,128]{2,0,1:T(8,128)S(1)}, f32[384,5,128]{2,0,1:T(8,128)}, u32[]{:S(2)}) copy-start(f32[384,5,128]{2,0,1:T(8,128)} %param.10) | copy-start | bytes 2949124
  3.2 18.3 %all-to-all-start = ((f32[8,88,128]{2,1,0:T(8,128)}), f32[8,88,128]{2,1,0:T(8,128)S(1)}, u32[]{:S(2)}, u32[]{:S(2)}) async-start(f32[8,88,128]{2,1,0:T(8,128)} %shard_map.95), calls=%async_computation | async-start | bytes 720896 | tf_op jit(solution)/shard_map/all_to_all | solution.py:282
  10.6 0.8 copy-start.4
  10.8 0.7 copy-start.3
  13.6 2.3 %collective-permute-start = (f32[3,264,128]{2,1,0:T(8,128)S(1)}, f32[3,264,128]{2,1,0:T(8,128)S(1)}, u32[]{:S(2)}, u32[]{:S(2)}) collective-permute-start(f32[3,264,128]{2,1,0:T(8,128)S(1)} %get-tuple-element.25.refs_0_), channel_id=1, source_target_pairs={{0,1},{1,0},{2,3},{3,2},{4,5},{5,4},{6,7},{7,6},{8,9},{9,8},{10,11... | collective-permute-start | bytes 1216520 | tf_op jit(solution)/shard_map/ppermute | solution.py:281
  13.6 11.8 %collective-permute-start.1 = (f32[3,264,128]{2,1,0:T(8,128)S(1)}, f32[3,264,128]{2,1,0:T(8,128)S(1)}, u32[]{:S(2)}, u32[]{:S(2)}) collective-permute-start(f32[3,264,128]{2,1,0:T(8,128)S(1)} %get-tuple-element.25.refs_0_), channel_id=1, source_target_pairs={{0,2},{1,3},{2,0},{3,1},{4,6},{5,7},{6,4},{7,5},{8,10},{9,11},{10,... | collective-permute-start | bytes 1216520 | tf_op jit(solution)/shard_map/ppermute | solution.py:281
  15.2 0.7 copy-start.6
  25.4 8.4 %collective-permute-start.2 = (f32[3,264,128]{2,1,0:T(8,128)S(1)}, f32[3,264,128]{2,1,0:T(8,128)S(1)}, u32[]{:S(2)}, u32[]{:S(2)}) collective-permute-start(f32[3,264,128]{2,1,0:T(8,128)S(1)} %collective-permute-done.1.refs_0_), channel_id=1, source_target_pairs={{0,1},{1,0},{2,3},{3,2},{4,5},{5,4},{6,7},{7,6},{8,9},{9,8},{10,11... | collective-permute-start | bytes 1216520 | tf_op jit(solution)/shard_map/ppermute | solution.py:281
  27.1 11.3 %collective-permute-start.3 = (f32[360,128]{1,0:T(8,128)S(1)}, f32[360,128]{1,0:T(8,128)S(1)}, u32[]{:S(2)}, u32[]{:S(2)}) collective-permute-start(f32[360,128]{1,0:T(8,128)S(1)} %get-tuple-element.31), channel_id=1, source_target_pairs={{0,8},{8,0},{16,24},{24,16},{28,20},{20,28},{12,4},{4,12},{5,13},{... | collective-permute-start | bytes 552968 | tf_op jit(solution)/shard_map/ppermute | solution.py:281
  29.2 9.2 %collective-permute-start.4 = (f32[360,128]{1,0:T(8,128)S(1)}, f32[360,128]{1,0:T(8,128)S(1)}, u32[]{:S(2)}, u32[]{:S(2)}) collective-permute-start(f32[360,128]{1,0:T(8,128)S(1)} %get-tuple-element.34), channel_id=1, source_target_pairs={{8,16},{16,8},{24,28},{28,24},{20,12},{12,20},{4,5},{5,4},{13,21},... | collective-permute-start | bytes 552968 | tf_op jit(solution)/shard_map/ppermute | solution.py:281
  38.3 14.7 %copy-start.5 = (f32[32,8]{1,0:T(8,128)S(1)}, f32[32,8]{1,0:T(8,128)}, u32[]{:S(2)}) copy-start(f32[32,8]{1,0:T(8,128)} %constant.101.clone.tab_ref) | copy-start | bytes 3076
  77.5 14.2 %all-to-all-start.1 = ((f32[8,80,128]{2,1,0:T(8,128)}), f32[8,80,128]{2,1,0:T(8,128)S(1)}, u32[]{:S(2)}, u32[]{:S(2)}) async-start(f32[8,80,128]{2,1,0:T(8,128)} %bitcast.6), calls=%async_computation.1 | async-start | bytes 655360 | tf_op jit(solution)/shard_map/all_to_all | solution.py:282
